TPU v7x, 128 devices: a whole 4x4x4 slice. The times are simulated.
128 devices in a mesh: depth: 16 (over z, x), tile: 8 (over y, core).
Axes of the slice: x: 4, y: 4, z: 4, core: 2. Of those that a mesh axis runs over, the one named last changes fastest.
Arguments:
- phase_map: float32 [64, 2048, 256], P('depth', 'tile'), may hold values from -3.140625 to 3.140625
- absorb: float32 [64, 2048, 256], P('depth', 'tile'), may hold values from 0.01 to 0.1
- probe_wave: float32 [2, 128, 128], replicated, may hold values from -6 to 6
- waves_in: float32 [16, 32, 2, 128, 128], P('depth', 'tile'), may hold values from -6 to 6
- scan_rows: int32 [18, 32], P(None, 'tile'), may hold values from 0 to 2047, as said below
- scan_cols: int32 [18, 32], P(None, 'tile'), may hold values from 0 to 128
Outputs:
- leaving: float32 [3, 16, 32, 2, 128, 128], P(None, 'depth', 'tile')
Inputs may be any that keep to these rules, and one draw needn't show every extreme that they name: The row scan_rows[b, p] lies among the 256 object rows of the tile that holds probe p, that is between (p // 4) * 256 and that plus 256 - 1; in batch 0 every tile's first probe starts at its tile's first row and its second probe at its tile's last row.
All inputs are finite; a program needn't handle non-finite values.
Results may differ from a plain program's by a relative error of at most 0.00026.
Values sent between devices are 32-bit elements; how exact they have to be, the bound alone decides.
No kernel may reach another device: no remote copies, remote signals or barrier semaphores. Data moves between devices by JAX's collectives and lax.ppermute only.
A program may use at most 128 MiB of HBM per device.

v0:
```python
import math

import jax
import jax.numpy as jnp
from jax import lax
from jax.sharding import PartitionSpec as P

TICKS = 3


fresnel = 0.1
highest = lax.Precision.HIGHEST


def passed_along(x, axis, by):
    length = lax.axis_size(axis)
    return lax.ppermute(x, axis, [(i, (i + by) % length) for i in range(length)])


def from_behind(x, axis, by):
    length = lax.axis_size(axis)
    pairs = [(i, i + by) for i in range(length) if 0 <= i + by < length]
    return lax.ppermute(x, axis, pairs)


def dft_tables(patch_size):
    index_vec = jnp.arange(patch_size, dtype=jnp.int32)
    product = index_vec[:, None] * index_vec[None, :] % patch_size
    angles = -2.0 * math.pi / patch_size * product.astype(jnp.float32)
    return (jnp.cos(angles), jnp.sin(angles))


def propagator(patch_size):
    index_vec = jnp.arange(patch_size, dtype=jnp.int32)
    frequency = jnp.where(index_vec < patch_size // 2, index_vec, index_vec - patch_size).astype(
        jnp.float32
    )
    squared = frequency[:, None] ** 2 + frequency[None, :] ** 2
    angles = -fresnel * math.pi / patch_size * squared
    return (jnp.cos(angles), jnp.sin(angles))


def transmission(phase_map, absorb):
    damping = jnp.exp(-absorb)
    return jnp.stack([damping * jnp.cos(phase_map), damping * jnp.sin(phase_map)], 1)


def left_apply(matrix, wavefield):
    return jnp.einsum("jk,nkl->njl", matrix, wavefield, precision=highest)


def right_apply(wavefield, matrix):
    return jnp.einsum("nkl,lm->nkm", wavefield, matrix, precision=highest)


def two_sided(real_part, imag_part, cos_table, sin_table):
    mid_real = left_apply(cos_table, real_part) - left_apply(sin_table, imag_part)
    mid_imag = left_apply(cos_table, imag_part) + left_apply(sin_table, real_part)
    out_real = right_apply(mid_real, cos_table) - right_apply(mid_imag, sin_table)
    out_imag = right_apply(mid_real, sin_table) + right_apply(mid_imag, cos_table)
    return (out_real, out_imag)


def advance(current, patches, tables):
    cos_table, sin_table, kernel_real, kernel_imag = tables
    patch_size = cos_table.shape[0]
    inverse_scale = 1.0 / (patch_size * patch_size)
    real_part, imag_part = (current[:, 0], current[:, 1])
    for layer_num in range(patches.shape[1]):
        trans_real = patches[:, layer_num, 0]
        trans_imag = patches[:, layer_num, 1]
        real_part, imag_part = (
            real_part * trans_real - imag_part * trans_imag,
            real_part * trans_imag + imag_part * trans_real,
        )
        spec_real, spec_imag = two_sided(real_part, imag_part, cos_table, sin_table)
        spec_real, spec_imag = (
            spec_real * kernel_real - spec_imag * kernel_imag,
            spec_real * kernel_imag + spec_imag * kernel_real,
        )
        back_real, back_imag = two_sided(spec_real, spec_imag, cos_table, -sin_table)
        real_part, imag_part = (back_real * inverse_scale, back_imag * inverse_scale)
    return jnp.stack([real_part, imag_part], 1)


def extract(extended, row_starts, col_starts, patch_size):

    def cut_patch(row_start, col_start):
        return lax.dynamic_slice(
            extended,
            (jnp.int32(0), jnp.int32(0), row_start, col_start),
            (extended.shape[0], 2, patch_size, patch_size),
        )

    return jax.vmap(cut_patch)(row_starts, col_starts)


def shards(phase_map, absorb, probe_wave, waves_in, scan_rows, scan_cols):
    patch_size = probe_wave.shape[-1]
    depth_pos = lax.axis_index("depth")
    tile_pos = lax.axis_index("tile")
    depth_count = lax.axis_size("depth")
    tile_rows = phase_map.shape[1]
    resident = transmission(phase_map, absorb)
    fields = passed_along(
        jnp.stack([phase_map[:, :patch_size], absorb[:, :patch_size]], 1), "tile", -1
    )
    upper_rim = transmission(fields[:, 0], fields[:, 1])
    extended = jnp.concatenate([resident, upper_rim], 2)
    cos_table, sin_table = dft_tables(patch_size)
    kernel_real, kernel_imag = propagator(patch_size)
    tables = (cos_table, sin_table, kernel_real, kernel_imag)
    current = waves_in[0]
    entering = jnp.broadcast_to(probe_wave, current.shape)
    row_offset = tile_pos * tile_rows
    results = []
    for tick_num in range(TICKS):
        batch_num = tick_num - depth_pos + depth_count - 1
        row_starts = lax.dynamic_index_in_dim(scan_rows, batch_num, 0, keepdims=False) - row_offset
        col_starts = lax.dynamic_index_in_dim(scan_cols, batch_num, 0, keepdims=False)
        patches = extract(extended, row_starts, col_starts, patch_size)
        more_ticks = tick_num + 1 < TICKS
        outgoing = advance(current, patches, tables)
        if more_ticks:
            arrived = from_behind(outgoing, "depth", 1)
        results.append(outgoing)
        if more_ticks:
            current = jnp.where(depth_pos == 0, entering, arrived)
    return jnp.stack(results)[:, None]


def solution(mesh):
    return jax.shard_map(
        shards,
        mesh=mesh,
        in_specs=(
            P("depth", "tile", None),
            P("depth", "tile", None),
            P(),
            P("depth", "tile", None, None, None),
            P(None, "tile"),
            P(None, "tile"),
        ),
        out_specs=P(None, "depth", "tile", None, None, None),
        check_vma=False,
    )
```

profile of v0, /device:TPU:96, one launch (start us, length us, event | category | flops | bytes accessed | tf_op | source)
XLA Modules:
  0.0 226.2 jit_solution(11952041311354827390)
XLA Ops:
  0.0 1.3 slice_bitcast_fusion
  1.3 1.0 pad_maximum_fusion
  2.4 2.5 %collective-permute-start = (f32[4,2,128,256]{3,2,1,0:T(8,128)}, f32[4,2,128,256]{3,2,1,0:T(8,128)S(1)}, u32[]{:S(2)}, u32[]{:S(2)}) collective-permute-start(f32[4,2,128,256]{3,2,1,0:T(8,128)} %pad_maximum_fusion), channel_id=1, source_target_pairs={{0,7},{1,0},{2,1},{3,2},{4,3},{5,4},{6,5},{7,6},{8,15},{9,8},{10,9... | collective-permute-start | bytes 3145736 | tf_op jit(solution)/shard_map/ppermute | solution.py:17
  5.9 1.9 copy.436
  8.2 3.8 %multiply_bitcast_fusion.1 = (f32[4,1,256,256]{3,2,1,0:T(8,128)S(1)}, f32[4,1,256,256]{3,2,1,0:T(8,128)S(1)}) fusion(f32[4,256,256]{2,1,0:T(8,128)S(1)} %copy-done.1, f32[4,256,256]{2,1,0:T(8,128)S(1)} %copy-done), kind=kLoop, calls=%fused_computation.184 | loop fusion | flops 786432 | bytes 4194304 | tf_op jit(solution)/shard_map/stack | solution.py:45
  12.0 5.5 %collective-permute-done = f32[4,2,128,256]{3,2,1,0:T(8,128)S(1)} collective-permute-done((f32[4,2,128,256]{3,2,1,0:T(8,128)}, f32[4,2,128,256]{3,2,1,0:T(8,128)S(1)}, u32[]{:S(2)}, u32[]{:S(2)}) %collective-permute-start) | collective-permute-done | bytes 1048608 | tf_op jit(solution)/shard_map/ppermute | solution.py:17
  17.5 2.0 cosine_multiply_fusion
  19.8 11.4 %while.3 = (s32[]{:T(128)}, f32[4,2,384,256]{3,2,1,0:T(8,128)S(1)}, s32[4,4]{1,0:T(4,128)S(1)}, f32[4,4,2,128,128]{4,3,2,1,0:T(8,128)}, s32[]{:T(128)}) while((s32[]{:T(128)}, f32[4,2,384,256]{3,2,1,0:T(8,128)S(1)}, s32[4,4]{1,0:T(4,128)S(1)}, f32[4,4,2,128,128]{4,3,2,1,0:T(8,128)}, s32[]{:T(128)}) %tuple.74), condition=%wide.while_cond, body=%wide.while_body.sunk | while | flops 2 | bytes 1050225 | solution.py:89
  20.4 2.2 bitcast_dynamic-update-slice_fusion.6
  23.2 2.2 bitcast_dynamic-update-slice_fusion.6
  26.0 2.2 bitcast_dynamic-update-slice_fusion.6
  28.8 2.2 bitcast_dynamic-update-slice_fusion.6
  31.1 1.3 fusion.96
  39.0 0.8 fusion.379
  42.0 0.8 fusion.74
  43.5 0.9 multiply_add_fusion.13
  51.1 0.8 fusion.365
  51.9 0.8 fusion.69
  54.1 0.8 fusion.68
  55.6 1.1 multiply_add_fusion.11
  63.4 0.8 fusion.351
  64.1 0.8 fusion.63
  66.4 0.8 fusion.62
  67.9 0.9 multiply_add_fusion.9
  75.4 0.8 fusion.337
  76.2 0.8 fusion.57
  78.4 0.8 fusion.56
  79.9 1.1 fusion.53
  81.1 1.1 fusion.1359
  82.1 3.4 %collective-permute-start.1 = (f32[4,2,128,128]{3,2,0,1:T(8,128)}, f32[4,2,128,128]{3,2,0,1:T(8,128)}, u32[]{:S(2)}, u32[]{:S(2)}) collective-permute-start(f32[4,2,128,128]{3,2,0,1:T(8,128)} %get-tuple-element.94), channel_id=1, source_target_pairs={{0,8},{8,16},{16,24},{24,32},{32,40},{40,48},{48,56},{56,64},{64,7... | collective-permute-start | bytes 1572872 | tf_op jit(solution)/shard_map/ppermute | solution.py:23
  85.5 1.6 broadcast.197.clone2
  87.1 10.8 %while.4 = (s32[]{:T(128)}, f32[4,2,384,256]{3,2,1,0:T(8,128)S(1)}, s32[4,4]{1,0:T(4,128)S(1)}, f32[4,4,2,128,128]{4,3,0,2,1:T(8,128)}, s32[]{:T(128)}) while((s32[]{:T(128)}, f32[4,2,384,256]{3,2,1,0:T(8,128)S(1)}, s32[4,4]{1,0:T(4,128)S(1)}, f32[4,4,2,128,128]{4,3,0,2,1:T(8,128)}, s32[]{:T(128)}) %tuple.83), condition=%wide.while_cond.1, body=%wide.while_body.1.sunk | while | flops 2 | bytes 1050225 | solution.py:89
  87.7 2.1 bitcast_dynamic-update-slice_fusion.7
  90.4 2.1 bitcast_dynamic-update-slice_fusion.7
  93.1 2.1 bitcast_dynamic-update-slice_fusion.7
  95.8 2.1 bitcast_dynamic-update-slice_fusion.7
  97.9 1.7 collective-permute-done.1
  99.6 1.1 broadcast_select_fusion.1
  100.7 1.1 fusion.94
  108.4 0.8 fusion.323
  109.2 0.8 fusion.49
  111.4 0.8 fusion.48
  112.9 1.9 fusion.92
  121.5 0.8 fusion.309
  124.5 0.8 fusion.42
  126.0 2.0 fusion.90
  137.6 0.8 fusion.36
  139.1 2.2 fusion.88
  152.5 0.9 fusion.27
  153.4 1.1 fusion.1358
  154.5 1.9 collective-permute-start.2
  156.4 1.6 broadcast.197.clone2.1
  158.0 11.3 %while.5 = (s32[]{:T(128)}, f32[4,2,384,256]{3,2,1,0:T(8,128)S(1)}, s32[4,4]{1,0:T(4,128)S(1)}, f32[4,4,2,128,128]{4,3,0,2,1:T(8,128)}, s32[]{:T(128)}) while((s32[]{:T(128)}, f32[4,2,384,256]{3,2,1,0:T(8,128)S(1)}, s32[4,4]{1,0:T(4,128)S(1)}, f32[4,4,2,128,128]{4,3,0,2,1:T(8,128)}, s32[]{:T(128)}) %tuple.84), condition=%wide.while_cond.2, body=%wide.while_body.2.sunk | while | flops 2 | bytes 1050225 | solution.py:89
  158.6 2.2 bitcast_dynamic-update-slice_fusion.8
  161.4 2.2 bitcast_dynamic-update-slice_fusion.8
  164.2 2.2 bitcast_dynamic-update-slice_fusion.8
  167.1 2.2 bitcast_dynamic-update-slice_fusion.8
  169.3 1.7 collective-permute-done.2
  171.0 1.1 broadcast_select_fusion
  172.1 1.1 fusion.86
  184.3 2.2 fusion.84
  197.5 1.9 fusion.82
  210.6 2.0 fusion.80
  224.6 1.3 copy.230
  (224 shorter events, 128.8 us)
Async XLA Ops:
  0.0 4.8 %copy-start.6 = (s32[18,4]{0,1:T(4,128)S(1)}, s32[18,4]{0,1:T(4,128)}, u32[]{:S(2)}) copy-start(s32[18,4]{0,1:T(4,128)} %param.11) | copy-start | bytes 868
  0.0 5.0 %copy-start.7 = (s32[18,4]{0,1:T(4,128)S(1)}, s32[18,4]{0,1:T(4,128)}, u32[]{:S(2)}) copy-start(s32[18,4]{0,1:T(4,128)} %param.10) | copy-start | bytes 868
  1.3 6.8 %copy-start = (f32[4,256,256]{2,1,0:T(8,128)S(1)}, f32[4,256,256]{2,1,0:T(8,128)}, u32[]{:S(2)}) copy-start(f32[4,256,256]{2,1,0:T(8,128)} %param.7) | copy-start | bytes 3145732
  1.3 6.8 %copy-start.1 = (f32[4,256,256]{2,1,0:T(8,128)S(1)}, f32[4,256,256]{2,1,0:T(8,128)}, u32[]{:S(2)}) copy-start(f32[4,256,256]{2,1,0:T(8,128)} %param.6) | copy-start | bytes 3145732
  2.4 15.1 %collective-permute-start = (f32[4,2,128,256]{3,2,1,0:T(8,128)}, f32[4,2,128,256]{3,2,1,0:T(8,128)S(1)}, u32[]{:S(2)}, u32[]{:S(2)}) collective-permute-start(f32[4,2,128,256]{3,2,1,0:T(8,128)} %pad_maximum_fusion), channel_id=1, source_target_pairs={{0,7},{1,0},{2,1},{3,2},{4,3},{5,4},{6,5},{7,6},{8,15},{9,8},{10,9... | collective-permute-start | bytes 3145736 | tf_op jit(solution)/shard_map/ppermute | solution.py:17
  39.8 3.8 %copy-start.2 = (f32[4,4,2,128,128]{4,3,2,1,0:T(8,128)S(1)}, f32[4,4,2,128,128]{4,3,2,1,0:T(8,128)}, u32[]{:S(2)}) copy-start(f32[4,4,2,128,128]{4,3,2,1,0:T(8,128)} %get-tuple-element.12) | copy-start | bytes 6291460
  82.1 17.4 %collective-permute-start.1 = (f32[4,2,128,128]{3,2,0,1:T(8,128)}, f32[4,2,128,128]{3,2,0,1:T(8,128)}, u32[]{:S(2)}, u32[]{:S(2)}) collective-permute-start(f32[4,2,128,128]{3,2,0,1:T(8,128)} %get-tuple-element.94), channel_id=1, source_target_pairs={{0,8},{8,16},{16,24},{24,32},{32,40},{40,48},{48,56},{56,64},{64,7... | collective-permute-start | bytes 1572872 | tf_op jit(solution)/shard_map/ppermute | solution.py:23
  87.1 12.5 %copy-start.5 = (f32[2,128,128]{2,1,0:T(8,128)S(1)}, f32[2,128,128]{2,1,0:T(8,128)}, u32[]{:S(2)}) copy-start(f32[2,128,128]{2,1,0:T(8,128)} %param.8) | copy-start | bytes 393220
  154.5 16.5 %collective-permute-start.2 = (f32[4,2,128,128]{3,2,0,1:T(8,128)}, f32[4,2,128,128]{3,2,0,1:T(8,128)}, u32[]{:S(2)}, u32[]{:S(2)}) collective-permute-start(f32[4,2,128,128]{3,2,0,1:T(8,128)} %get-tuple-element.96), channel_id=1, source_target_pairs={{0,8},{8,16},{16,24},{24,32},{32,40},{40,48},{48,56},{56,64},{64,7... | collective-permute-start | bytes 1572872 | tf_op jit(solution)/shard_map/ppermute | solution.py:23
  221.4 3.0 %copy-start.3 = (f32[1,4,2,128,128]{4,3,1,2,0:T(8,128)S(1)}, f32[1,4,2,128,128]{4,3,1,2,0:T(8,128)}, u32[]{:S(2)}) copy-start(f32[1,4,2,128,128]{4,3,1,2,0:T(8,128)} %get-tuple-element.93) | copy-start | bytes 1572868
  221.4 3.0 %copy-start.4 = (f32[1,4,2,128,128]{4,3,1,2,0:T(8,128)S(1)}, f32[1,4,2,128,128]{4,3,1,2,0:T(8,128)}, u32[]{:S(2)}) copy-start(f32[1,4,2,128,128]{4,3,1,2,0:T(8,128)} %get-tuple-element.95) | copy-start | bytes 1572868
where the time goes:
time: 230 us; the launch traced here: 226 us
  matrix products  150 us (65%)
  local copies, waits for them, and re-layouts  41.7 us (18%)
  other arithmetic  15.7 us (7%)
  waiting for transfers between devices  8.85 us (4%)
  starting transfers between devices  7.76 us (3%)
    dot_general x96, matrix products, right_apply(): return jnp.einsum('nkl,lm->nkm', wavefield, matrix, precision=highest)  78.8 us
    dot_general x96, matrix products, left_apply(): return jnp.einsum('jk,nkl->njl', matrix, wavefield, precision=highest)  71.3 us
    gather x36, local copies, waits for them, and re-layouts  33.3 us
    ppermute x1, waiting for transfers between devices, passed_along(): lax.ppermute(x, axis, [(i, (i + by) % length) for i in range(length)])  5.47 us
    ppermute x2, starting transfers between devices, from_behind(): return lax.ppermute(x, axis, pairs)  5.3 us
    unnamed x19, local copies, waits for them, and re-layouts  5.05 us
  transfers between devices with their start and end apart: 3, of which 3 were waited for; matrix products, arithmetic and copies ran while one was open for 14% of the time, Pallas kernels for 0%

commit v1 on v0

v1 whole, which is shorter than its diff:
```python
import functools
import math

import jax
import jax.numpy as jnp
import ml_dtypes
import numpy as np
from jax import lax
from jax.experimental import pallas as pl
from jax.experimental.pallas import tpu as pltpu
from jax.sharding import PartitionSpec as P

TICKS = 3
CHUNKS = 2
RIM_CHUNKS = 2

fresnel = 0.1
VMEM_LIMIT = 24 * 1024 * 1024

SIN_TERMS = [(-1.0) ** j / math.factorial(2 * j + 1) for j in range(7)]
COS_TERMS = [(-1.0) ** j / math.factorial(2 * j) for j in range(8)]


def hop_tables(size):
    index = np.arange(size)
    frequency = np.where(index < size // 2, index, index - size).astype(np.float64)
    k = np.exp(-1j * fresnel * math.pi * frequency**2 / size)
    lag = np.fft.ifft(k)
    g = lag[(index[:, None] - index[None, :]) % size]
    right = np.block([[g.real, g.imag], [-g.imag, g.real]])
    high = right.astype(ml_dtypes.bfloat16)
    low = (right - high.astype(np.float64)).astype(ml_dtypes.bfloat16)
    right = np.stack([high, low])
    return right, np.ascontiguousarray(right.transpose(0, 2, 1))


def series(z, terms):
    total = jnp.full_like(z, terms[-1])
    for term in terms[-2::-1]:
        total = total * z + term
    return total


def transmission(phase, absorb):
    t = 0.5 * phase
    z = t * t
    s = t * series(z, SIN_TERMS)
    c = series(z, COS_TERMS)
    damping = jnp.exp(-absorb)
    return damping * (1.0 - 2.0 * (s * s)), damping * (2.0 * (s * c))


def split(x):
    high = x.astype(jnp.bfloat16)
    return high, (x - high.astype(jnp.float32)).astype(jnp.bfloat16)


def product(a, b):
    return jnp.dot(a, b, preferred_element_type=jnp.float32)


def trans_kernel(phase_ref, absorb_ref, out_ref):
    size = out_ref.shape[-1]
    rows = phase_ref.shape[1]
    step = 32

    def body(i, carry):
        at = pl.ds(pl.multiple_of(i * step, step), step)
        for layer in range(phase_ref.shape[0]):
            for half in range(2):
                cols = slice(half * size, (half + 1) * size)
                real, imag = transmission(phase_ref[layer, at, cols], absorb_ref[layer, at, cols])
                out_ref[layer, 0, half, at, :] = real
                out_ref[layer, 1, half, at, :] = imag
        return carry

    lax.fori_loop(0, rows // step, body, 0)


def section_kernel(
    tick, layers, probes, with_rim, starts, ends, with_probe, tile_rows, *refs
):
    refs = list(refs)
    rows_ref, cols_ref = refs.pop(0), refs.pop(0)
    wave_ref = refs.pop(0)
    probe_ref = refs.pop(0) if with_probe else None
    right_ref, left_ref = refs.pop(0), refs.pop(0)
    count = len(layers)
    if with_rim:
        whole_ref, rim_ref = refs.pop(0), refs.pop(0)
        out_ref = refs.pop(0)
        ext_refs = [refs.pop(0) for _ in range(count)]
    else:
        ext_refs = [refs.pop(0) for _ in range(count)]
        out_ref = refs.pop(0)
    state, x_high, x_low, r_high, r_low = refs

    size = out_ref.shape[-1]
    depth = lax.axis_index("depth")
    batch = tick - depth + lax.axis_size("depth") - 1
    offset = lax.axis_index("tile") * tile_rows
    row_at = [rows_ref[batch, p] - offset for p in probes]
    col_at = [cols_ref[batch, p] for p in probes]
    lane = lax.broadcasted_iota(jnp.int32, (size, size), 1)

    for n in range(len(probes)):
        for part in range(2):
            wave = wave_ref[n, part]
            if with_probe:
                wave = jnp.where(depth == 0, probe_ref[part], wave)
            if starts:
                wave = pltpu.roll(wave, col_at[n] & (size - 1), 1)
            state[n, part] = wave

    for j in range(count):
        ext = ext_refs[j]
        if with_rim:
            for part in range(2):
                for half in range(2):
                    ext[part, half, :tile_rows, :] = whole_ref[j, part, half]
            for half in range(2):
                cols = slice(half * size, (half + 1) * size)
                real, imag = transmission(rim_ref[0, j, :, cols], rim_ref[1, j, :, cols])
                ext[0, half, tile_rows:, :] = real
                ext[1, half, tile_rows:, :] = imag
        for n in range(len(probes)):
            at = pl.ds(row_at[n], size)
            inside = lane >= col_at[n]
            t_real = jnp.where(inside, ext[0, 0, at, :], ext[0, 1, at, :])
            t_imag = jnp.where(inside, ext[1, 0, at, :], ext[1, 1, at, :])
            real, imag = state[n, 0], state[n, 1]
            rows = slice(n * size, (n + 1) * size)
            x_high[rows, :size], x_low[rows, :size] = split(real * t_real - imag * t_imag)
            x_high[rows, size:], x_low[rows, size:] = split(real * t_imag + imag * t_real)
        y = (
            product(x_high[...], right_ref[0])
            + product(x_high[...], right_ref[1])
            + product(x_low[...], right_ref[0])
        )
        for n in range(len(probes)):
            rows = slice(n * size, (n + 1) * size)
            r_high[:size, rows], r_low[:size, rows] = split(y[rows, :size])
            r_high[size:, rows], r_low[size:, rows] = split(y[rows, size:])
        z = (
            product(left_ref[0], r_high[...])
            + product(left_ref[1], r_high[...])
            + product(left_ref[0], r_low[...])
        )
        for n in range(len(probes)):
            rows = slice(n * size, (n + 1) * size)
            for part in range(2):
                wave = z[part * size : (part + 1) * size, rows]
                if j == count - 1:
                    if ends:
                        wave = pltpu.roll(wave, (size - col_at[n]) & (size - 1), 1)
                    out_ref[n, part] = wave
                else:
                    state[n, part] = wave


def vmem():
    return pl.BlockSpec(memory_space=pltpu.VMEM)


def section(
    tick, layers, probes, scans, tables, wave, *, whole=None, rim=None, exts=None,
    probe_wave=None, starts, ends, tile_rows, name
):
    size = wave.shape[-1]
    with_rim = rim is not None
    count = len(layers)
    n = len(probes)
    operands = [*scans, wave]
    specs = [pl.BlockSpec(memory_space=pltpu.SMEM)] * 2
    first = probes[0] if wave.shape[0] != n else 0
    specs.append(pl.BlockSpec((n, 2, size, size), lambda i: (first // n, 0, 0, 0)))
    if probe_wave is not None:
        operands.append(probe_wave)
        specs.append(vmem())
    operands += list(tables)
    specs += [vmem()] * 2
    out_shape = [jax.ShapeDtypeStruct((n, 2, size, size), jnp.float32)]
    out_specs = [vmem()]
    if with_rim:
        operands += [whole, rim]
        block = layers[0] // count
        specs += [
            pl.BlockSpec((count, 2, 2, tile_rows, size), lambda i: (block, 0, 0, 0, 0)),
            vmem(),
        ]
        out_shape += [
            jax.ShapeDtypeStruct((2, 2, tile_rows + size, size), jnp.float32)
        ] * count
        out_specs += [vmem()] * count
    else:
        operands += list(exts)
        specs += [vmem()] * count
    flops = count * n * 2 * 3 * 2 * size * (2 * size) ** 2
    return pl.pallas_call(
        functools.partial(
            section_kernel, tick, layers, probes, with_rim, starts, ends,
            probe_wave is not None, tile_rows,
        ),
        grid=(1,),
        in_specs=specs,
        out_specs=out_specs,
        out_shape=out_shape,
        scratch_shapes=[
            pltpu.VMEM((n, 2, size, size), jnp.float32),
            pltpu.VMEM((n * size, 2 * size), jnp.bfloat16),
            pltpu.VMEM((n * size, 2 * size), jnp.bfloat16),
            pltpu.VMEM((2 * size, n * size), jnp.bfloat16),
            pltpu.VMEM((2 * size, n * size), jnp.bfloat16),
        ],
        compiler_params=pltpu.CompilerParams(vmem_limit_bytes=VMEM_LIMIT),
        cost_estimate=pl.CostEstimate(
            flops=flops, bytes_accessed=count * 2 * 2 * 384 * size * 4, transcendentals=0
        ),
        name=name,
    )(*operands)


def shards(phase_map, absorb, probe_wave, waves_in, scan_rows, scan_cols):
    size = probe_wave.shape[-1]
    slices, tile_rows = phase_map.shape[:2]
    tiles = lax.axis_size("tile")
    depth_count = lax.axis_size("depth")
    back = [(i, (i - 1) % tiles) for i in range(tiles)]
    onward = [(i, i + 1) for i in range(depth_count - 1)]

    per_rim = slices // RIM_CHUNKS
    rims = []
    for r in range(RIM_CHUNKS):
        at = slice(r * per_rim, (r + 1) * per_rim)
        own = jnp.stack([phase_map[at, :size], absorb[at, :size]])
        rims.append(lax.ppermute(own, "tile", back))

    tables = [jnp.asarray(table) for table in hop_tables(size)]
    scans = (scan_rows, scan_cols)
    whole = pl.pallas_call(
        trans_kernel,
        out_shape=jax.ShapeDtypeStruct((slices, 2, 2, tile_rows, size), jnp.float32),
        in_specs=[vmem()] * 2,
        out_specs=vmem(),
        compiler_params=pltpu.CompilerParams(vmem_limit_bytes=VMEM_LIMIT),
        cost_estimate=pl.CostEstimate(
            flops=slices * tile_rows * 2 * size * 40,
            bytes_accessed=slices * tile_rows * 2 * size * 16,
            transcendentals=slices * tile_rows * 2 * size,
        ),
        name="trans",
    )(phase_map, absorb)

    held = waves_in[0]
    count = held.shape[0]
    per_chunk = count // CHUNKS
    groups = [list(range(c * per_chunk, (c + 1) * per_chunk)) for c in range(CHUNKS)]
    exts = []
    for r in range(RIM_CHUNKS - 1):
        layers = list(range(r * per_rim, (r + 1) * per_rim))
        held, *made = section(
            0, layers, list(range(count)), scans, tables, held, whole=whole, rim=rims[r],
            starts=r == 0, ends=False, tile_rows=tile_rows, name=f"enter{r}",
        )
        exts += made
    results = [[]]
    layers = list(range(slices - per_rim, slices))
    for c, group in enumerate(groups):
        rest = dict(starts=RIM_CHUNKS == 1, ends=True, tile_rows=tile_rows, name=f"leave{c}")
        if c == 0:
            done, *made = section(
                0, layers, group, scans, tables, held, whole=whole, rim=rims[-1], **rest
            )
            exts += made
        else:
            (done,) = section(
                0, layers, group, scans, tables, held, exts=exts[-per_rim:], **rest
            )
        results[0].append(done)

    for tick in range(1, TICKS):
        arrived = [lax.ppermute(done, "depth", onward) for done in results[-1]]
        results.append([])
        for c, group in enumerate(groups):
            (done,) = section(
                tick, list(range(slices)), group, scans, tables, arrived[c], exts=exts,
                probe_wave=probe_wave, starts=True, ends=True, tile_rows=tile_rows,
                name=f"tick{tick}_{c}",
            )
            results[-1].append(done)
    out = jnp.stack([jnp.concatenate(parts, 0) for parts in results])
    return out[:, None]


def solution(mesh):
    return jax.shard_map(
        shards,
        mesh=mesh,
        in_specs=(
            P("depth", "tile", None),
            P("depth", "tile", None),
            P(),
            P("depth", "tile", None, None, None),
            P(None, "tile"),
            P(None, "tile"),
        ),
        out_specs=P(None, "depth", "tile", None, None, None),
        check_vma=False,
    )
```

time: 230 us -> 58 us (0.25); the launches traced: 226 us -> 57.1 us
  matrix products: 150 us -> 0 us
  local copies, waits for them, and re-layouts: 41.7 us -> 1.52 us
  Pallas kernels: 0 us -> 25.4 us
  other arithmetic: 15.7 us -> 3.04 us
  starting transfers between devices: 7.76 us -> 15 us
  waiting for transfers between devices: 8.85 us -> 12 us
    dot_general x192 -> x0, matrix products: 150 us -> none  [the longest x96 78.8 us: right_apply(): return jnp.einsum('nkl,lm->nkm', wavefield, matrix, precision=highest)]
    gather x36 -> x0, local copies, waits for them, and re-layouts: 33.3 us -> none
    pallas_call x0 -> x8, Pallas kernels: none -> 25.4 us  [the longest x7 24 us: section(): pl.pallas_call(functools.partial(section_kernel, tick, layers, probes, wi...]
    ppermute x3 -> x6, starting transfers between devices: 7.76 us -> 15 us  [the longest x4 11.9 us: shards(): arrived = [lax.ppermute(done, 'depth', onward) for done in results[-1]]]
    another operation x5, other arithmetic: 7.05 us -> 1.78 us  [the longest x2 1.67 us: shards(): own = jnp.stack([phase_map[at, :size], absorb[at, :size]])]
    unnamed x19 -> x18, local copies, waits for them, and re-layouts: 5.05 us -> 0.24 us
    add x3 -> x0, other arithmetic: 3.45 us -> none  [advance(): real_part * trans_imag + imag_part * trans_real]
    ppermute x3 -> x6, waiting for transfers between devices: 8.85 us -> 12 us  [the longest x2 6.08 us: shards(): rims.append(lax.ppermute(own, 'tile', back))]
  transfers between devices with their start and end apart: 3 -> 6, of which waited for: 3 -> 5; matrix products, arithmetic and copies ran while one was open for 14% -> 2% of each run, Pallas kernels for 0% -> 33%
where the time goes in v1:
time: 58 us; the launch traced here: 57.1 us
  Pallas kernels  25.4 us (44%)
  starting transfers between devices  15 us (26%)
  waiting for transfers between devices  12 us (21%)
  other arithmetic  3.04 us (5%)
  local copies, waits for them, and re-layouts  1.52 us (3%)
    pallas_call x7, Pallas kernels, section(): pl.pallas_call(functools.partial(section_kernel, tick, layers, probes, wi...  24 us
    ppermute x4, starting transfers between devices, shards(): arrived = [lax.ppermute(done, 'depth', onward) for done in results[-1]]  11.9 us
    ppermute x2, waiting for transfers between devices, shards(): rims.append(lax.ppermute(own, 'tile', back))  6.08 us
    ppermute x4, waiting for transfers between devices, shards(): arrived = [lax.ppermute(done, 'depth', onward) for done in results[-1]]  5.88 us
    ppermute x2, starting transfers between devices, shards(): rims.append(lax.ppermute(own, 'tile', back))  3.13 us
    another operation x2, other arithmetic, shards(): own = jnp.stack([phase_map[at, :size], absorb[at, :size]])  1.67 us
    pallas_call x1, Pallas kernels, shards(): pl.pallas_call(trans_kernel, out_shape=jax.ShapeDtypeStruct((slices, 2, 2...  1.38 us
    another operation x1, local copies, waits for them, and re-layouts, shards(): own = jnp.stack([phase_map[at, :size], absorb[at, :size]])  1.28 us
  transfers between devices with their start and end apart: 6, of which 5 were waited for; matrix products, arithmetic and copies ran while one was open for 2% of the time, Pallas kernels for 33%

profile of v1, /device:TPU:96, one launch (start us, length us, event | category | flops | bytes accessed | tf_op | source)
XLA Modules:
  0.0 57.1 jit_solution(14047141674603790171)
XLA Ops:
  0.0 1.3 %slice_bitcast_fusion = (f32[1,2,128,256]{3,2,1,0:T(8,128)S(1)}, f32[1,2,128,256]{3,2,1,0:T(8,128)S(1)}, f32[1,2,128,256]{3,2,1,0:T(8,128)S(1)}, f32[1,2,128,256]{3,2,1,0:T(8,128)S(1)}) fusion(f32[4,256,256]{2,1,0:T(8,128)} %absorb_ref.1, f32[4,256,256]{2,1,0:T(8,128)} %phase_ref.1), kind=kLoop, calls=%fused_computation.6 | loop fusion | bytes 2097152 | tf_op jit(solution)/shard_map/stack | solution.py:235
  1.3 0.0 copy-start.6
  1.3 0.0 copy-start.7
  1.3 0.0 copy-start.2
  1.3 0.0 copy-start.3
  1.3 0.8 %pad_maximum_fusion = f32[2,2,128,256]{3,2,1,0:T(8,128)} fusion(f32[1,2,128,256]{3,2,1,0:T(8,128)S(1)} %get-tuple-element.20, f32[1,2,128,256]{3,2,1,0:T(8,128)S(1)} %get-tuple-element.21), kind=kLoop, calls=%fused_computation.1 | loop fusion | flops 131072 | bytes 1048576 | tf_op jit(solution)/shard_map/stack | solution.py:235
  2.2 2.5 %collective-permute-start = (f32[2,2,128,256]{3,2,1,0:T(8,128)}, f32[2,2,128,256]{3,2,1,0:T(8,128)S(1)}, u32[]{:S(2)}, u32[]{:S(2)}) collective-permute-start(f32[2,2,128,256]{3,2,1,0:T(8,128)} %pad_maximum_fusion), channel_id=1, source_target_pairs={{0,7},{1,0},{2,1},{3,2},{4,3},{5,4},{6,5},{7,6},{8,15},{9,8},{10,9... | collective-permute-start | bytes 1572872 | tf_op jit(solution)/shard_map/ppermute | solution.py:236
  4.6 0.8 %pad_maximum_fusion.1 = f32[2,2,128,256]{3,2,1,0:T(8,128)} fusion(f32[1,2,128,256]{3,2,1,0:T(8,128)S(1)} %get-tuple-element.19, f32[1,2,128,256]{3,2,1,0:T(8,128)S(1)} %get-tuple-element.22), kind=kLoop, calls=%fused_computation.2 | loop fusion | flops 131072 | bytes 1048576 | tf_op jit(solution)/shard_map/stack | solution.py:235
  5.5 0.7 %collective-permute-start.1 = (f32[2,2,128,256]{3,2,1,0:T(8,128)}, f32[2,2,128,256]{3,2,1,0:T(8,128)S(1)}, u32[]{:S(2)}, u32[]{:S(2)}) collective-permute-start(f32[2,2,128,256]{3,2,1,0:T(8,128)} %pad_maximum_fusion.1), channel_id=1, source_target_pairs={{0,7},{1,0},{2,1},{3,2},{4,3},{5,4},{6,5},{7,6},{8,15},{9,8},{10,9... | collective-permute-start | bytes 1572872 | tf_op jit(solution)/shard_map/ppermute | solution.py:236
  6.1 0.0 copy-done.6
  6.1 0.1 copy.11.refs_0_
  6.2 0.0 copy-done.7
  6.2 0.1 copy.12.refs_1_
  6.3 0.0 copy-done.2
  6.3 0.0 copy-done.3
  6.3 0.0 copy-start
  6.4 0.0 copy-start.1
  6.4 0.0 copy-start.5
  6.4 1.4 %trans.1.refs_5_ = f32[4,2,2,256,128]{4,3,2,1,0:T(8,128)S(1)} custom-call(f32[4,256,256]{2,1,0:T(8,128)S(1)} %copy-done.2, f32[4,256,256]{2,1,0:T(8,128)S(1)} %copy-done.3), custom_call_target="tpu_custom_call" | custom-call | flops 10485760 | bytes 4194304 | tf_op jit(solution)/shard_map/trans/pallas_call | solution.py:240
  7.8 3.9 %collective-permute-done.refs_6_ = f32[2,2,128,256]{3,2,1,0:T(8,128)S(1)} collective-permute-done((f32[2,2,128,256]{3,2,1,0:T(8,128)}, f32[2,2,128,256]{3,2,1,0:T(8,128)S(1)}, u32[]{:S(2)}, u32[]{:S(2)}) %collective-permute-start) | collective-permute-done | bytes 524320 | tf_op jit(solution)/shard_map/ppermute | solution.py:236
  11.6 0.0 copy-done
  11.6 0.0 copy-done.1
  11.7 0.0 copy-done.5
  11.7 3.4 %enter0.1 = (f32[4,2,128,128]{3,2,1,0:T(8,128)S(1)}, f32[2,2,384,128]{3,2,1,0:T(8,128)S(1)}, f32[2,2,384,128]{3,2,1,0:T(8,128)S(1)}) custom-call(s32[18,4]{1,0:T(8,128)S(1)} %copy.11.refs_0_, s32[18,4]{1,0:T(8,128)S(1)} %copy.12.refs_1_, f32[4,2,128,128]{3,2,1,0:T(8,128)S(1)} %bitcast.19, bf16[2,256,256]{2,1,0:T(8,128)(2,1)S(1)} %copy-done.1, ...), custom_call_target="tpu_custom_call" | custom-call | flops 805306368 | bytes 1572864 | tf_op jit(solution)/shard_map/enter0/pallas_call | solution.py:199
  15.1 2.2 %collective-permute-done.1.refs_6_ = f32[2,2,128,256]{3,2,1,0:T(8,128)S(1)} collective-permute-done((f32[2,2,128,256]{3,2,1,0:T(8,128)}, f32[2,2,128,256]{3,2,1,0:T(8,128)S(1)}, u32[]{:S(2)}, u32[]{:S(2)}) %collective-permute-start.1) | collective-permute-done | bytes 524320 | tf_op jit(solution)/shard_map/ppermute | solution.py:236
  17.3 2.7 %leave0.1 = (f32[2,2,128,128]{3,2,1,0:T(8,128)S(1)}, f32[2,2,384,128]{3,2,1,0:T(8,128)S(1)}, f32[2,2,384,128]{3,2,1,0:T(8,128)S(1)}) custom-call(s32[18,4]{1,0:T(8,128)S(1)} %copy.11.refs_0_, s32[18,4]{1,0:T(8,128)S(1)} %copy.12.refs_1_, f32[4,2,128,128]{3,2,1,0:T(8,128)S(1)} %get-tuple-element.11.refs_2_, bf16[2,256,256]{2,1,0:T(8,128)(2,1)S(1)} %copy-done.1, ...), custom_call_target="tpu_custom_call" | custom-call | flops 402653184 | bytes 1572864 | tf_op jit(solution)/shard_map/leave0/pallas_call | solution.py:199
  20.0 0.0 copy-start.4
  20.0 3.5 %collective-permute-start.2 = (f32[2,2,128,128]{3,2,1,0:T(8,128)S(1)}, f32[2,2,128,128]{3,2,1,0:T(8,128)S(1)}, u32[]{:S(2)}, u32[]{:S(2)}) collective-permute-start(f32[2,2,128,128]{3,2,1,0:T(8,128)S(1)} %get-tuple-element.12), channel_id=1, source_target_pairs={{0,8},{8,16},{16,24},{24,32},{32,40},{40,48},{48,56},{56,64},{64,7... | collective-permute-start | bytes 786440 | tf_op jit(solution)/shard_map/ppermute | solution.py:282
  23.5 2.4 %leave1.1 = f32[2,2,128,128]{3,2,1,0:T(8,128)S(1)} custom-call(s32[18,4]{1,0:T(8,128)S(1)} %copy.11.refs_0_, s32[18,4]{1,0:T(8,128)S(1)} %copy.12.refs_1_, f32[4,2,128,128]{3,2,1,0:T(8,128)S(1)} %get-tuple-element.11.refs_2_, bf16[2,256,256]{2,1,0:T(8,128)(2,1)S(1)} %copy-done.1, bf16[2,256,256]{2,1,0:T(8,128)(2,1)S(1)} %copy-done, ...), custom_call_target="tpu_custom_call" | custom-call | flops 402653184 | bytes 1572864 | tf_op jit(solution)/shard_map/leave1/pallas_call | solution.py:199
  26.0 3.4 %collective-permute-start.3 = (f32[2,2,128,128]{3,2,1,0:T(8,128)S(1)}, f32[2,2,128,128]{3,2,1,0:T(8,128)S(1)}, u32[]{:S(2)}, u32[]{:S(2)}) collective-permute-start(f32[2,2,128,128]{3,2,1,0:T(8,128)S(1)} %leave1.1), channel_id=1, source_target_pairs={{0,8},{8,16},{16,24},{24,32},{32,40},{40,48},{48,56},{56,64},{64,7... | collective-permute-start | bytes 786440 | tf_op jit(solution)/shard_map/ppermute | solution.py:282
  29.4 2.3 %collective-permute-done.2.refs_2_ = f32[2,2,128,128]{3,2,1,0:T(8,128)S(1)} collective-permute-done((f32[2,2,128,128]{3,2,1,0:T(8,128)S(1)}, f32[2,2,128,128]{3,2,1,0:T(8,128)S(1)}, u32[]{:S(2)}, u32[]{:S(2)}) %collective-permute-start.2) | collective-permute-done | bytes 262176 | tf_op jit(solution)/shard_map/ppermute | solution.py:282
  31.6 0.0 copy-done.4
  31.7 3.9 %tick1_0.1 = f32[2,2,128,128]{3,2,1,0:T(8,128)S(1)} custom-call(s32[18,4]{1,0:T(8,128)S(1)} %copy.11.refs_0_, s32[18,4]{1,0:T(8,128)S(1)} %copy.12.refs_1_, f32[2,2,128,128]{3,2,1,0:T(8,128)S(1)} %collective-permute-done.2.refs_2_, f32[2,128,128]{2,1,0:T(8,128)S(1)} %copy-done.4, bf16[2,256,256]{2,1,0:T(8,128)(2,1)S(1)} %copy-done.1, ...), custom_call_target="tpu_custom_call" | custom-call | flops 805306368 | bytes 3145728 | tf_op jit(solution)/shard_map/tick1_0/pallas_call | solution.py:199
  35.5 1.9 %collective-permute-start.4 = (f32[2,2,128,128]{3,2,1,0:T(8,128)S(1)}, f32[2,2,128,128]{3,2,1,0:T(8,128)S(1)}, u32[]{:S(2)}, u32[]{:S(2)}) collective-permute-start(f32[2,2,128,128]{3,2,1,0:T(8,128)S(1)} %tick1_0.1), channel_id=1, source_target_pairs={{0,8},{8,16},{16,24},{24,32},{32,40},{40,48},{48,56},{56,64},{64,7... | collective-permute-start | bytes 786440 | tf_op jit(solution)/shard_map/ppermute | solution.py:282
  37.5 0.0 collective-permute-done.3.refs_2_
  37.5 3.9 %tick1_1.1 = f32[2,2,128,128]{3,2,1,0:T(8,128)S(1)} custom-call(s32[18,4]{1,0:T(8,128)S(1)} %copy.11.refs_0_, s32[18,4]{1,0:T(8,128)S(1)} %copy.12.refs_1_, f32[2,2,128,128]{3,2,1,0:T(8,128)S(1)} %collective-permute-done.3.refs_2_, f32[2,128,128]{2,1,0:T(8,128)S(1)} %copy-done.4, bf16[2,256,256]{2,1,0:T(8,128)(2,1)S(1)} %copy-done.1, ...), custom_call_target="tpu_custom_call" | custom-call | flops 805306368 | bytes 3145728 | tf_op jit(solution)/shard_map/tick1_1/pallas_call | solution.py:199
  41.3 3.0 %collective-permute-start.5 = (f32[2,2,128,128]{3,2,1,0:T(8,128)S(1)}, f32[2,2,128,128]{3,2,1,0:T(8,128)S(1)}, u32[]{:S(2)}, u32[]{:S(2)}) collective-permute-start(f32[2,2,128,128]{3,2,1,0:T(8,128)S(1)} %tick1_1.1), channel_id=1, source_target_pairs={{0,8},{8,16},{16,24},{24,32},{32,40},{40,48},{48,56},{56,64},{64,7... | collective-permute-start | bytes 786440 | tf_op jit(solution)/shard_map/ppermute | solution.py:282
  44.5 1.6 %collective-permute-done.4.refs_2_ = f32[2,2,128,128]{3,2,1,0:T(8,128)S(1)} collective-permute-done((f32[2,2,128,128]{3,2,1,0:T(8,128)S(1)}, f32[2,2,128,128]{3,2,1,0:T(8,128)S(1)}, u32[]{:S(2)}, u32[]{:S(2)}) %collective-permute-start.4) | collective-permute-done | bytes 262176 | tf_op jit(solution)/shard_map/ppermute | solution.py:282
  46.1 3.8 %tick2_0.1 = f32[2,2,128,128]{3,2,1,0:T(8,128)S(1)} custom-call(s32[18,4]{1,0:T(8,128)S(1)} %copy.11.refs_0_, s32[18,4]{1,0:T(8,128)S(1)} %copy.12.refs_1_, f32[2,2,128,128]{3,2,1,0:T(8,128)S(1)} %collective-permute-done.4.refs_2_, f32[2,128,128]{2,1,0:T(8,128)S(1)} %copy-done.4, bf16[2,256,256]{2,1,0:T(8,128)(2,1)S(1)} %copy-done.1, ...), custom_call_target="tpu_custom_call" | custom-call | flops 805306368 | bytes 3145728 | tf_op jit(solution)/shard_map/tick2_0/pallas_call | solution.py:199
  50.0 2.0 %collective-permute-done.5.refs_2_ = f32[2,2,128,128]{3,2,1,0:T(8,128)S(1)} collective-permute-done((f32[2,2,128,128]{3,2,1,0:T(8,128)S(1)}, f32[2,2,128,128]{3,2,1,0:T(8,128)S(1)}, u32[]{:S(2)}, u32[]{:S(2)}) %collective-permute-start.5) | collective-permute-done | bytes 262176 | tf_op jit(solution)/shard_map/ppermute | solution.py:282
  51.9 3.9 %tick2_1.1 = f32[2,2,128,128]{3,2,1,0:T(8,128)S(1)} custom-call(s32[18,4]{1,0:T(8,128)S(1)} %copy.11.refs_0_, s32[18,4]{1,0:T(8,128)S(1)} %copy.12.refs_1_, f32[2,2,128,128]{3,2,1,0:T(8,128)S(1)} %collective-permute-done.5.refs_2_, f32[2,128,128]{2,1,0:T(8,128)S(1)} %copy-done.4, bf16[2,256,256]{2,1,0:T(8,128)(2,1)S(1)} %copy-done.1, ...), custom_call_target="tpu_custom_call" | custom-call | flops 805306368 | bytes 3145728 | tf_op jit(solution)/shard_map/tick2_1/pallas_call | solution.py:199
  55.9 1.3 %maximum_bitcast_fusion = f32[3,1,4,2,128,128]{5,4,3,2,1,0:T(8,128)} fusion(f32[1,4,2,128,128]{4,3,2,1,0:T(8,128)S(1)} %maximum_bitcast_fusion.3, f32[1,4,2,128,128]{4,3,2,1,0:T(8,128)S(1)} %maximum_bitcast_fusion.2, f32[1,4,2,128,128]{4,3,2,1,0:T(8,128)S(1)} %maximum_bitcast_fusion.1), kind=kLoop, calls=%fused_computation | loop fusion | flops 786432 | bytes 3145728 | tf_op jit(solution)/shard_map/broadcast_in_dim | solution.py:292
  (3 shorter events, 0.1 us)
Async XLA Ops:
  1.3 4.9 %copy-start.6 = (s32[18,4]{0,1:T(4,128)S(1)}, s32[18,4]{0,1:T(4,128)}, u32[]{:S(2)}) copy-start(s32[18,4]{0,1:T(4,128)} %param.12) | copy-start | bytes 868
  1.3 4.9 %copy-start.7 = (s32[18,4]{0,1:T(4,128)S(1)}, s32[18,4]{0,1:T(4,128)}, u32[]{:S(2)}) copy-start(s32[18,4]{0,1:T(4,128)} %param.13) | copy-start | bytes 868
  1.3 5.0 %copy-start.2 = (f32[4,256,256]{2,1,0:T(8,128)S(1)}, f32[4,256,256]{2,1,0:T(8,128)}, u32[]{:S(2)}) copy-start(f32[4,256,256]{2,1,0:T(8,128)} %phase_ref.1) | copy-start | bytes 3145732
  1.3 5.0 %copy-start.3 = (f32[4,256,256]{2,1,0:T(8,128)S(1)}, f32[4,256,256]{2,1,0:T(8,128)}, u32[]{:S(2)}) copy-start(f32[4,256,256]{2,1,0:T(8,128)} %absorb_ref.1) | copy-start | bytes 3145732
  2.2 9.5 %collective-permute-start = (f32[2,2,128,256]{3,2,1,0:T(8,128)}, f32[2,2,128,256]{3,2,1,0:T(8,128)S(1)}, u32[]{:S(2)}, u32[]{:S(2)}) collective-permute-start(f32[2,2,128,256]{3,2,1,0:T(8,128)} %pad_maximum_fusion), channel_id=1, source_target_pairs={{0,7},{1,0},{2,1},{3,2},{4,3},{5,4},{6,5},{7,6},{8,15},{9,8},{10,9... | collective-permute-start | bytes 1572872 | tf_op jit(solution)/shard_map/ppermute | solution.py:236
  5.5 11.8 %collective-permute-start.1 = (f32[2,2,128,256]{3,2,1,0:T(8,128)}, f32[2,2,128,256]{3,2,1,0:T(8,128)S(1)}, u32[]{:S(2)}, u32[]{:S(2)}) collective-permute-start(f32[2,2,128,256]{3,2,1,0:T(8,128)} %pad_maximum_fusion.1), channel_id=1, source_target_pairs={{0,7},{1,0},{2,1},{3,2},{4,3},{5,4},{6,5},{7,6},{8,15},{9,8},{10,9... | collective-permute-start | bytes 1572872 | tf_op jit(solution)/shard_map/ppermute | solution.py:236
  6.3 5.3 %copy-start = (bf16[2,256,256]{2,1,0:T(8,128)(2,1)S(1)}, bf16[2,256,256]{2,1,0:T(8,128)(2,1)}, u32[]{:S(2)}) copy-start(bf16[2,256,256]{2,1,0:T(8,128)(2,1)} %constant.5.clone.refs_4_.refs_5_) | copy-start | bytes 786436
  6.4 5.3 %copy-start.1 = (bf16[2,256,256]{2,1,0:T(8,128)(2,1)S(1)}, bf16[2,256,256]{2,1,0:T(8,128)(2,1)}, u32[]{:S(2)}) copy-start(bf16[2,256,256]{2,1,0:T(8,128)(2,1)} %constant.4.clone.refs_3_.refs_4_) | copy-start | bytes 786436
  6.4 5.3 %copy-start.5 = (f32[1,4,2,128,128]{4,3,2,1,0:T(8,128)S(1)}, f32[1,4,2,128,128]{4,3,2,1,0:T(8,128)}, u32[]{:S(2)}) copy-start(f32[1,4,2,128,128]{4,3,2,1,0:T(8,128)} %param.11) | copy-start | bytes 1572868
  20.0 11.7 %copy-start.4 = (f32[2,128,128]{2,1,0:T(8,128)S(1)}, f32[2,128,128]{2,1,0:T(8,128)}, u32[]{:S(2)}) copy-start(f32[2,128,128]{2,1,0:T(8,128)} %refs_3_.10) | copy-start | bytes 393220
  20.0 11.6 %collective-permute-start.2 = (f32[2,2,128,128]{3,2,1,0:T(8,128)S(1)}, f32[2,2,128,128]{3,2,1,0:T(8,128)S(1)}, u32[]{:S(2)}, u32[]{:S(2)}) collective-permute-start(f32[2,2,128,128]{3,2,1,0:T(8,128)S(1)} %get-tuple-element.12), channel_id=1, source_target_pairs={{0,8},{8,16},{16,24},{24,32},{32,40},{40,48},{48,56},{56,64},{64,7... | collective-permute-start | bytes 786440 | tf_op jit(solution)/shard_map/ppermute | solution.py:282
  26.0 11.5 %collective-permute-start.3 = (f32[2,2,128,128]{3,2,1,0:T(8,128)S(1)}, f32[2,2,128,128]{3,2,1,0:T(8,128)S(1)}, u32[]{:S(2)}, u32[]{:S(2)}) collective-permute-start(f32[2,2,128,128]{3,2,1,0:T(8,128)S(1)} %leave1.1), channel_id=1, source_target_pairs={{0,8},{8,16},{16,24},{24,32},{32,40},{40,48},{48,56},{56,64},{64,7... | collective-permute-start | bytes 786440 | tf_op jit(solution)/shard_map/ppermute | solution.py:282
  35.5 10.6 %collective-permute-start.4 = (f32[2,2,128,128]{3,2,1,0:T(8,128)S(1)}, f32[2,2,128,128]{3,2,1,0:T(8,128)S(1)}, u32[]{:S(2)}, u32[]{:S(2)}) collective-permute-start(f32[2,2,128,128]{3,2,1,0:T(8,128)S(1)} %tick1_0.1), channel_id=1, source_target_pairs={{0,8},{8,16},{16,24},{24,32},{32,40},{40,48},{48,56},{56,64},{64,7... | collective-permute-start | bytes 786440 | tf_op jit(solution)/shard_map/ppermute | solution.py:282
  41.3 10.6 %collective-permute-start.5 = (f32[2,2,128,128]{3,2,1,0:T(8,128)S(1)}, f32[2,2,128,128]{3,2,1,0:T(8,128)S(1)}, u32[]{:S(2)}, u32[]{:S(2)}) collective-permute-start(f32[2,2,128,128]{3,2,1,0:T(8,128)S(1)} %tick1_1.1), channel_id=1, source_target_pairs={{0,8},{8,16},{16,24},{24,32},{32,40},{40,48},{48,56},{56,64},{64,7... | collective-permute-start | bytes 786440 | tf_op jit(solution)/shard_map/ppermute | solution.py:282

commit v2 on v1

--- a/solution.py
+++ b/solution.py
@@ -12,7 +12,7 @@
 
 TICKS = 3
 CHUNKS = 2
-RIM_CHUNKS = 2
+RIM_CHUNKS = 4
 
 fresnel = 0.1
 VMEM_LIMIT = 24 * 1024 * 1024
@@ -61,7 +61,6 @@
 
 def trans_kernel(phase_ref, absorb_ref, out_ref):
     size = out_ref.shape[-1]
-    rows = phase_ref.shape[1]
     step = 32
 
     def body(i, carry):
@@ -74,11 +73,69 @@
                 out_ref[layer, 1, half, at, :] = imag
         return carry
 
-    lax.fori_loop(0, rows // step, body, 0)
+    lax.fori_loop(0, phase_ref.shape[1] // step, body, 0)
+
+
+def trans_rows(phase_map, absorb, size, layers, block, name):
+    count = len(layers)
+    columns = phase_map.shape[2]
+    at = layers[0] // count
+    spec = pl.BlockSpec((count, size, columns), lambda i: (at, block, 0))
+    values = count * size * columns
+    return pl.pallas_call(
+        trans_kernel,
+        grid=(1,),
+        out_shape=jax.ShapeDtypeStruct((count, 2, columns // size, size, size), jnp.float32),
+        in_specs=[spec] * 2,
+        out_specs=vmem(),
+        compiler_params=pltpu.CompilerParams(vmem_limit_bytes=VMEM_LIMIT),
+        cost_estimate=pl.CostEstimate(
+            flops=values * 40, bytes_accessed=values * 16, transcendentals=values
+        ),
+        name=name,
+    )(phase_map, absorb)
+
+
+def store_kernel(tick, count, *refs):
+    parts = refs[:count]
+    out, sem = refs[-2:]
+    copies = []
+    at = 0
+    for part in parts:
+        copies.append(
+            pltpu.make_async_copy(
+                part, out.at[tick, pl.ds(at, part.shape[0])], sem.at[len(copies)]
+            )
+        )
+        copies[-1].start()
+        at += part.shape[0]
+    for copy in copies:
+        copy.wait()
+
+
+def store(tick, parts, out, out_shape):
+    count = len(parts)
+    operands = list(parts)
+    specs = [vmem()] * count
+    aliases = {}
+    if out is not None:
+        aliases = {count: 0}
+        operands.append(out)
+        specs.append(pl.BlockSpec(memory_space=pltpu.HBM))
+    return pl.pallas_call(
+        functools.partial(store_kernel, tick, count),
+        out_shape=out_shape,
+        in_specs=specs,
+        out_specs=pl.BlockSpec(memory_space=pltpu.HBM),
+        input_output_aliases=aliases,
+        scratch_shapes=[pltpu.SemaphoreType.DMA((count,))],
+        compiler_params=pltpu.CompilerParams(vmem_limit_bytes=VMEM_LIMIT),
+        name=f"store{tick}",
+    )(*operands)
 
 
 def section_kernel(
-    tick, layers, probes, with_rim, starts, ends, with_probe, tile_rows, *refs
+    tick, layers, probes, with_rim, starts, ends, with_probe, with_out, tile_rows, *refs
 ):
     refs = list(refs)
     rows_ref, cols_ref = refs.pop(0), refs.pop(0)
@@ -87,12 +144,18 @@
     right_ref, left_ref = refs.pop(0), refs.pop(0)
     count = len(layers)
     if with_rim:
-        whole_ref, rim_ref = refs.pop(0), refs.pop(0)
+        piece_refs = [refs.pop(0) for _ in range(3)]
         out_ref = refs.pop(0)
         ext_refs = [refs.pop(0) for _ in range(count)]
     else:
         ext_refs = [refs.pop(0) for _ in range(count)]
+        if with_out:
+            refs.pop(0)
         out_ref = refs.pop(0)
+    if with_out:
+        final_ref = out_ref
+        out_ref = refs.pop()
+        sem = refs.pop()
     state, x_high, x_low, r_high, r_low = refs
 
     size = out_ref.shape[-1]
@@ -115,14 +178,11 @@
     for j in range(count):
         ext = ext_refs[j]
         if with_rim:
-            for part in range(2):
-                for half in range(2):
-                    ext[part, half, :tile_rows, :] = whole_ref[j, part, half]
-            for half in range(2):
-                cols = slice(half * size, (half + 1) * size)
-                real, imag = transmission(rim_ref[0, j, :, cols], rim_ref[1, j, :, cols])
-                ext[0, half, tile_rows:, :] = real
-                ext[1, half, tile_rows:, :] = imag
+            for piece, piece_ref in enumerate(piece_refs):
+                rows = slice(piece * size, (piece + 1) * size)
+                for part in range(2):
+                    for half in range(2):
+                        ext[part, half, rows, :] = piece_ref[j, part, half]
         for n in range(len(probes)):
             at = pl.ds(row_at[n], size)
             inside = lane >= col_at[n]
@@ -156,6 +216,12 @@
                     out_ref[n, part] = wave
                 else:
                     state[n, part] = wave
+    if with_out:
+        copy = pltpu.make_async_copy(
+            out_ref, final_ref.at[tick, pl.ds(probes[0], len(probes))], sem
+        )
+        copy.start()
+        copy.wait()
 
 
 def vmem():
@@ -163,11 +229,11 @@
 
 
 def section(
-    tick, layers, probes, scans, tables, wave, *, whole=None, rim=None, exts=None,
-    probe_wave=None, starts, ends, tile_rows, name
+    tick, layers, probes, scans, tables, wave, *, pieces=None, exts=None,
+    probe_wave=None, out=None, starts, ends, tile_rows, name
 ):
     size = wave.shape[-1]
-    with_rim = rim is not None
+    with_rim = pieces is not None
     count = len(layers)
     n = len(probes)
     operands = [*scans, wave]
@@ -182,12 +248,11 @@
     out_shape = [jax.ShapeDtypeStruct((n, 2, size, size), jnp.float32)]
     out_specs = [vmem()]
     if with_rim:
-        operands += [whole, rim]
-        block = layers[0] // count
-        specs += [
-            pl.BlockSpec((count, 2, 2, tile_rows, size), lambda i: (block, 0, 0, 0, 0)),
-            vmem(),
-        ]
+        operands += [piece for piece, _ in pieces]
+        for _, at in pieces:
+            specs.append(
+                pl.BlockSpec((count, 2, 2, size, size), lambda i, at=at: (at, 0, 0, 0, 0))
+            )
         out_shape += [
             jax.ShapeDtypeStruct((2, 2, tile_rows + size, size), jnp.float32)
         ] * count
@@ -195,12 +260,22 @@
     else:
         operands += list(exts)
         specs += [vmem()] * count
+    aliases = {}
+    scratch = []
+    if out is not None:
+        aliases = {len(operands): 0}
+        operands.append(out)
+        specs.append(pl.BlockSpec(memory_space=pltpu.HBM))
+        out_shape = [jax.ShapeDtypeStruct(out.shape, out.dtype)]
+        out_specs = [pl.BlockSpec(memory_space=pltpu.HBM)]
+        scratch = [pltpu.SemaphoreType.DMA, pltpu.VMEM((n, 2, size, size), jnp.float32)]
     flops = count * n * 2 * 3 * 2 * size * (2 * size) ** 2
     return pl.pallas_call(
         functools.partial(
             section_kernel, tick, layers, probes, with_rim, starts, ends,
-            probe_wave is not None, tile_rows,
+            probe_wave is not None, out is not None, tile_rows,
         ),
+        input_output_aliases=aliases,
         grid=(1,),
         in_specs=specs,
         out_specs=out_specs,
@@ -211,6 +286,7 @@
             pltpu.VMEM((n * size, 2 * size), jnp.bfloat16),
             pltpu.VMEM((2 * size, n * size), jnp.bfloat16),
             pltpu.VMEM((2 * size, n * size), jnp.bfloat16),
+            *scratch,
         ],
         compiler_params=pltpu.CompilerParams(vmem_limit_bytes=VMEM_LIMIT),
         cost_estimate=pl.CostEstimate(
@@ -226,69 +302,57 @@
     tiles = lax.axis_size("tile")
     depth_count = lax.axis_size("depth")
     back = [(i, (i - 1) % tiles) for i in range(tiles)]
-    onward = [(i, i + 1) for i in range(depth_count - 1)]
+    onward = [(i, (i + 1) % depth_count) for i in range(depth_count)]
 
     per_rim = slices // RIM_CHUNKS
-    rims = []
-    for r in range(RIM_CHUNKS):
-        at = slice(r * per_rim, (r + 1) * per_rim)
-        own = jnp.stack([phase_map[at, :size], absorb[at, :size]])
-        rims.append(lax.ppermute(own, "tile", back))
+    spans = [list(range(r * per_rim, (r + 1) * per_rim)) for r in range(RIM_CHUNKS)]
+    firsts, rims = [], []
+    for r, layers in enumerate(spans):
+        firsts.append(trans_rows(phase_map, absorb, size, layers, 0, f"rim{r}"))
+        rims.append(lax.ppermute(firsts[-1], "tile", back))
+    rest = trans_rows(phase_map, absorb, size, list(range(slices)), 1, "rest")
 
     tables = [jnp.asarray(table) for table in hop_tables(size)]
     scans = (scan_rows, scan_cols)
-    whole = pl.pallas_call(
-        trans_kernel,
-        out_shape=jax.ShapeDtypeStruct((slices, 2, 2, tile_rows, size), jnp.float32),
-        in_specs=[vmem()] * 2,
-        out_specs=vmem(),
-        compiler_params=pltpu.CompilerParams(vmem_limit_bytes=VMEM_LIMIT),
-        cost_estimate=pl.CostEstimate(
-            flops=slices * tile_rows * 2 * size * 40,
-            bytes_accessed=slices * tile_rows * 2 * size * 16,
-            transcendentals=slices * tile_rows * 2 * size,
-        ),
-        name="trans",
-    )(phase_map, absorb)
-
     held = waves_in[0]
     count = held.shape[0]
     per_chunk = count // CHUNKS
     groups = [list(range(c * per_chunk, (c + 1) * per_chunk)) for c in range(CHUNKS)]
     exts = []
-    for r in range(RIM_CHUNKS - 1):
-        layers = list(range(r * per_rim, (r + 1) * per_rim))
-        held, *made = section(
-            0, layers, list(range(count)), scans, tables, held, whole=whole, rim=rims[r],
-            starts=r == 0, ends=False, tile_rows=tile_rows, name=f"enter{r}",
-        )
-        exts += made
-    results = [[]]
-    layers = list(range(slices - per_rim, slices))
-    for c, group in enumerate(groups):
-        rest = dict(starts=RIM_CHUNKS == 1, ends=True, tile_rows=tile_rows, name=f"leave{c}")
-        if c == 0:
-            done, *made = section(
-                0, layers, group, scans, tables, held, whole=whole, rim=rims[-1], **rest
+    done = []
+    for r, layers in enumerate(spans):
+        pieces = [(firsts[r], 0), (rest, r), (rims[r], 0)]
+        common = dict(starts=r == 0, ends=r == RIM_CHUNKS - 1, tile_rows=tile_rows)
+        if r < RIM_CHUNKS - 1:
+            held, *made = section(
+                0, layers, list(range(count)), scans, tables, held, pieces=pieces,
+                name=f"enter{r}", **common,
             )
             exts += made
-        else:
-            (done,) = section(
-                0, layers, group, scans, tables, held, exts=exts[-per_rim:], **rest
-            )
-        results[0].append(done)
-
+            continue
+        for c, group in enumerate(groups):
+            sources = dict(pieces=pieces) if c == 0 else dict(exts=exts[-per_rim:])
+            left, *made = section(
+                0, layers, group, scans, tables, held, name=f"leave{c}", **sources, **common
+            )
+            exts += made
+            done.append(left)
+
+    out = None
     for tick in range(1, TICKS):
-        arrived = [lax.ppermute(done, "depth", onward) for done in results[-1]]
-        results.append([])
+        arrived = [lax.ppermute(left, "depth", onward) for left in done]
+        out_shape = jax.ShapeDtypeStruct((TICKS, *held.shape), held.dtype)
+        out = store(tick - 1, done, out, out_shape)
+        done = []
         for c, group in enumerate(groups):
-            (done,) = section(
+            (left,) = section(
                 tick, list(range(slices)), group, scans, tables, arrived[c], exts=exts,
-                probe_wave=probe_wave, starts=True, ends=True, tile_rows=tile_rows,
-                name=f"tick{tick}_{c}",
-            )
-            results[-1].append(done)
-    out = jnp.stack([jnp.concatenate(parts, 0) for parts in results])
+                probe_wave=probe_wave, out=out if tick == TICKS - 1 else None,
+                starts=True, ends=True, tile_rows=tile_rows, name=f"tick{tick}_{c}",
+            )
+            if tick == TICKS - 1:
+                out = left
+            done.append(left)
     return out[:, None]
 
 

time: 58 us -> 56.9 us (0.981)
  the two profiles are of different devices: /device:TPU:96 before, /device:TPU:0 now
where the time goes in v2:
time: 56.9 us; the launch traced here: 56.6 us
  Pallas kernels  29.8 us (52%)
  waiting for transfers between devices  16.3 us (29%)
  starting transfers between devices  7.39 us (13%)
  local copies, waits for them, and re-layouts  2.93 us (5%)
    pallas_call x9, Pallas kernels, section(): pl.pallas_call(functools.partial(section_kernel, tick, layers, probes, wi...  26.7 us
    ppermute x4, waiting for transfers between devices, shards(): arrived = [lax.ppermute(left, 'depth', onward) for left in done]  13.8 us
    ppermute x4, starting transfers between devices, shards(): rims.append(lax.ppermute(firsts[-1], 'tile', back))  4.12 us
    ppermute x4, starting transfers between devices, shards(): arrived = [lax.ppermute(left, 'depth', onward) for left in done]  3.27 us
    unnamed x22, local copies, waits for them, and re-layouts  2.93 us
    ppermute x4, waiting for transfers between devices, shards(): rims.append(lax.ppermute(firsts[-1], 'tile', back))  2.54 us
    pallas_call x2, Pallas kernels, store(): pl.pallas_call(functools.partial(store_kernel, tick, count), out_shape=ou...  1.62 us
    pallas_call x5, Pallas kernels, trans_rows(): pl.pallas_call(trans_kernel, grid=(1,), out_shape=jax.ShapeDtypeStruct((c...  1.49 us
  transfers between devices with their start and end apart: 8, of which 8 were waited for; matrix products, arithmetic and copies ran while one was open for 0% of the time, Pallas kernels for 41%

profile of v2, /device:TPU:0, one launch (start us, length us, event | category | flops | bytes accessed | tf_op | source)
XLA Modules:
  0.0 56.6 jit_solution(11998951650277279644)
XLA Ops:
  0.0 0.0 copy-start
  0.0 1.2 %copy-done = f32[4,256,256]{2,1,0:T(8,128)S(1)} copy-done((f32[4,256,256]{2,1,0:T(8,128)S(1)}, f32[4,256,256]{2,1,0:T(8,128)}, u32[]{:S(2)}) %copy-start) | copy-done | bytes 1048600
  1.2 0.0 copy-start.2
  1.2 1.2 %copy-done.2 = f32[4,256,256]{2,1,0:T(8,128)S(1)} copy-done((f32[4,256,256]{2,1,0:T(8,128)S(1)}, f32[4,256,256]{2,1,0:T(8,128)}, u32[]{:S(2)}) %copy-start.2) | copy-done | bytes 1048600
  2.5 0.2 rim0.1.refs_5_
  2.6 2.5 %collective-permute-start = (f32[1,2,2,128,128]{4,3,2,1,0:T(8,128)S(1)}, f32[1,2,2,128,128]{4,3,2,1,0:T(8,128)}, u32[]{:S(2)}, u32[]{:S(2)}) collective-permute-start(f32[1,2,2,128,128]{4,3,2,1,0:T(8,128)S(1)} %rim0.1.refs_5_), channel_id=1, source_target_pairs={{0,7},{1,0},{2,1},{3,2},{4,3},{5,4},{6,5},{7,6},{8,15},{9,8},{10,9... | collective-permute-start | bytes 786440 | tf_op jit(solution)/shard_map/ppermute | solution.py:312
  5.2 0.2 rim1.1.refs_5_
  5.4 0.7 %collective-permute-start.1 = (f32[1,2,2,128,128]{4,3,2,1,0:T(8,128)S(1)}, f32[1,2,2,128,128]{4,3,2,1,0:T(8,128)}, u32[]{:S(2)}, u32[]{:S(2)}) collective-permute-start(f32[1,2,2,128,128]{4,3,2,1,0:T(8,128)S(1)} %rim1.1.refs_5_), channel_id=1, source_target_pairs={{0,7},{1,0},{2,1},{3,2},{4,3},{5,4},{6,5},{7,6},{8,15},{9,8},{10,9... | collective-permute-start | bytes 786440 | tf_op jit(solution)/shard_map/ppermute | solution.py:312
  6.1 0.2 rim2.1.refs_5_
  6.3 0.0 copy-start.8
  6.3 0.0 copy-start.9
  6.3 0.0 copy-start.1
  6.3 0.0 copy-start.3
  6.3 0.2 collective-permute-start.2
  6.5 0.2 rim3.1.refs_5_
  6.7 0.7 %collective-permute-start.3 = (f32[1,2,2,128,128]{4,3,2,1,0:T(8,128)S(1)}, f32[1,2,2,128,128]{4,3,2,1,0:T(8,128)S(1)}, u32[]{:S(2)}, u32[]{:S(2)}) collective-permute-start(f32[1,2,2,128,128]{4,3,2,1,0:T(8,128)S(1)} %rim3.1.refs_5_), channel_id=1, source_target_pairs={{0,7},{1,0},{2,1},{3,2},{4,3},{5,4},{6,5},{7,6},{8,15},{9,8},{10,9... | collective-permute-start | bytes 786440 | tf_op jit(solution)/shard_map/ppermute | solution.py:312
  7.4 0.0 copy-done.8
  7.4 0.1 copy.28.refs_0_
  7.5 0.0 copy-done.9
  7.5 0.1 copy.29.refs_1_
  7.6 0.0 copy-done.1
  7.6 0.3 copy-done.3
  7.8 0.0 copy-start.4
  7.8 0.0 copy-start.5
  7.8 0.0 copy-start.7
  7.8 0.8 %rest.1.refs_6_ = f32[4,2,2,128,128]{4,3,2,1,0:T(8,128)S(1)} custom-call(f32[4,256,256]{2,1,0:T(8,128)S(1)} %copy-done.1, f32[4,256,256]{2,1,0:T(8,128)S(1)} %copy-done.3), custom_call_target="tpu_custom_call" | custom-call | flops 5242880 | bytes 2097152 | tf_op jit(solution)/shard_map/rest/pallas_call | solution.py:85
  8.6 0.5 collective-permute-done.refs_7_
  9.1 0.0 copy-done.4
  9.1 0.0 copy-done.5
  9.1 0.0 copy-done.7
  9.1 2.2 %enter0.1 = (f32[4,2,128,128]{3,2,1,0:T(8,128)S(1)}, f32[2,2,384,128]{3,2,1,0:T(8,128)S(1)}) custom-call(s32[18,4]{1,0:T(8,128)S(1)} %copy.28.refs_0_, s32[18,4]{1,0:T(8,128)S(1)} %copy.29.refs_1_, f32[4,2,128,128]{3,2,1,0:T(8,128)S(1)} %bitcast.4, bf16[2,256,256]{2,1,0:T(8,128)(2,1)S(1)} %copy-done.4, bf16[2,256,256]{2,1,0:T(8,128)(2,1)S(1)} %copy-done.5, ...), custom_call_target="tpu_custom_call" | custom-call | flops 402653184 | bytes 786432 | tf_op jit(solution)/shard_map/enter0/pallas_call | solution.py:273
  11.2 0.6 %collective-permute-done.1.refs_7_ = f32[1,2,2,128,128]{4,3,2,1,0:T(8,128)} collective-permute-done((f32[1,2,2,128,128]{4,3,2,1,0:T(8,128)S(1)}, f32[1,2,2,128,128]{4,3,2,1,0:T(8,128)}, u32[]{:S(2)}, u32[]{:S(2)}) %collective-permute-start.1) | collective-permute-done | bytes 262176 | tf_op jit(solution)/shard_map/ppermute | solution.py:312
  11.9 2.1 %enter1.1 = (f32[4,2,128,128]{3,2,1,0:T(8,128)S(1)}, f32[2,2,384,128]{3,2,1,0:T(8,128)S(1)}) custom-call(s32[18,4]{1,0:T(8,128)S(1)} %copy.28.refs_0_, s32[18,4]{1,0:T(8,128)S(1)} %copy.29.refs_1_, f32[4,2,128,128]{3,2,1,0:T(8,128)S(1)} %get-tuple-element.13.refs_2_, bf16[2,256,256]{2,1,0:T(8,128)(2,1)S(1)} %copy-done.4, bf16[2,256,256]{2,1,0:T(8,128)(2,1)S(1)} %copy-done.5, ...), custom_call_target="tpu_custom_call" | custom-call | flops 402653184 | bytes 786432 | tf_op jit(solution)/shard_map/enter1/pallas_call | solution.py:273
  14.0 0.7 %collective-permute-done.2.refs_7_ = f32[1,2,2,128,128]{4,3,2,1,0:T(8,128)} collective-permute-done((f32[1,2,2,128,128]{4,3,2,1,0:T(8,128)S(1)}, f32[1,2,2,128,128]{4,3,2,1,0:T(8,128)}, u32[]{:S(2)}, u32[]{:S(2)}) %collective-permute-start.2) | collective-permute-done | bytes 262176 | tf_op jit(solution)/shard_map/ppermute | solution.py:312
  14.7 2.1 %enter2.1 = (f32[4,2,128,128]{3,2,1,0:T(8,128)S(1)}, f32[2,2,384,128]{3,2,1,0:T(8,128)S(1)}) custom-call(s32[18,4]{1,0:T(8,128)S(1)} %copy.28.refs_0_, s32[18,4]{1,0:T(8,128)S(1)} %copy.29.refs_1_, f32[4,2,128,128]{3,2,1,0:T(8,128)S(1)} %get-tuple-element.14.refs_2_, bf16[2,256,256]{2,1,0:T(8,128)(2,1)S(1)} %copy-done.4, bf16[2,256,256]{2,1,0:T(8,128)(2,1)S(1)} %copy-done.5, ...), custom_call_target="tpu_custom_call" | custom-call | flops 402653184 | bytes 786432 | tf_op jit(solution)/shard_map/enter2/pallas_call | solution.py:273
  16.8 0.7 %collective-permute-done.3.refs_7_ = f32[1,2,2,128,128]{4,3,2,1,0:T(8,128)S(1)} collective-permute-done((f32[1,2,2,128,128]{4,3,2,1,0:T(8,128)S(1)}, f32[1,2,2,128,128]{4,3,2,1,0:T(8,128)S(1)}, u32[]{:S(2)}, u32[]{:S(2)}) %collective-permute-start.3) | collective-permute-done | bytes 262176 | tf_op jit(solution)/shard_map/ppermute | solution.py:312
  17.5 1.8 %leave0.1 = (f32[2,2,128,128]{3,2,1,0:T(8,128)S(1)}, f32[2,2,384,128]{3,2,1,0:T(8,128)S(1)}) custom-call(s32[18,4]{1,0:T(8,128)S(1)} %copy.28.refs_0_, s32[18,4]{1,0:T(8,128)S(1)} %copy.29.refs_1_, f32[4,2,128,128]{3,2,1,0:T(8,128)S(1)} %get-tuple-element.15.refs_2_, bf16[2,256,256]{2,1,0:T(8,128)(2,1)S(1)} %copy-done.4, bf16[2,256,256]{2,1,0:T(8,128)(2,1)S(1)} %copy-done.5, ...), custom_call_target="tpu_custom_call" | custom-call | flops 201326592 | bytes 786432 | tf_op jit(solution)/shard_map/leave0/pallas_call | solution.py:273
  19.3 0.0 copy-start.6
  19.3 1.6 %collective-permute-start.6 = (f32[2,2,128,128]{3,2,1,0:T(8,128)S(1)}, f32[2,2,128,128]{3,2,1,0:T(8,128)S(1)}, u32[]{:S(2)}, u32[]{:S(2)}) collective-permute-start(f32[2,2,128,128]{3,2,1,0:T(8,128)S(1)} %get-tuple-element.20.refs_0_), channel_id=1, source_target_pairs={{0,8},{8,16},{16,24},{24,32},{32,40},{40,48},{48,56},{56,64},{64,7... | collective-permute-start | bytes 786440 | tf_op jit(solution)/shard_map/ppermute | solution.py:343
  20.8 1.7 %leave1.1.refs_1_ = f32[2,2,128,128]{3,2,1,0:T(8,128)S(1)} custom-call(s32[18,4]{1,0:T(8,128)S(1)} %copy.28.refs_0_, s32[18,4]{1,0:T(8,128)S(1)} %copy.29.refs_1_, f32[4,2,128,128]{3,2,1,0:T(8,128)S(1)} %get-tuple-element.15.refs_2_, bf16[2,256,256]{2,1,0:T(8,128)(2,1)S(1)} %copy-done.4, bf16[2,256,256]{2,1,0:T(8,128)(2,1)S(1)} %copy-done.5, ...), custom_call_target="tpu_custom_call" | custom-call | flops 201326592 | bytes 786432 | tf_op jit(solution)/shard_map/leave1/pallas_call | solution.py:273
  22.6 1.6 %collective-permute-start.4 = (f32[2,2,128,128]{3,2,1,0:T(8,128)S(1)}, f32[2,2,128,128]{3,2,1,0:T(8,128)S(1)}, u32[]{:S(2)}, u32[]{:S(2)}) collective-permute-start(f32[2,2,128,128]{3,2,1,0:T(8,128)S(1)} %leave1.1.refs_1_), channel_id=1, source_target_pairs={{0,8},{8,16},{16,24},{24,32},{32,40},{40,48},{48,56},{56,64},{64,7... | collective-permute-start | bytes 786440 | tf_op jit(solution)/shard_map/ppermute | solution.py:343
  24.1 8.7 %collective-permute-done.6.refs_2_ = f32[2,2,128,128]{3,2,1,0:T(8,128)S(1)} collective-permute-done((f32[2,2,128,128]{3,2,1,0:T(8,128)S(1)}, f32[2,2,128,128]{3,2,1,0:T(8,128)S(1)}, u32[]{:S(2)}, u32[]{:S(2)}) %collective-permute-start.6) | collective-permute-done | bytes 262176 | tf_op jit(solution)/shard_map/ppermute | solution.py:343
  32.8 0.0 copy-done.6
  32.8 3.8 %tick1_0.1.refs_0_ = f32[2,2,128,128]{3,2,1,0:T(8,128)S(1)} custom-call(s32[18,4]{1,0:T(8,128)S(1)} %copy.28.refs_0_, s32[18,4]{1,0:T(8,128)S(1)} %copy.29.refs_1_, f32[2,2,128,128]{3,2,1,0:T(8,128)S(1)} %collective-permute-done.6.refs_2_, f32[2,128,128]{2,1,0:T(8,128)S(1)} %copy-done.6, bf16[2,256,256]{2,1,0:T(8,128)(2,1)S(1)} %copy-done.4, ...), custom_call_target="tpu_custom_call" | custom-call | flops 805306368 | bytes 3145728 | tf_op jit(solution)/shard_map/tick1_0/pallas_call | solution.py:273
  36.6 0.1 collective-permute-start.7
  36.7 0.4 collective-permute-done.4.refs_2_
  37.1 3.9 %tick1_1.1.refs_1_ = f32[2,2,128,128]{3,2,1,0:T(8,128)S(1)} custom-call(s32[18,4]{1,0:T(8,128)S(1)} %copy.28.refs_0_, s32[18,4]{1,0:T(8,128)S(1)} %copy.29.refs_1_, f32[2,2,128,128]{3,2,1,0:T(8,128)S(1)} %collective-permute-done.4.refs_2_, f32[2,128,128]{2,1,0:T(8,128)S(1)} %copy-done.6, bf16[2,256,256]{2,1,0:T(8,128)(2,1)S(1)} %copy-done.4, ...), custom_call_target="tpu_custom_call" | custom-call | flops 805306368 | bytes 3145728 | tf_op jit(solution)/shard_map/tick1_1/pallas_call | solution.py:273
  40.9 0.1 collective-permute-start.5
  41.0 0.8 %store0.1.refs_2_ = f32[3,4,2,128,128]{4,3,2,1,0:T(8,128)} custom-call(f32[2,2,128,128]{3,2,1,0:T(8,128)S(1)} %get-tuple-element.20.refs_0_, f32[2,2,128,128]{3,2,1,0:T(8,128)S(1)} %leave1.1.refs_1_), custom_call_target="tpu_custom_call" | custom-call | tf_op jit(solution)/shard_map/store0/pallas_call | solution.py:125
  41.8 0.8 %store1.1.refs_10_ = f32[3,4,2,128,128]{4,3,2,1,0:T(8,128)} custom-call(f32[2,2,128,128]{3,2,1,0:T(8,128)S(1)} %tick1_0.1.refs_0_, f32[2,2,128,128]{3,2,1,0:T(8,128)S(1)} %tick1_1.1.refs_1_, f32[3,4,2,128,128]{4,3,2,1,0:T(8,128)} %store0.1.refs_2_), custom_call_target="tpu_custom_call", output_to_operand_aliasing={{}: (2, {})} | custom-call | tf_op jit(solution)/shard_map/store1/pallas_call | solution.py:125
  42.7 4.3 %collective-permute-done.7.refs_2_ = f32[2,2,128,128]{3,2,1,0:T(8,128)S(1)} collective-permute-done((f32[2,2,128,128]{3,2,1,0:T(8,128)S(1)}, f32[2,2,128,128]{3,2,1,0:T(8,128)S(1)}, u32[]{:S(2)}, u32[]{:S(2)}) %collective-permute-start.7) | collective-permute-done | bytes 262176 | tf_op jit(solution)/shard_map/ppermute | solution.py:343
  47.0 4.6 %tick2_0.1.refs_10_ = f32[3,4,2,128,128]{4,3,2,1,0:T(8,128)} custom-call(s32[18,4]{1,0:T(8,128)S(1)} %copy.28.refs_0_, s32[18,4]{1,0:T(8,128)S(1)} %copy.29.refs_1_, f32[2,2,128,128]{3,2,1,0:T(8,128)S(1)} %collective-permute-done.7.refs_2_, f32[2,128,128]{2,1,0:T(8,128)S(1)} %copy-done.6, ...), custom_call_target="tpu_custom_call", output_to_operand_aliasing={{}: (10, {})} | custom-call | flops 805306368 | bytes 3145728 | tf_op jit(solution)/shard_map/tick2_0/pallas_call | solution.py:273
  51.6 0.4 collective-permute-done.5.refs_2_
  52.0 4.6 %tick2_1.1 = f32[3,4,2,128,128]{4,3,2,1,0:T(8,128)} custom-call(s32[18,4]{1,0:T(8,128)S(1)} %copy.28.refs_0_, s32[18,4]{1,0:T(8,128)S(1)} %copy.29.refs_1_, f32[2,2,128,128]{3,2,1,0:T(8,128)S(1)} %collective-permute-done.5.refs_2_, f32[2,128,128]{2,1,0:T(8,128)S(1)} %copy-done.6, ...), custom_call_target="tpu_custom_call", output_to_operand_aliasing={{}: (10, {})} | custom-call | flops 805306368 | bytes 3145728 | tf_op jit(solution)/shard_map/tick2_1/pallas_call | solution.py:273
Async XLA Ops:
  0.0 1.2 %copy-start = (f32[4,256,256]{2,1,0:T(8,128)S(1)}, f32[4,256,256]{2,1,0:T(8,128)}, u32[]{:S(2)}) copy-start(f32[4,256,256]{2,1,0:T(8,128)} %phase_ref.9) | copy-start | bytes 3145732
  1.2 1.2 %copy-start.2 = (f32[4,256,256]{2,1,0:T(8,128)S(1)}, f32[4,256,256]{2,1,0:T(8,128)}, u32[]{:S(2)}) copy-start(f32[4,256,256]{2,1,0:T(8,128)} %absorb_ref.9) | copy-start | bytes 3145732
  2.6 6.4 %collective-permute-start = (f32[1,2,2,128,128]{4,3,2,1,0:T(8,128)S(1)}, f32[1,2,2,128,128]{4,3,2,1,0:T(8,128)}, u32[]{:S(2)}, u32[]{:S(2)}) collective-permute-start(f32[1,2,2,128,128]{4,3,2,1,0:T(8,128)S(1)} %rim0.1.refs_5_), channel_id=1, source_target_pairs={{0,7},{1,0},{2,1},{3,2},{4,3},{5,4},{6,5},{7,6},{8,15},{9,8},{10,9... | collective-permute-start | bytes 786440 | tf_op jit(solution)/shard_map/ppermute | solution.py:312
  5.4 6.5 %collective-permute-start.1 = (f32[1,2,2,128,128]{4,3,2,1,0:T(8,128)S(1)}, f32[1,2,2,128,128]{4,3,2,1,0:T(8,128)}, u32[]{:S(2)}, u32[]{:S(2)}) collective-permute-start(f32[1,2,2,128,128]{4,3,2,1,0:T(8,128)S(1)} %rim1.1.refs_5_), channel_id=1, source_target_pairs={{0,7},{1,0},{2,1},{3,2},{4,3},{5,4},{6,5},{7,6},{8,15},{9,8},{10,9... | collective-permute-start | bytes 786440 | tf_op jit(solution)/shard_map/ppermute | solution.py:312
  6.3 1.1 %copy-start.8 = (s32[18,4]{0,1:T(4,128)S(1)}, s32[18,4]{0,1:T(4,128)}, u32[]{:S(2)}) copy-start(s32[18,4]{0,1:T(4,128)} %param.12) | copy-start | bytes 868
  6.3 1.2 %copy-start.9 = (s32[18,4]{0,1:T(4,128)S(1)}, s32[18,4]{0,1:T(4,128)}, u32[]{:S(2)}) copy-start(s32[18,4]{0,1:T(4,128)} %param.13) | copy-start | bytes 868
  6.3 1.3 %copy-start.1 = (f32[4,256,256]{2,1,0:T(8,128)S(1)}, f32[4,256,256]{2,1,0:T(8,128)}, u32[]{:S(2)}) copy-start(f32[4,256,256]{2,1,0:T(8,128)} %phase_ref.9) | copy-start | bytes 3145732
  6.3 1.5 %copy-start.3 = (f32[4,256,256]{2,1,0:T(8,128)S(1)}, f32[4,256,256]{2,1,0:T(8,128)}, u32[]{:S(2)}) copy-start(f32[4,256,256]{2,1,0:T(8,128)} %absorb_ref.9) | copy-start | bytes 3145732
  6.3 8.4 %collective-permute-start.2 = (f32[1,2,2,128,128]{4,3,2,1,0:T(8,128)S(1)}, f32[1,2,2,128,128]{4,3,2,1,0:T(8,128)}, u32[]{:S(2)}, u32[]{:S(2)}) collective-permute-start(f32[1,2,2,128,128]{4,3,2,1,0:T(8,128)S(1)} %rim2.1.refs_5_), channel_id=1, source_target_pairs={{0,7},{1,0},{2,1},{3,2},{4,3},{5,4},{6,5},{7,6},{8,15},{9,8},{10,9... | collective-permute-start | bytes 786440 | tf_op jit(solution)/shard_map/ppermute | solution.py:312
  6.7 10.8 %collective-permute-start.3 = (f32[1,2,2,128,128]{4,3,2,1,0:T(8,128)S(1)}, f32[1,2,2,128,128]{4,3,2,1,0:T(8,128)S(1)}, u32[]{:S(2)}, u32[]{:S(2)}) collective-permute-start(f32[1,2,2,128,128]{4,3,2,1,0:T(8,128)S(1)} %rim3.1.refs_5_), channel_id=1, source_target_pairs={{0,7},{1,0},{2,1},{3,2},{4,3},{5,4},{6,5},{7,6},{8,15},{9,8},{10,9... | collective-permute-start | bytes 786440 | tf_op jit(solution)/shard_map/ppermute | solution.py:312
  7.8 1.2 %copy-start.4 = (bf16[2,256,256]{2,1,0:T(8,128)(2,1)S(1)}, bf16[2,256,256]{2,1,0:T(8,128)(2,1)}, u32[]{:S(2)}) copy-start(bf16[2,256,256]{2,1,0:T(8,128)(2,1)} %constant.4.clone.refs_3_.refs_4_) | copy-start | bytes 786436
  7.8 1.2 %copy-start.5 = (bf16[2,256,256]{2,1,0:T(8,128)(2,1)S(1)}, bf16[2,256,256]{2,1,0:T(8,128)(2,1)}, u32[]{:S(2)}) copy-start(bf16[2,256,256]{2,1,0:T(8,128)(2,1)} %constant.5.clone.refs_4_.refs_5_) | copy-start | bytes 786436
  7.8 1.2 %copy-start.7 = (f32[1,4,2,128,128]{4,3,2,1,0:T(8,128)S(1)}, f32[1,4,2,128,128]{4,3,2,1,0:T(8,128)}, u32[]{:S(2)}) copy-start(f32[1,4,2,128,128]{4,3,2,1,0:T(8,128)} %param.11) | copy-start | bytes 1572868
  19.3 13.5 %copy-start.6 = (f32[2,128,128]{2,1,0:T(8,128)S(1)}, f32[2,128,128]{2,1,0:T(8,128)}, u32[]{:S(2)}) copy-start(f32[2,128,128]{2,1,0:T(8,128)} %refs_3_.12) | copy-start | bytes 393220
  19.3 13.5 %collective-permute-start.6 = (f32[2,2,128,128]{3,2,1,0:T(8,128)S(1)}, f32[2,2,128,128]{3,2,1,0:T(8,128)S(1)}, u32[]{:S(2)}, u32[]{:S(2)}) collective-permute-start(f32[2,2,128,128]{3,2,1,0:T(8,128)S(1)} %get-tuple-element.20.refs_0_), channel_id=1, source_target_pairs={{0,8},{8,16},{16,24},{24,32},{32,40},{40,48},{48,56},{56,64},{64,7... | collective-permute-start | bytes 786440 | tf_op jit(solution)/shard_map/ppermute | solution.py:343
  22.6 14.5 %collective-permute-start.4 = (f32[2,2,128,128]{3,2,1,0:T(8,128)S(1)}, f32[2,2,128,128]{3,2,1,0:T(8,128)S(1)}, u32[]{:S(2)}, u32[]{:S(2)}) collective-permute-start(f32[2,2,128,128]{3,2,1,0:T(8,128)S(1)} %leave1.1.refs_1_), channel_id=1, source_target_pairs={{0,8},{8,16},{16,24},{24,32},{32,40},{40,48},{48,56},{56,64},{64,7... | collective-permute-start | bytes 786440 | tf_op jit(solution)/shard_map/ppermute | solution.py:343
  36.6 10.4 %collective-permute-start.7 = (f32[2,2,128,128]{3,2,1,0:T(8,128)S(1)}, f32[2,2,128,128]{3,2,1,0:T(8,128)S(1)}, u32[]{:S(2)}, u32[]{:S(2)}) collective-permute-start(f32[2,2,128,128]{3,2,1,0:T(8,128)S(1)} %tick1_0.1.refs_0_), channel_id=1, source_target_pairs={{0,8},{8,16},{16,24},{24,32},{32,40},{40,48},{48,56},{56,64},{64,7... | collective-permute-start | bytes 786440 | tf_op jit(solution)/shard_map/ppermute | solution.py:343
  40.9 11.1 %collective-permute-start.5 = (f32[2,2,128,128]{3,2,1,0:T(8,128)S(1)}, f32[2,2,128,128]{3,2,1,0:T(8,128)S(1)}, u32[]{:S(2)}, u32[]{:S(2)}) collective-permute-start(f32[2,2,128,128]{3,2,1,0:T(8,128)S(1)} %tick1_1.1.refs_1_), channel_id=1, source_target_pairs={{0,8},{8,16},{16,24},{24,32},{32,40},{40,48},{48,56},{56,64},{64,7... | collective-permute-start | bytes 786440 | tf_op jit(solution)/shard_map/ppermute | solution.py:343

commit v3 on v2

v3 whole, which is shorter than its diff:
```python
import functools
import math

import jax
import jax.numpy as jnp
import ml_dtypes
import numpy as np
from jax import lax
from jax.experimental import pallas as pl
from jax.experimental.pallas import tpu as pltpu
from jax.sharding import PartitionSpec as P

TICKS = 3
CHUNKS = 2
RIM_CHUNKS = 4

fresnel = 0.1
VMEM_LIMIT = 24 * 1024 * 1024

SIN_TERMS = [(-1.0) ** j / math.factorial(2 * j + 1) for j in range(7)]
COS_TERMS = [(-1.0) ** j / math.factorial(2 * j) for j in range(8)]


def hop_tables(size):
    index = np.arange(size)
    frequency = np.where(index < size // 2, index, index - size).astype(np.float64)
    k = np.exp(-1j * fresnel * math.pi * frequency**2 / size)
    lag = np.fft.ifft(k)
    g = lag[(index[:, None] - index[None, :]) % size]
    right = np.block([[g.real, g.imag], [-g.imag, g.real]])
    high = right.astype(ml_dtypes.bfloat16)
    low = (right - high.astype(np.float64)).astype(ml_dtypes.bfloat16)
    right = np.stack([high, low])
    return right, np.ascontiguousarray(right.transpose(0, 2, 1))


def series(z, terms):
    total = jnp.full_like(z, terms[-1])
    for term in terms[-2::-1]:
        total = total * z + term
    return total


def transmission(phase, absorb):
    t = 0.5 * phase
    z = t * t
    s = t * series(z, SIN_TERMS)
    c = series(z, COS_TERMS)
    damping = jnp.exp(-absorb)
    return damping * (1.0 - 2.0 * (s * s)), damping * (2.0 * (s * c))


def split(x):
    high = x.astype(jnp.bfloat16)
    return high, (x - high.astype(jnp.float32)).astype(jnp.bfloat16)


def product(a, b):
    return jnp.dot(a, b, preferred_element_type=jnp.float32)


def trans_kernel(phase_ref, absorb_ref, out_ref):
    size = out_ref.shape[-1]
    step = 32

    def body(i, carry):
        at = pl.ds(pl.multiple_of(i * step, step), step)
        for layer in range(phase_ref.shape[0]):
            for half in range(2):
                cols = slice(half * size, (half + 1) * size)
                real, imag = transmission(phase_ref[layer, at, cols], absorb_ref[layer, at, cols])
                out_ref[layer, 0, half, at, :] = real
                out_ref[layer, 1, half, at, :] = imag
        return carry

    lax.fori_loop(0, phase_ref.shape[1] // step, body, 0)


def first_trans_kernel(phase_ref, absorb_ref, out_ref, phase_buf, absorb_buf, sem):
    copies = []
    for n, (ref, buf) in enumerate([(phase_ref, phase_buf), (absorb_ref, absorb_buf)]):
        source = ref.at[pl.ds(0, buf.shape[0]), pl.ds(0, buf.shape[1])]
        copies.append(pltpu.make_async_copy(source, buf, sem.at[n]))
        copies[-1].start()
    for copy in copies:
        copy.wait()
    trans_kernel(phase_buf, absorb_buf, out_ref)


def trans_rows(phase_map, absorb, size, layers, block, name, direct=False):
    count = len(layers)
    columns = phase_map.shape[2]
    at = layers[0] // count
    spec = pl.BlockSpec((count, size, columns), lambda i: (at, block, 0))
    values = count * size * columns
    kernel, scratch = trans_kernel, []
    if direct:
        kernel = first_trans_kernel
        spec = pl.BlockSpec(memory_space=pltpu.HBM)
        scratch = [pltpu.VMEM((count, size, columns), jnp.float32)] * 2
        scratch.append(pltpu.SemaphoreType.DMA((2,)))
    return pl.pallas_call(
        kernel,
        grid=(1,),
        scratch_shapes=scratch,
        out_shape=jax.ShapeDtypeStruct((count, 2, columns // size, size, size), jnp.float32),
        in_specs=[spec] * 2,
        out_specs=vmem(),
        compiler_params=pltpu.CompilerParams(vmem_limit_bytes=VMEM_LIMIT),
        cost_estimate=pl.CostEstimate(
            flops=values * 40, bytes_accessed=values * 16, transcendentals=values
        ),
        name=name,
    )(phase_map, absorb)


def advance(
    tick, layers, probes, starts, ends, piece_refs, ext_refs, scans, waves, put, tables, scratch
):
    rows_ref, cols_ref, tile_rows = scans
    right_ref, left_ref = tables
    state, x_high, x_low, r_high, r_low = scratch
    size = state.shape[-1]
    batch = tick - lax.axis_index("depth") + lax.axis_size("depth") - 1
    offset = lax.axis_index("tile") * tile_rows
    row_at = [rows_ref[batch, p] - offset for p in probes]
    col_at = [cols_ref[batch, p] for p in probes]
    lane = lax.broadcasted_iota(jnp.int32, (size, size), 1)
    count = len(layers)

    for n in range(len(probes)):
        for part in range(2):
            wave = waves(n, part)
            if starts:
                wave = pltpu.roll(wave, col_at[n] & (size - 1), 1)
            state[n, part] = wave

    for j in range(count):
        ext = ext_refs[j]
        for piece, piece_ref in enumerate(piece_refs):
            rows = slice(piece * size, (piece + 1) * size)
            for part in range(2):
                for half in range(2):
                    ext[part, half, rows, :] = piece_ref[j, part, half]
        for n in range(len(probes)):
            at = pl.ds(row_at[n], size)
            inside = lane >= col_at[n]
            t_real = jnp.where(inside, ext[0, 0, at, :], ext[0, 1, at, :])
            t_imag = jnp.where(inside, ext[1, 0, at, :], ext[1, 1, at, :])
            real, imag = state[n, 0], state[n, 1]
            rows = slice(n * size, (n + 1) * size)
            x_high[rows, :size], x_low[rows, :size] = split(real * t_real - imag * t_imag)
            x_high[rows, size:], x_low[rows, size:] = split(real * t_imag + imag * t_real)
        y = (
            product(x_high[...], right_ref[0])
            + product(x_high[...], right_ref[1])
            + product(x_low[...], right_ref[0])
        )
        for n in range(len(probes)):
            rows = slice(n * size, (n + 1) * size)
            r_high[:size, rows], r_low[:size, rows] = split(y[rows, :size])
            r_high[size:, rows], r_low[size:, rows] = split(y[rows, size:])
        z = (
            product(left_ref[0], r_high[...])
            + product(left_ref[1], r_high[...])
            + product(left_ref[0], r_low[...])
        )
        for n in range(len(probes)):
            rows = slice(n * size, (n + 1) * size)
            for part in range(2):
                wave = z[part * size : (part + 1) * size, rows]
                if j < count - 1:
                    state[n, part] = wave
                    continue
                if ends:
                    wave = pltpu.roll(wave, (size - col_at[n]) & (size - 1), 1)
                put(n, part, wave)


def take(refs, count):
    return [refs.pop(0) for _ in range(count)]


def entry_kernel(layers, probes, with_pieces, starts, ends, tile_rows, *refs):
    refs = list(refs)
    rows_ref, cols_ref, wave_ref, right_ref, left_ref = take(refs, 5)
    if with_pieces:
        piece_refs = take(refs, 3)
        (out_ref,) = take(refs, 1)
        ext_refs = take(refs, len(layers))
    else:
        piece_refs = []
        ext_refs = take(refs, len(layers))
        (out_ref,) = take(refs, 1)

    def put(n, part, wave):
        out_ref[n, part] = wave

    advance(
        0, layers, probes, starts, ends, piece_refs, ext_refs, (rows_ref, cols_ref, tile_rows),
        lambda n, part: wave_ref[n, part], put, (right_ref, left_ref), refs,
    )


def first_kernel(tick, layers, tile_rows, *refs):
    refs = list(refs)
    rows_ref, cols_ref, probe_ref, right_ref, left_ref = take(refs, 5)
    ext_refs = take(refs, len(layers))
    _, out_ref = take(refs, 2)
    count = out_ref.shape[0]
    probes = [pl.program_id(0) * count + n for n in range(count)]

    def put(n, part, wave):
        out_ref[n, part] = wave

    @pl.when(lax.axis_index("depth") == 0)
    def _():
        advance(
            tick, layers, probes, True, True, [], ext_refs, (rows_ref, cols_ref, tile_rows),
            lambda n, part: probe_ref[part], put, (right_ref, left_ref), refs,
        )


def tick_kernel(tick, layers, probes, stores, own_store, tile_rows, *refs):
    refs = list(refs)
    rows_ref, cols_ref, wave_ref, right_ref, left_ref = take(refs, 5)
    ext_refs = take(refs, len(layers))
    (first_ref,) = take(refs, 1)
    stored_refs = take(refs, len(stores))
    if own_store:
        take(refs, 1)
        (final_ref,) = take(refs, 1)
        sem, out_ref = refs.pop(), refs.pop()
    elif stores:
        out_ref, final_ref = take(refs, 2)
        sem = refs.pop()
    else:
        (out_ref,) = take(refs, 1)

    copies = []
    for n, ((to, at), ref) in enumerate(zip(stores, stored_refs)):
        into = final_ref.at[to, pl.ds(at, ref.shape[0])]
        copies.append(pltpu.make_async_copy(ref, into, sem.at[n]))
        copies[-1].start()

    def put(n, part, wave):
        out_ref[n, part] = wave

    depth = lax.axis_index("depth")

    @pl.when(depth == 0)
    def _():
        out_ref[...] = first_ref[...]

    @pl.when(depth != 0)
    def _():
        advance(
            tick, layers, probes, True, True, [], ext_refs, (rows_ref, cols_ref, tile_rows),
            lambda n, part: wave_ref[n, part], put, (right_ref, left_ref), refs,
        )

    if own_store:
        into = final_ref.at[tick, pl.ds(probes[0], len(probes))]
        copies.append(pltpu.make_async_copy(out_ref, into, sem.at[len(stores)]))
        copies[-1].start()
    for copy in copies:
        copy.wait()


def vmem():
    return pl.BlockSpec(memory_space=pltpu.VMEM)


def smem():
    return pl.BlockSpec(memory_space=pltpu.SMEM)


def hbm():
    return pl.BlockSpec(memory_space=pltpu.HBM)


def call(kernel, operands, specs, out_shape, out_specs, n, size, layers, name, **rest):
    grid = rest.pop("grid", (1,))
    flops = grid[0] * layers * n * 2 * 3 * 2 * size * (2 * size) ** 2
    return pl.pallas_call(
        kernel,
        grid=grid,
        in_specs=specs,
        out_specs=out_specs,
        out_shape=out_shape,
        scratch_shapes=[
            pltpu.VMEM((n, 2, size, size), jnp.float32),
            pltpu.VMEM((n * size, 2 * size), jnp.bfloat16),
            pltpu.VMEM((n * size, 2 * size), jnp.bfloat16),
            pltpu.VMEM((2 * size, n * size), jnp.bfloat16),
            pltpu.VMEM((2 * size, n * size), jnp.bfloat16),
            *rest.pop("scratch", []),
        ],
        compiler_params=pltpu.CompilerParams(vmem_limit_bytes=VMEM_LIMIT),
        cost_estimate=pl.CostEstimate(
            flops=flops, bytes_accessed=layers * 2 * 2 * 384 * size * 4, transcendentals=0
        ),
        name=name,
        **rest,
    )(*operands)


def entry(layers, probes, scans, tables, wave, pieces, exts, starts, ends, tile_rows, name):
    size = wave.shape[-1]
    count, n = len(layers), len(probes)
    first = probes[0] // n if wave.shape[0] != n else 0
    operands = [*scans, wave, *tables]
    specs = [
        smem(), smem(), pl.BlockSpec((n, 2, size, size), lambda i: (first, 0, 0, 0)),
        vmem(), vmem(),
    ]
    out_shape = [jax.ShapeDtypeStruct((n, 2, size, size), jnp.float32)]
    if pieces is not None:
        operands += [piece for piece, _ in pieces]
        for _, at in pieces:
            specs.append(
                pl.BlockSpec((count, 2, 2, size, size), lambda i, at=at: (at, 0, 0, 0, 0))
            )
        out_shape += [
            jax.ShapeDtypeStruct((2, 2, tile_rows + size, size), jnp.float32)
        ] * count
    else:
        operands += exts
        specs += [vmem()] * count
    kernel = functools.partial(
        entry_kernel, layers, probes, pieces is not None, starts, ends, tile_rows
    )
    return call(
        kernel, operands, specs, out_shape, [vmem()] * len(out_shape), n, size, count, name
    )


def first_section(tick, n, scans, tables, probe_wave, exts, after, tile_rows, chunks):
    size = probe_wave.shape[-1]
    layers = list(range(len(exts)))
    return call(
        functools.partial(first_kernel, tick, layers, tile_rows),
        [*scans, probe_wave, *tables, *exts, after],
        [smem()] * 2 + [vmem()] * (3 + len(exts)) + [pl.BlockSpec(memory_space=pl.ANY)],
        jax.ShapeDtypeStruct((chunks * n, 2, size, size), jnp.float32),
        pl.BlockSpec((n, 2, size, size), lambda i: (i, 0, 0, 0)),
        n, size, len(exts), f"first{tick}", grid=(chunks,),
    )


def tick_section(
    tick, c, n, scans, tables, wave, exts, first, tile_rows, stored=(), out_shape=None, out=None
):
    size = wave.shape[-1]
    count = len(exts)
    probes = list(range(c * n, (c + 1) * n))
    operands = [*scans, wave, *tables, *exts, first, *(part for _, part in stored)]
    specs = [smem()] * 2 + [vmem()] * (3 + count)
    specs.append(pl.BlockSpec((n, 2, size, size), lambda i: (c, 0, 0, 0)))
    specs += [vmem()] * len(stored)
    shape = [jax.ShapeDtypeStruct((n, 2, size, size), jnp.float32)]
    out_specs = [vmem()]
    rest = {}
    if out is not None:
        rest["input_output_aliases"] = {len(operands): 0}
        operands.append(out)
        specs.append(hbm())
        shape, out_specs = [jax.ShapeDtypeStruct(out.shape, out.dtype)], [hbm()]
        rest["scratch"] = [
            pltpu.VMEM((n, 2, size, size), jnp.float32),
            pltpu.SemaphoreType.DMA((len(stored) + 1,)),
        ]
    elif stored:
        shape.append(out_shape)
        out_specs.append(hbm())
        rest["scratch"] = [pltpu.SemaphoreType.DMA((len(stored),))]
    kernel = functools.partial(
        tick_kernel, tick, list(range(count)), probes, [to for to, _ in stored],
        out is not None, tile_rows,
    )
    return call(
        kernel, operands, specs, shape, out_specs, n, size, count, f"tick{tick}_{c}", **rest
    )


def shards(phase_map, absorb, probe_wave, waves_in, scan_rows, scan_cols):
    size = probe_wave.shape[-1]
    slices, tile_rows = phase_map.shape[:2]
    tiles = lax.axis_size("tile")
    depth_count = lax.axis_size("depth")
    back = [(i, (i - 1) % tiles) for i in range(tiles)]
    onward = [(i, (i + 1) % depth_count) for i in range(depth_count)]

    per_rim = slices // RIM_CHUNKS
    spans = [list(range(r * per_rim, (r + 1) * per_rim)) for r in range(RIM_CHUNKS)]
    firsts, rims = [], []
    for r, layers in enumerate(spans):
        firsts.append(trans_rows(phase_map, absorb, size, layers, 0, f"rim{r}", r == 0))
        rims.append(lax.ppermute(firsts[-1], "tile", back))
    rest = trans_rows(phase_map, absorb, size, list(range(slices)), 1, "rest")

    tables = [jnp.asarray(table) for table in hop_tables(size)]
    scans = (scan_rows, scan_cols)
    held = waves_in[0]
    count = held.shape[0]
    per_chunk = count // CHUNKS
    groups = [list(range(c * per_chunk, (c + 1) * per_chunk)) for c in range(CHUNKS)]
    exts = []
    done = []
    for r, layers in enumerate(spans):
        pieces = [(firsts[r], 0), (rest, r), (rims[r], 0)]
        edges = (r == 0, r == RIM_CHUNKS - 1, tile_rows)
        if r < RIM_CHUNKS - 1:
            held, *made = entry(
                layers, list(range(count)), scans, tables, held, pieces, None, *edges, f"enter{r}"
            )
            exts += made
            continue
        for c, group in enumerate(groups):
            sources = (pieces, None) if c == 0 else (None, exts[-per_rim:])
            left, *made = entry(
                layers, group, scans, tables, held, *sources, *edges, f"leave{c}"
            )
            exts += made
            done.append(left)

    stored = []
    for tick in range(1, TICKS):
        stored += [((tick - 1, c * per_chunk), part) for c, part in enumerate(done)]
        arrived = [lax.ppermute(left, "depth", onward) for left in done]
        first = first_section(
            tick, per_chunk, scans, tables, probe_wave, exts, done[-1], tile_rows, CHUNKS
        )
        done = []
        out = None
        for c in range(CHUNKS):
            last = {}
            if tick == TICKS - 1:
                shape = jax.ShapeDtypeStruct((TICKS, count, *held.shape[1:]), held.dtype)
                last = dict(stored=stored, out_shape=shape)
                if c == CHUNKS - 1:
                    last = dict(stored=stored, out=out)
            left, *made = tick_section(
                tick, c, per_chunk, scans, tables, arrived[c], exts, first, tile_rows, **last
            )
            if made:
                out = made[0]
                stored = [((tick, c * per_chunk), left)]
            done.append(left)
    out = done[-1]
    return out[:, None]


def solution(mesh):
    return jax.shard_map(
        shards,
        mesh=mesh,
        in_specs=(
            P("depth", "tile", None),
            P("depth", "tile", None),
            P(),
            P("depth", "tile", None, None, None),
            P(None, "tile"),
            P(None, "tile"),
        ),
        out_specs=P(None, "depth", "tile", None, None, None),
        check_vma=False,
    )
```

time: 56.9 us -> 54.1 us (0.951)
  the two profiles are of different devices: /device:TPU:0 before, /device:TPU:96 now
where the time goes in v3:
time: 54.1 us; the launch traced here: 53.7 us
  Pallas kernels  30 us (55%)
  waiting for transfers between devices  12.3 us (23%)
  starting transfers between devices  8.16 us (15%)
  local copies, waits for them, and re-layouts  2.93 us (5%)
    pallas_call x11, Pallas kernels, call(): pl.pallas_call(kernel, grid=grid, in_specs=specs, out_specs=out_specs, ou...  28.2 us
    ppermute x4, waiting for transfers between devices, shards(): arrived = [lax.ppermute(left, 'depth', onward) for left in done]  9.75 us
    ppermute x4, starting transfers between devices, shards(): arrived = [lax.ppermute(left, 'depth', onward) for left in done]  4.12 us
    ppermute x4, starting transfers between devices, shards(): rims.append(lax.ppermute(firsts[-1], 'tile', back))  4.04 us
    unnamed x22, local copies, waits for them, and re-layouts  2.93 us
    ppermute x4, waiting for transfers between devices, shards(): rims.append(lax.ppermute(firsts[-1], 'tile', back))  2.53 us
    pallas_call x5, Pallas kernels, trans_rows(): pl.pallas_call(kernel, grid=(1,), scratch_shapes=scratch, out_shape=jax.S...  1.82 us
  transfers between devices with their start and end apart: 8, of which 7 were waited for; matrix products, arithmetic and copies ran while one was open for 0% of the time, Pallas kernels for 43%

profile of v3, /device:TPU:96, one launch (start us, length us, event | category | flops | bytes accessed | tf_op | source)
XLA Modules:
  0.0 53.7 jit_solution(10056288906949210393)
XLA Ops:
  0.0 0.0 copy-start
  0.0 1.2 %copy-done = f32[4,256,256]{2,1,0:T(8,128)S(1)} copy-done((f32[4,256,256]{2,1,0:T(8,128)S(1)}, f32[4,256,256]{2,1,0:T(8,128)}, u32[]{:S(2)}) %copy-start) | copy-done | bytes 1048600
  1.2 0.0 copy-start.2
  1.2 1.2 %copy-done.2 = f32[4,256,256]{2,1,0:T(8,128)S(1)} copy-done((f32[4,256,256]{2,1,0:T(8,128)S(1)}, f32[4,256,256]{2,1,0:T(8,128)}, u32[]{:S(2)}) %copy-start.2) | copy-done | bytes 1048600
  2.5 0.5 rim0.1.refs_5_
  3.0 2.5 %collective-permute-start = (f32[1,2,2,128,128]{4,3,2,1,0:T(8,128)S(1)}, f32[1,2,2,128,128]{4,3,2,1,0:T(8,128)}, u32[]{:S(2)}, u32[]{:S(2)}) collective-permute-start(f32[1,2,2,128,128]{4,3,2,1,0:T(8,128)S(1)} %rim0.1.refs_5_), channel_id=1, source_target_pairs={{0,7},{1,0},{2,1},{3,2},{4,3},{5,4},{6,5},{7,6},{8,15},{9,8},{10,9... | collective-permute-start | bytes 786440 | tf_op jit(solution)/shard_map/ppermute | solution.py:399
  5.4 0.2 rim1.1.refs_5_
  5.6 0.7 %collective-permute-start.1 = (f32[1,2,2,128,128]{4,3,2,1,0:T(8,128)S(1)}, f32[1,2,2,128,128]{4,3,2,1,0:T(8,128)}, u32[]{:S(2)}, u32[]{:S(2)}) collective-permute-start(f32[1,2,2,128,128]{4,3,2,1,0:T(8,128)S(1)} %rim1.1.refs_5_), channel_id=1, source_target_pairs={{0,7},{1,0},{2,1},{3,2},{4,3},{5,4},{6,5},{7,6},{8,15},{9,8},{10,9... | collective-permute-start | bytes 786440 | tf_op jit(solution)/shard_map/ppermute | solution.py:399
  6.3 0.2 rim2.1.refs_5_
  6.5 0.0 copy-start.8
  6.5 0.0 copy-start.9
  6.5 0.0 copy-start.1
  6.5 0.0 copy-start.3
  6.6 0.2 collective-permute-start.2
  6.8 0.2 rim3.1.refs_5_
  6.9 0.7 %collective-permute-start.3 = (f32[1,2,2,128,128]{4,3,2,1,0:T(8,128)S(1)}, f32[1,2,2,128,128]{4,3,2,1,0:T(8,128)S(1)}, u32[]{:S(2)}, u32[]{:S(2)}) collective-permute-start(f32[1,2,2,128,128]{4,3,2,1,0:T(8,128)S(1)} %rim3.1.refs_5_), channel_id=1, source_target_pairs={{0,7},{1,0},{2,1},{3,2},{4,3},{5,4},{6,5},{7,6},{8,15},{9,8},{10,9... | collective-permute-start | bytes 786440 | tf_op jit(solution)/shard_map/ppermute | solution.py:399
  7.6 0.0 copy-done.8
  7.6 0.1 copy.30.refs_0_
  7.7 0.0 copy-done.9
  7.7 0.1 copy.31.refs_1_
  7.8 0.0 copy-done.1
  7.8 0.3 copy-done.3
  8.1 0.0 copy-start.4
  8.1 0.0 copy-start.5
  8.1 0.0 copy-start.6
  8.1 0.8 %rest.1.refs_6_ = f32[4,2,2,128,128]{4,3,2,1,0:T(8,128)S(1)} custom-call(f32[4,256,256]{2,1,0:T(8,128)S(1)} %copy-done.1, f32[4,256,256]{2,1,0:T(8,128)S(1)} %copy-done.3), custom_call_target="tpu_custom_call" | custom-call | flops 5242880 | bytes 2097152 | tf_op jit(solution)/shard_map/rest/pallas_call | solution.py:102
  8.9 0.5 collective-permute-done.refs_7_
  9.3 0.0 copy-done.4
  9.3 0.0 copy-done.5
  9.3 0.0 copy-done.6
  9.3 2.2 %enter0.1 = (f32[4,2,128,128]{3,2,1,0:T(8,128)S(1)}, f32[2,2,384,128]{3,2,1,0:T(8,128)S(1)}) custom-call(s32[18,4]{1,0:T(8,128)S(1)} %copy.30.refs_0_, s32[18,4]{1,0:T(8,128)S(1)} %copy.31.refs_1_, f32[4,2,128,128]{3,2,1,0:T(8,128)S(1)} %bitcast.4, bf16[2,256,256]{2,1,0:T(8,128)(2,1)S(1)} %copy-done.5, bf16[2,256,256]{2,1,0:T(8,128)(2,1)S(1)} %copy-done.4, ...), custom_call_target="tpu_custom_call" | custom-call | flops 402653184 | bytes 786432 | tf_op jit(solution)/shard_map/enter0/pallas_call | solution.py:285
  11.5 0.6 %collective-permute-done.1.refs_7_ = f32[1,2,2,128,128]{4,3,2,1,0:T(8,128)} collective-permute-done((f32[1,2,2,128,128]{4,3,2,1,0:T(8,128)S(1)}, f32[1,2,2,128,128]{4,3,2,1,0:T(8,128)}, u32[]{:S(2)}, u32[]{:S(2)}) %collective-permute-start.1) | collective-permute-done | bytes 262176 | tf_op jit(solution)/shard_map/ppermute | solution.py:399
  12.1 2.1 %enter1.1 = (f32[4,2,128,128]{3,2,1,0:T(8,128)S(1)}, f32[2,2,384,128]{3,2,1,0:T(8,128)S(1)}) custom-call(s32[18,4]{1,0:T(8,128)S(1)} %copy.30.refs_0_, s32[18,4]{1,0:T(8,128)S(1)} %copy.31.refs_1_, f32[4,2,128,128]{3,2,1,0:T(8,128)S(1)} %get-tuple-element.15.refs_2_, bf16[2,256,256]{2,1,0:T(8,128)(2,1)S(1)} %copy-done.5, bf16[2,256,256]{2,1,0:T(8,128)(2,1)S(1)} %copy-done.4, ...), custom_call_target="tpu_custom_call" | custom-call | flops 402653184 | bytes 786432 | tf_op jit(solution)/shard_map/enter1/pallas_call | solution.py:285
  14.2 0.7 %collective-permute-done.2.refs_7_ = f32[1,2,2,128,128]{4,3,2,1,0:T(8,128)} collective-permute-done((f32[1,2,2,128,128]{4,3,2,1,0:T(8,128)S(1)}, f32[1,2,2,128,128]{4,3,2,1,0:T(8,128)}, u32[]{:S(2)}, u32[]{:S(2)}) %collective-permute-start.2) | collective-permute-done | bytes 262176 | tf_op jit(solution)/shard_map/ppermute | solution.py:399
  14.9 2.1 %enter2.1 = (f32[4,2,128,128]{3,2,1,0:T(8,128)S(1)}, f32[2,2,384,128]{3,2,1,0:T(8,128)S(1)}) custom-call(s32[18,4]{1,0:T(8,128)S(1)} %copy.30.refs_0_, s32[18,4]{1,0:T(8,128)S(1)} %copy.31.refs_1_, f32[4,2,128,128]{3,2,1,0:T(8,128)S(1)} %get-tuple-element.16.refs_2_, bf16[2,256,256]{2,1,0:T(8,128)(2,1)S(1)} %copy-done.5, bf16[2,256,256]{2,1,0:T(8,128)(2,1)S(1)} %copy-done.4, ...), custom_call_target="tpu_custom_call" | custom-call | flops 402653184 | bytes 786432 | tf_op jit(solution)/shard_map/enter2/pallas_call | solution.py:285
  17.0 0.7 %collective-permute-done.3.refs_7_ = f32[1,2,2,128,128]{4,3,2,1,0:T(8,128)S(1)} collective-permute-done((f32[1,2,2,128,128]{4,3,2,1,0:T(8,128)S(1)}, f32[1,2,2,128,128]{4,3,2,1,0:T(8,128)S(1)}, u32[]{:S(2)}, u32[]{:S(2)}) %collective-permute-start.3) | collective-permute-done | bytes 262176 | tf_op jit(solution)/shard_map/ppermute | solution.py:399
  17.8 1.8 %leave0.1 = (f32[2,2,128,128]{3,2,1,0:T(8,128)S(1)}, f32[2,2,384,128]{3,2,1,0:T(8,128)S(1)}) custom-call(s32[18,4]{1,0:T(8,128)S(1)} %copy.30.refs_0_, s32[18,4]{1,0:T(8,128)S(1)} %copy.31.refs_1_, f32[4,2,128,128]{3,2,1,0:T(8,128)S(1)} %get-tuple-element.17.refs_2_, bf16[2,256,256]{2,1,0:T(8,128)(2,1)S(1)} %copy-done.5, bf16[2,256,256]{2,1,0:T(8,128)(2,1)S(1)} %copy-done.4, ...), custom_call_target="tpu_custom_call" | custom-call | flops 201326592 | bytes 786432 | tf_op jit(solution)/shard_map/leave0/pallas_call | solution.py:285
  19.5 0.0 copy-start.7
  19.5 1.6 %collective-permute-start.6 = (f32[2,2,128,128]{3,2,1,0:T(8,128)S(1)}, f32[2,2,128,128]{3,2,1,0:T(8,128)S(1)}, u32[]{:S(2)}, u32[]{:S(2)}) collective-permute-start(f32[2,2,128,128]{3,2,1,0:T(8,128)S(1)} %get-tuple-element.22.refs_10_), channel_id=1, source_target_pairs={{0,8},{8,16},{16,24},{24,32},{32,40},{40,48},{48,56},{56,64},{64,7... | collective-permute-start | bytes 786440 | tf_op jit(solution)/shard_map/ppermute | solution.py:430
  21.1 1.7 %leave1.1.refs_9_.refs_11_ = f32[2,2,128,128]{3,2,1,0:T(8,128)S(1)} custom-call(s32[18,4]{1,0:T(8,128)S(1)} %copy.30.refs_0_, s32[18,4]{1,0:T(8,128)S(1)} %copy.31.refs_1_, f32[4,2,128,128]{3,2,1,0:T(8,128)S(1)} %get-tuple-element.17.refs_2_, bf16[2,256,256]{2,1,0:T(8,128)(2,1)S(1)} %copy-done.5, bf16[2,256,256]{2,1,0:T(8,128)(2,1)S(1)} %copy-done.4, ...), custom_call_target="tpu_custom_call" | custom-call | flops 201326592 | bytes 786432 | tf_op jit(solution)/shard_map/leave1/pallas_call | solution.py:285
  22.8 1.6 %collective-permute-start.4 = (f32[2,2,128,128]{3,2,1,0:T(8,128)S(1)}, f32[2,2,128,128]{3,2,1,0:T(8,128)S(1)}, u32[]{:S(2)}, u32[]{:S(2)}) collective-permute-start(f32[2,2,128,128]{3,2,1,0:T(8,128)S(1)} %leave1.1.refs_9_.refs_11_), channel_id=1, source_target_pairs={{0,8},{8,16},{16,24},{24,32},{32,40},{40,48},{48,56},{56,64},{64,7... | collective-permute-start | bytes 786440 | tf_op jit(solution)/shard_map/ppermute | solution.py:430
  24.4 0.0 copy-done.7
  24.4 1.0 %first1.1.refs_9_ = f32[4,2,128,128]{3,2,1,0:T(8,128)S(1)} custom-call(s32[18,4]{1,0:T(8,128)S(1)} %copy.30.refs_0_, s32[18,4]{1,0:T(8,128)S(1)} %copy.31.refs_1_, f32[2,128,128]{2,1,0:T(8,128)S(1)} %copy-done.7, bf16[2,256,256]{2,1,0:T(8,128)(2,1)S(1)} %copy-done.5, bf16[2,256,256]{2,1,0:T(8,128)(2,1)S(1)} %copy-done.4, ...), custom_call_target="tpu_custom_call" | custom-call | flops 1610612736 | bytes 3145728 | tf_op jit(solution)/shard_map/first1/pallas_call | solution.py:285
  25.4 5.6 %collective-permute-done.6.refs_2_ = f32[2,2,128,128]{3,2,1,0:T(8,128)S(1)} collective-permute-done((f32[2,2,128,128]{3,2,1,0:T(8,128)S(1)}, f32[2,2,128,128]{3,2,1,0:T(8,128)S(1)}, u32[]{:S(2)}, u32[]{:S(2)}) %collective-permute-start.6) | collective-permute-done | bytes 262176 | tf_op jit(solution)/shard_map/ppermute | solution.py:430
  30.9 3.9 %tick1_0.1.refs_12_ = f32[2,2,128,128]{3,2,1,0:T(8,128)S(1)} custom-call(s32[18,4]{1,0:T(8,128)S(1)} %copy.30.refs_0_, s32[18,4]{1,0:T(8,128)S(1)} %copy.31.refs_1_, f32[2,2,128,128]{3,2,1,0:T(8,128)S(1)} %collective-permute-done.6.refs_2_, bf16[2,256,256]{2,1,0:T(8,128)(2,1)S(1)} %copy-done.5, bf16[2,256,256]{2,1,0:T(8,128)(2,1)S(1)} %copy-done.4, ...), custom_call_target="tpu_custom_call" | custom-call | flops 805306368 | bytes 3145728 | tf_op jit(solution)/shard_map/tick1_0/pallas_call | solution.py:285
  34.8 0.1 collective-permute-start.7
  34.9 0.0 collective-permute-done.4.refs_2_
  34.9 3.9 %tick1_1.1.refs_9_.refs_13_ = f32[2,2,128,128]{3,2,1,0:T(8,128)S(1)} custom-call(s32[18,4]{1,0:T(8,128)S(1)} %copy.30.refs_0_, s32[18,4]{1,0:T(8,128)S(1)} %copy.31.refs_1_, f32[2,2,128,128]{3,2,1,0:T(8,128)S(1)} %collective-permute-done.4.refs_2_, bf16[2,256,256]{2,1,0:T(8,128)(2,1)S(1)} %copy-done.5, bf16[2,256,256]{2,1,0:T(8,128)(2,1)S(1)} %copy-done.4, ...), custom_call_target="tpu_custom_call" | custom-call | flops 805306368 | bytes 3145728 | tf_op jit(solution)/shard_map/tick1_1/pallas_call | solution.py:285
  38.8 0.9 %collective-permute-start.5 = (f32[2,2,128,128]{3,2,1,0:T(8,128)S(1)}, f32[2,2,128,128]{3,2,1,0:T(8,128)S(1)}, u32[]{:S(2)}, u32[]{:S(2)}) collective-permute-start(f32[2,2,128,128]{3,2,1,0:T(8,128)S(1)} %tick1_1.1.refs_9_.refs_13_), channel_id=1, source_target_pairs={{0,8},{8,16},{16,24},{24,32},{32,40},{40,48},{48,56},{56,64},{64,7... | collective-permute-start | bytes 786440 | tf_op jit(solution)/shard_map/ppermute | solution.py:430
  39.7 1.0 %first2.1.refs_9_ = f32[4,2,128,128]{3,2,1,0:T(8,128)S(1)} custom-call(s32[18,4]{1,0:T(8,128)S(1)} %copy.30.refs_0_, s32[18,4]{1,0:T(8,128)S(1)} %copy.31.refs_1_, f32[2,128,128]{2,1,0:T(8,128)S(1)} %copy-done.7, bf16[2,256,256]{2,1,0:T(8,128)(2,1)S(1)} %copy-done.5, bf16[2,256,256]{2,1,0:T(8,128)(2,1)S(1)} %copy-done.4, ...), custom_call_target="tpu_custom_call" | custom-call | flops 1610612736 | bytes 3145728 | tf_op jit(solution)/shard_map/first2/pallas_call | solution.py:285
  40.7 3.9 %collective-permute-done.7.refs_2_ = f32[2,2,128,128]{3,2,1,0:T(8,128)S(1)} collective-permute-done((f32[2,2,128,128]{3,2,1,0:T(8,128)S(1)}, f32[2,2,128,128]{3,2,1,0:T(8,128)S(1)}, u32[]{:S(2)}, u32[]{:S(2)}) %collective-permute-start.7) | collective-permute-done | bytes 262176 | tf_op jit(solution)/shard_map/ppermute | solution.py:430
  44.6 4.1 %tick2_0.1 = (f32[2,2,128,128]{3,2,1,0:T(8,128)S(1)}, f32[3,4,2,128,128]{4,3,2,1,0:T(8,128)}) custom-call(s32[18,4]{1,0:T(8,128)S(1)} %copy.30.refs_0_, s32[18,4]{1,0:T(8,128)S(1)} %copy.31.refs_1_, f32[2,2,128,128]{3,2,1,0:T(8,128)S(1)} %collective-permute-done.7.refs_2_, bf16[2,256,256]{2,1,0:T(8,128)(2,1)S(1)} %copy-done.5, ...), custom_call_target="tpu_custom_call" | custom-call | flops 805306368 | bytes 3145728 | tf_op jit(solution)/shard_map/tick2_0/pallas_call | solution.py:285
  48.7 0.3 collective-permute-done.5.refs_2_
  49.0 4.6 %tick2_1.1 = f32[3,4,2,128,128]{4,3,2,1,0:T(8,128)} custom-call(s32[18,4]{1,0:T(8,128)S(1)} %copy.30.refs_0_, s32[18,4]{1,0:T(8,128)S(1)} %copy.31.refs_1_, f32[2,2,128,128]{3,2,1,0:T(8,128)S(1)} %collective-permute-done.5.refs_2_, bf16[2,256,256]{2,1,0:T(8,128)(2,1)S(1)} %copy-done.5, ...), custom_call_target="tpu_custom_call", output_to_operand_aliasing={{}: (11, {})} | custom-call | flops 805306368 | bytes 3145728 | tf_op jit(solution)/shard_map/tick2_1/pallas_call | solution.py:285
Async XLA Ops:
  0.0 1.2 %copy-start = (f32[4,256,256]{2,1,0:T(8,128)S(1)}, f32[4,256,256]{2,1,0:T(8,128)}, u32[]{:S(2)}) copy-start(f32[4,256,256]{2,1,0:T(8,128)} %phase_ref.9) | copy-start | bytes 3145732
  1.2 1.2 %copy-start.2 = (f32[4,256,256]{2,1,0:T(8,128)S(1)}, f32[4,256,256]{2,1,0:T(8,128)}, u32[]{:S(2)}) copy-start(f32[4,256,256]{2,1,0:T(8,128)} %absorb_ref.9) | copy-start | bytes 3145732
  3.0 6.4 %collective-permute-start = (f32[1,2,2,128,128]{4,3,2,1,0:T(8,128)S(1)}, f32[1,2,2,128,128]{4,3,2,1,0:T(8,128)}, u32[]{:S(2)}, u32[]{:S(2)}) collective-permute-start(f32[1,2,2,128,128]{4,3,2,1,0:T(8,128)S(1)} %rim0.1.refs_5_), channel_id=1, source_target_pairs={{0,7},{1,0},{2,1},{3,2},{4,3},{5,4},{6,5},{7,6},{8,15},{9,8},{10,9... | collective-permute-start | bytes 786440 | tf_op jit(solution)/shard_map/ppermute | solution.py:399
  5.6 6.5 %collective-permute-start.1 = (f32[1,2,2,128,128]{4,3,2,1,0:T(8,128)S(1)}, f32[1,2,2,128,128]{4,3,2,1,0:T(8,128)}, u32[]{:S(2)}, u32[]{:S(2)}) collective-permute-start(f32[1,2,2,128,128]{4,3,2,1,0:T(8,128)S(1)} %rim1.1.refs_5_), channel_id=1, source_target_pairs={{0,7},{1,0},{2,1},{3,2},{4,3},{5,4},{6,5},{7,6},{8,15},{9,8},{10,9... | collective-permute-start | bytes 786440 | tf_op jit(solution)/shard_map/ppermute | solution.py:399
  6.5 1.1 %copy-start.8 = (s32[18,4]{0,1:T(4,128)S(1)}, s32[18,4]{0,1:T(4,128)}, u32[]{:S(2)}) copy-start(s32[18,4]{0,1:T(4,128)} %param.12) | copy-start | bytes 868
  6.5 1.2 %copy-start.9 = (s32[18,4]{0,1:T(4,128)S(1)}, s32[18,4]{0,1:T(4,128)}, u32[]{:S(2)}) copy-start(s32[18,4]{0,1:T(4,128)} %param.13) | copy-start | bytes 868
  6.5 1.3 %copy-start.1 = (f32[4,256,256]{2,1,0:T(8,128)S(1)}, f32[4,256,256]{2,1,0:T(8,128)}, u32[]{:S(2)}) copy-start(f32[4,256,256]{2,1,0:T(8,128)} %phase_ref.9) | copy-start | bytes 3145732
  6.5 1.5 %copy-start.3 = (f32[4,256,256]{2,1,0:T(8,128)S(1)}, f32[4,256,256]{2,1,0:T(8,128)}, u32[]{:S(2)}) copy-start(f32[4,256,256]{2,1,0:T(8,128)} %absorb_ref.9) | copy-start | bytes 3145732
  6.6 8.4 %collective-permute-start.2 = (f32[1,2,2,128,128]{4,3,2,1,0:T(8,128)S(1)}, f32[1,2,2,128,128]{4,3,2,1,0:T(8,128)}, u32[]{:S(2)}, u32[]{:S(2)}) collective-permute-start(f32[1,2,2,128,128]{4,3,2,1,0:T(8,128)S(1)} %rim2.1.refs_5_), channel_id=1, source_target_pairs={{0,7},{1,0},{2,1},{3,2},{4,3},{5,4},{6,5},{7,6},{8,15},{9,8},{10,9... | collective-permute-start | bytes 786440 | tf_op jit(solution)/shard_map/ppermute | solution.py:399
  6.9 10.8 %collective-permute-start.3 = (f32[1,2,2,128,128]{4,3,2,1,0:T(8,128)S(1)}, f32[1,2,2,128,128]{4,3,2,1,0:T(8,128)S(1)}, u32[]{:S(2)}, u32[]{:S(2)}) collective-permute-start(f32[1,2,2,128,128]{4,3,2,1,0:T(8,128)S(1)} %rim3.1.refs_5_), channel_id=1, source_target_pairs={{0,7},{1,0},{2,1},{3,2},{4,3},{5,4},{6,5},{7,6},{8,15},{9,8},{10,9... | collective-permute-start | bytes 786440 | tf_op jit(solution)/shard_map/ppermute | solution.py:399
  8.1 1.2 %copy-start.4 = (bf16[2,256,256]{2,1,0:T(8,128)(2,1)S(1)}, bf16[2,256,256]{2,1,0:T(8,128)(2,1)}, u32[]{:S(2)}) copy-start(bf16[2,256,256]{2,1,0:T(8,128)(2,1)} %constant.5.clone.refs_4_) | copy-start | bytes 786436
  8.1 1.2 %copy-start.5 = (bf16[2,256,256]{2,1,0:T(8,128)(2,1)S(1)}, bf16[2,256,256]{2,1,0:T(8,128)(2,1)}, u32[]{:S(2)}) copy-start(bf16[2,256,256]{2,1,0:T(8,128)(2,1)} %constant.4.clone.refs_3_) | copy-start | bytes 786436
  8.1 1.2 %copy-start.6 = (f32[1,4,2,128,128]{4,3,2,1,0:T(8,128)S(1)}, f32[1,4,2,128,128]{4,3,2,1,0:T(8,128)}, u32[]{:S(2)}) copy-start(f32[1,4,2,128,128]{4,3,2,1,0:T(8,128)} %param.11) | copy-start | bytes 1572868
  19.5 4.9 %copy-start.7 = (f32[2,128,128]{2,1,0:T(8,128)S(1)}, f32[2,128,128]{2,1,0:T(8,128)}, u32[]{:S(2)}) copy-start(f32[2,128,128]{2,1,0:T(8,128)} %refs_2_.3) | copy-start | bytes 393220
  19.5 11.4 %collective-permute-start.6 = (f32[2,2,128,128]{3,2,1,0:T(8,128)S(1)}, f32[2,2,128,128]{3,2,1,0:T(8,128)S(1)}, u32[]{:S(2)}, u32[]{:S(2)}) collective-permute-start(f32[2,2,128,128]{3,2,1,0:T(8,128)S(1)} %get-tuple-element.22.refs_10_), channel_id=1, source_target_pairs={{0,8},{8,16},{16,24},{24,32},{32,40},{40,48},{48,56},{56,64},{64,7... | collective-permute-start | bytes 786440 | tf_op jit(solution)/shard_map/ppermute | solution.py:430
  22.8 12.1 %collective-permute-start.4 = (f32[2,2,128,128]{3,2,1,0:T(8,128)S(1)}, f32[2,2,128,128]{3,2,1,0:T(8,128)S(1)}, u32[]{:S(2)}, u32[]{:S(2)}) collective-permute-start(f32[2,2,128,128]{3,2,1,0:T(8,128)S(1)} %leave1.1.refs_9_.refs_11_), channel_id=1, source_target_pairs={{0,8},{8,16},{16,24},{24,32},{32,40},{40,48},{48,56},{56,64},{64,7... | collective-permute-start | bytes 786440 | tf_op jit(solution)/shard_map/ppermute | solution.py:430
  34.8 9.8 %collective-permute-start.7 = (f32[2,2,128,128]{3,2,1,0:T(8,128)S(1)}, f32[2,2,128,128]{3,2,1,0:T(8,128)S(1)}, u32[]{:S(2)}, u32[]{:S(2)}) collective-permute-start(f32[2,2,128,128]{3,2,1,0:T(8,128)S(1)} %tick1_0.1.refs_12_), channel_id=1, source_target_pairs={{0,8},{8,16},{16,24},{24,32},{32,40},{40,48},{48,56},{56,64},{64,7... | collective-permute-start | bytes 786440 | tf_op jit(solution)/shard_map/ppermute | solution.py:430
  38.8 10.2 %collective-permute-start.5 = (f32[2,2,128,128]{3,2,1,0:T(8,128)S(1)}, f32[2,2,128,128]{3,2,1,0:T(8,128)S(1)}, u32[]{:S(2)}, u32[]{:S(2)}) collective-permute-start(f32[2,2,128,128]{3,2,1,0:T(8,128)S(1)} %tick1_1.1.refs_9_.refs_13_), channel_id=1, source_target_pairs={{0,8},{8,16},{16,24},{24,32},{32,40},{40,48},{48,56},{56,64},{64,7... | collective-permute-start | bytes 786440 | tf_op jit(solution)/shard_map/ppermute | solution.py:430

commit v4 on v3

--- a/solution.py
+++ b/solution.py
@@ -12,10 +12,10 @@
 
 TICKS = 3
 CHUNKS = 2
-RIM_CHUNKS = 4
 
 fresnel = 0.1
 VMEM_LIMIT = 24 * 1024 * 1024
+WIDE_LIMIT = 62 * 1024 * 1024
 
 SIN_TERMS = [(-1.0) ** j / math.factorial(2 * j + 1) for j in range(7)]
 COS_TERMS = [(-1.0) ** j / math.factorial(2 * j) for j in range(8)]
@@ -59,72 +59,94 @@
     return jnp.dot(a, b, preferred_element_type=jnp.float32)
 
 
-def trans_kernel(phase_ref, absorb_ref, out_ref):
+def trans_layer(phase_ref, absorb_ref, out_ref):
+    rows, columns = phase_ref.shape
     size = out_ref.shape[-1]
     step = 32
 
     def body(i, carry):
         at = pl.ds(pl.multiple_of(i * step, step), step)
-        for layer in range(phase_ref.shape[0]):
-            for half in range(2):
-                cols = slice(half * size, (half + 1) * size)
-                real, imag = transmission(phase_ref[layer, at, cols], absorb_ref[layer, at, cols])
-                out_ref[layer, 0, half, at, :] = real
-                out_ref[layer, 1, half, at, :] = imag
+        for half in range(columns // size):
+            cols = slice(half * size, (half + 1) * size)
+            real, imag = transmission(phase_ref[at, cols], absorb_ref[at, cols])
+            out_ref[0, half, at, :] = real
+            out_ref[1, half, at, :] = imag
         return carry
 
-    lax.fori_loop(0, phase_ref.shape[1] // step, body, 0)
-
-
-def first_trans_kernel(phase_ref, absorb_ref, out_ref, phase_buf, absorb_buf, sem):
+    lax.fori_loop(0, rows // step, body, 0)
+
+
+def edge_kernel(phase_ref, absorb_ref, *refs):
+    *out_refs, phase_buf, absorb_buf, sem = refs
+    count, rows = phase_buf.shape[:2]
     copies = []
-    for n, (ref, buf) in enumerate([(phase_ref, phase_buf), (absorb_ref, absorb_buf)]):
-        source = ref.at[pl.ds(0, buf.shape[0]), pl.ds(0, buf.shape[1])]
-        copies.append(pltpu.make_async_copy(source, buf, sem.at[n]))
-        copies[-1].start()
-    for copy in copies:
-        copy.wait()
-    trans_kernel(phase_buf, absorb_buf, out_ref)
-
-
-def trans_rows(phase_map, absorb, size, layers, block, name, direct=False):
-    count = len(layers)
-    columns = phase_map.shape[2]
-    at = layers[0] // count
-    spec = pl.BlockSpec((count, size, columns), lambda i: (at, block, 0))
+    for layer in range(count):
+        for n, (ref, buf) in enumerate([(phase_ref, phase_buf), (absorb_ref, absorb_buf)]):
+            source = ref.at[layer, pl.ds(0, rows)]
+            copies.append(pltpu.make_async_copy(source, buf.at[layer], sem.at[2 * layer + n]))
+            copies[-1].start()
+    for layer in range(count):
+        copies[2 * layer].wait()
+        copies[2 * layer + 1].wait()
+        trans_layer(phase_buf.at[layer], absorb_buf.at[layer], out_refs[layer].at[0])
+
+
+def rest_kernel(phase_ref, absorb_ref, out_ref):
+    for layer in range(phase_ref.shape[0]):
+        trans_layer(phase_ref.at[layer], absorb_ref.at[layer], out_ref.at[layer])
+
+
+def edge_rows(phase_map, absorb, size):
+    count, _, columns = phase_map.shape
+    shape = jax.ShapeDtypeStruct((1, 2, columns // size, size, size), jnp.float32)
     values = count * size * columns
-    kernel, scratch = trans_kernel, []
-    if direct:
-        kernel = first_trans_kernel
-        spec = pl.BlockSpec(memory_space=pltpu.HBM)
-        scratch = [pltpu.VMEM((count, size, columns), jnp.float32)] * 2
-        scratch.append(pltpu.SemaphoreType.DMA((2,)))
     return pl.pallas_call(
-        kernel,
+        edge_kernel,
+        out_shape=[shape] * count,
+        in_specs=[hbm()] * 2,
+        out_specs=[vmem()] * count,
+        scratch_shapes=[
+            pltpu.VMEM((count, size, columns), jnp.float32),
+            pltpu.VMEM((count, size, columns), jnp.float32),
+            pltpu.SemaphoreType.DMA((2 * count,)),
+        ],
+        compiler_params=pltpu.CompilerParams(vmem_limit_bytes=WIDE_LIMIT),
+        cost_estimate=pl.CostEstimate(
+            flops=values * 40, bytes_accessed=values * 16, transcendentals=values
+        ),
+        name="edge",
+    )(phase_map, absorb)
+
+
+def rest_rows(phase_map, absorb, size):
+    count, rows, columns = phase_map.shape
+    spec = pl.BlockSpec((count, rows - size, columns), lambda i: (0, 1, 0))
+    values = count * (rows - size) * columns
+    return pl.pallas_call(
+        rest_kernel,
         grid=(1,),
-        scratch_shapes=scratch,
-        out_shape=jax.ShapeDtypeStruct((count, 2, columns // size, size, size), jnp.float32),
+        out_shape=jax.ShapeDtypeStruct((count, 2, columns // size, rows - size, size), jnp.float32),
         in_specs=[spec] * 2,
         out_specs=vmem(),
         compiler_params=pltpu.CompilerParams(vmem_limit_bytes=VMEM_LIMIT),
         cost_estimate=pl.CostEstimate(
             flops=values * 40, bytes_accessed=values * 16, transcendentals=values
         ),
-        name=name,
+        name="rest",
     )(phase_map, absorb)
 
 
 def advance(
-    tick, layers, probes, starts, ends, piece_refs, ext_refs, scans, waves, put, tables, scratch
+    tick, layers, probes, starts, ends, piece_refs, ext_refs, anchors_ref, waves, put, tables, scratch
 ):
-    rows_ref, cols_ref, tile_rows = scans
     right_ref, left_ref = tables
     state, x_high, x_low, r_high, r_low = scratch
     size = state.shape[-1]
-    batch = tick - lax.axis_index("depth") + lax.axis_size("depth") - 1
-    offset = lax.axis_index("tile") * tile_rows
-    row_at = [rows_ref[batch, p] - offset for p in probes]
-    col_at = [cols_ref[batch, p] for p in probes]
+    each = anchors_ref.shape[0] // (2 * TICKS)
+    row_at, col_at = [
+        [anchors_ref[pl.ds((2 * tick + axis) * each + p, 1), :][0, 0] for p in probes]
+        for axis in range(2)
+    ]
     lane = lax.broadcasted_iota(jnp.int32, (size, size), 1)
     count = len(layers)
 
@@ -181,9 +203,9 @@
     return [refs.pop(0) for _ in range(count)]
 
 
-def entry_kernel(layers, probes, with_pieces, starts, ends, tile_rows, *refs):
+def entry_kernel(layers, probes, with_pieces, starts, ends, *refs):
     refs = list(refs)
-    rows_ref, cols_ref, wave_ref, right_ref, left_ref = take(refs, 5)
+    anchors_ref, wave_ref, right_ref, left_ref = take(refs, 4)
     if with_pieces:
         piece_refs = take(refs, 3)
         (out_ref,) = take(refs, 1)
@@ -197,14 +219,14 @@
         out_ref[n, part] = wave
 
     advance(
-        0, layers, probes, starts, ends, piece_refs, ext_refs, (rows_ref, cols_ref, tile_rows),
+        0, layers, probes, starts, ends, piece_refs, ext_refs, anchors_ref,
         lambda n, part: wave_ref[n, part], put, (right_ref, left_ref), refs,
     )
 
 
-def first_kernel(tick, layers, tile_rows, *refs):
+def first_kernel(tick, layers, *refs):
     refs = list(refs)
-    rows_ref, cols_ref, probe_ref, right_ref, left_ref = take(refs, 5)
+    anchors_ref, probe_ref, right_ref, left_ref = take(refs, 4)
     ext_refs = take(refs, len(layers))
     _, out_ref = take(refs, 2)
     count = out_ref.shape[0]
@@ -216,14 +238,14 @@
     @pl.when(lax.axis_index("depth") == 0)
     def _():
         advance(
-            tick, layers, probes, True, True, [], ext_refs, (rows_ref, cols_ref, tile_rows),
+            tick, layers, probes, True, True, [], ext_refs, anchors_ref,
             lambda n, part: probe_ref[part], put, (right_ref, left_ref), refs,
         )
 
 
-def tick_kernel(tick, layers, probes, stores, own_store, tile_rows, *refs):
+def tick_kernel(tick, layers, probes, stores, own_store, *refs):
     refs = list(refs)
-    rows_ref, cols_ref, wave_ref, right_ref, left_ref = take(refs, 5)
+    anchors_ref, wave_ref, right_ref, left_ref = take(refs, 4)
     ext_refs = take(refs, len(layers))
     (first_ref,) = take(refs, 1)
     stored_refs = take(refs, len(stores))
@@ -255,7 +277,7 @@
     @pl.when(depth != 0)
     def _():
         advance(
-            tick, layers, probes, True, True, [], ext_refs, (rows_ref, cols_ref, tile_rows),
+            tick, layers, probes, True, True, [], ext_refs, anchors_ref,
             lambda n, part: wave_ref[n, part], put, (right_ref, left_ref), refs,
         )
 
@@ -269,10 +291,6 @@
 
 def vmem():
     return pl.BlockSpec(memory_space=pltpu.VMEM)
-
-
-def smem():
-    return pl.BlockSpec(memory_space=pltpu.SMEM)
 
 
 def hbm():
@@ -305,13 +323,13 @@
     )(*operands)
 
 
-def entry(layers, probes, scans, tables, wave, pieces, exts, starts, ends, tile_rows, name):
+def entry(layers, probes, anchors, tables, wave, pieces, exts, starts, ends, tile_rows, name):
     size = wave.shape[-1]
     count, n = len(layers), len(probes)
     first = probes[0] // n if wave.shape[0] != n else 0
-    operands = [*scans, wave, *tables]
+    operands = [anchors, wave, *tables]
     specs = [
-        smem(), smem(), pl.BlockSpec((n, 2, size, size), lambda i: (first, 0, 0, 0)),
+        vmem(), pl.BlockSpec((n, 2, size, size), lambda i: (first, 0, 0, 0)),
         vmem(), vmem(),
     ]
     out_shape = [jax.ShapeDtypeStruct((n, 2, size, size), jnp.float32)]
@@ -328,20 +346,20 @@
         operands += exts
         specs += [vmem()] * count
     kernel = functools.partial(
-        entry_kernel, layers, probes, pieces is not None, starts, ends, tile_rows
+        entry_kernel, layers, probes, pieces is not None, starts, ends
     )
     return call(
         kernel, operands, specs, out_shape, [vmem()] * len(out_shape), n, size, count, name
     )
 
 
-def first_section(tick, n, scans, tables, probe_wave, exts, after, tile_rows, chunks):
+def first_section(tick, n, anchors, tables, probe_wave, exts, after, chunks):
     size = probe_wave.shape[-1]
     layers = list(range(len(exts)))
     return call(
-        functools.partial(first_kernel, tick, layers, tile_rows),
-        [*scans, probe_wave, *tables, *exts, after],
-        [smem()] * 2 + [vmem()] * (3 + len(exts)) + [pl.BlockSpec(memory_space=pl.ANY)],
+        functools.partial(first_kernel, tick, layers),
+        [anchors, probe_wave, *tables, *exts, after],
+        [vmem()] * (4 + len(exts)) + [pl.BlockSpec(memory_space=pl.ANY)],
         jax.ShapeDtypeStruct((chunks * n, 2, size, size), jnp.float32),
         pl.BlockSpec((n, 2, size, size), lambda i: (i, 0, 0, 0)),
         n, size, len(exts), f"first{tick}", grid=(chunks,),
@@ -349,13 +367,13 @@
 
 
 def tick_section(
-    tick, c, n, scans, tables, wave, exts, first, tile_rows, stored=(), out_shape=None, out=None
+    tick, c, n, anchors, tables, wave, exts, first, stored=(), out_shape=None, out=None
 ):
     size = wave.shape[-1]
     count = len(exts)
     probes = list(range(c * n, (c + 1) * n))
-    operands = [*scans, wave, *tables, *exts, first, *(part for _, part in stored)]
-    specs = [smem()] * 2 + [vmem()] * (3 + count)
+    operands = [anchors, wave, *tables, *exts, first, *(part for _, part in stored)]
+    specs = [vmem()] * (4 + count)
     specs.append(pl.BlockSpec((n, 2, size, size), lambda i: (c, 0, 0, 0)))
     specs += [vmem()] * len(stored)
     shape = [jax.ShapeDtypeStruct((n, 2, size, size), jnp.float32)]
@@ -376,7 +394,7 @@
         rest["scratch"] = [pltpu.SemaphoreType.DMA((len(stored),))]
     kernel = functools.partial(
         tick_kernel, tick, list(range(count)), probes, [to for to, _ in stored],
-        out is not None, tile_rows,
+        out is not None,
     )
     return call(
         kernel, operands, specs, shape, out_specs, n, size, count, f"tick{tick}_{c}", **rest
@@ -391,35 +409,35 @@
     back = [(i, (i - 1) % tiles) for i in range(tiles)]
     onward = [(i, (i + 1) % depth_count) for i in range(depth_count)]
 
-    per_rim = slices // RIM_CHUNKS
-    spans = [list(range(r * per_rim, (r + 1) * per_rim)) for r in range(RIM_CHUNKS)]
-    firsts, rims = [], []
-    for r, layers in enumerate(spans):
-        firsts.append(trans_rows(phase_map, absorb, size, layers, 0, f"rim{r}", r == 0))
-        rims.append(lax.ppermute(firsts[-1], "tile", back))
-    rest = trans_rows(phase_map, absorb, size, list(range(slices)), 1, "rest")
+    firsts = edge_rows(phase_map, absorb, size)
+    rims = [lax.ppermute(first, "tile", back) for first in firsts]
+    rest = rest_rows(phase_map, absorb, size)
 
     tables = [jnp.asarray(table) for table in hop_tables(size)]
-    scans = (scan_rows, scan_cols)
+    depth, tile = lax.axis_index("depth"), lax.axis_index("tile")
+    anchors = jnp.stack([scan_rows - tile * tile_rows, scan_cols], 1)
+    anchors = lax.dynamic_slice_in_dim(anchors, depth_count - 1 - depth, TICKS, 0)
+    anchors = jnp.broadcast_to(anchors.reshape(-1, 1), (anchors.size, size))
     held = waves_in[0]
     count = held.shape[0]
     per_chunk = count // CHUNKS
     groups = [list(range(c * per_chunk, (c + 1) * per_chunk)) for c in range(CHUNKS)]
     exts = []
     done = []
-    for r, layers in enumerate(spans):
+    for r in range(slices):
+        layers = [r]
         pieces = [(firsts[r], 0), (rest, r), (rims[r], 0)]
-        edges = (r == 0, r == RIM_CHUNKS - 1, tile_rows)
-        if r < RIM_CHUNKS - 1:
+        edges = (r == 0, r == slices - 1, tile_rows)
+        if r < slices - 1:
             held, *made = entry(
-                layers, list(range(count)), scans, tables, held, pieces, None, *edges, f"enter{r}"
+                layers, list(range(count)), anchors, tables, held, pieces, None, *edges, f"enter{r}"
             )
             exts += made
             continue
         for c, group in enumerate(groups):
-            sources = (pieces, None) if c == 0 else (None, exts[-per_rim:])
+            sources = (pieces, None) if c == 0 else (None, exts[-1:])
             left, *made = entry(
-                layers, group, scans, tables, held, *sources, *edges, f"leave{c}"
+                layers, group, anchors, tables, held, *sources, *edges, f"leave{c}"
             )
             exts += made
             done.append(left)
@@ -429,7 +447,7 @@
         stored += [((tick - 1, c * per_chunk), part) for c, part in enumerate(done)]
         arrived = [lax.ppermute(left, "depth", onward) for left in done]
         first = first_section(
-            tick, per_chunk, scans, tables, probe_wave, exts, done[-1], tile_rows, CHUNKS
+            tick, per_chunk, anchors, tables, probe_wave, exts, done[-1], CHUNKS
         )
         done = []
         out = None
@@ -441,7 +459,7 @@
                 if c == CHUNKS - 1:
                     last = dict(stored=stored, out=out)
             left, *made = tick_section(
-                tick, c, per_chunk, scans, tables, arrived[c], exts, first, tile_rows, **last
+                tick, c, per_chunk, anchors, tables, arrived[c], exts, first, **last
             )
             if made:
                 out = made[0]

time: 54.1 us -> 51.3 us (0.948)
  Pallas kernels: 30 us -> 21.4 us
  waiting for transfers between devices: 12.3 us -> 20.5 us
  local copies, waits for them, and re-layouts: 2.93 us -> 1.55 us
  starting transfers between devices: 8.16 us -> 7.31 us
    pallas_call x11, Pallas kernels: 28.2 us -> 17.8 us  [call(): pl.pallas_call(kernel, grid=grid, in_specs=specs, out_specs=out_specs, ou...]
    ppermute x4, waiting for transfers between devices: 9.75 us -> 15.4 us  [shards(): arrived = [lax.ppermute(left, 'depth', onward) for left in done]]
    ppermute x4, waiting for transfers between devices: 2.53 us -> 5.13 us  [shards(): rims = [lax.ppermute(first, 'tile', back) for first in firsts]]
    pallas_call x5 -> x2, Pallas kernels: 1.82 us -> 3.62 us  [the longest x1 2.79 us: edge_rows(): pl.pallas_call(edge_kernel, out_shape=[shape] * count, in_specs=[hbm()] *...]
    unnamed x22 -> x24, local copies, waits for them, and re-layouts: 2.93 us -> 1.29 us
    ppermute x4, starting transfers between devices: 4.12 us -> 3.31 us  [shards(): arrived = [lax.ppermute(left, 'depth', onward) for left in done]]
  transfers between devices with their start and end apart: 8 -> 8, of which waited for: 7 -> 8; matrix products, arithmetic and copies ran while one was open for 0% -> 1% of each run, Pallas kernels for 43% -> 28%
where the time goes in v4:
time: 51.3 us; the launch traced here: 51.2 us
  Pallas kernels  21.4 us (42%)
  waiting for transfers between devices  20.5 us (40%)
  starting transfers between devices  7.31 us (14%)
  local copies, waits for them, and re-layouts  1.55 us (3%)
    pallas_call x11, Pallas kernels, call(): pl.pallas_call(kernel, grid=grid, in_specs=specs, out_specs=out_specs, ou...  17.8 us
    ppermute x4, waiting for transfers between devices, shards(): arrived = [lax.ppermute(left, 'depth', onward) for left in done]  15.4 us
    ppermute x4, waiting for transfers between devices, shards(): rims = [lax.ppermute(first, 'tile', back) for first in firsts]  5.13 us
    ppermute x4, starting transfers between devices, shards(): rims = [lax.ppermute(first, 'tile', back) for first in firsts]  4 us
    ppermute x4, starting transfers between devices, shards(): arrived = [lax.ppermute(left, 'depth', onward) for left in done]  3.31 us
    pallas_call x1, Pallas kernels, edge_rows(): pl.pallas_call(edge_kernel, out_shape=[shape] * count, in_specs=[hbm()] *...  2.79 us
    unnamed x24, local copies, waits for them, and re-layouts  1.29 us
  transfers between devices with their start and end apart: 8, of which 8 were waited for; matrix products, arithmetic and copies ran while one was open for 1% of the time, Pallas kernels for 28%

profile of v4, /device:TPU:96, one launch (start us, length us, event | category | flops | bytes accessed | tf_op | source)
XLA Modules:
  0.0 51.2 jit_solution(858592528782375591)
XLA Ops:
  0.0 0.0 copy-start.2
  0.0 0.0 copy-start.11
  0.0 0.0 copy-start.10
  0.0 2.8 %edge.1 = (f32[1,2,2,128,128]{4,3,2,1,0:T(8,128)}, f32[1,2,2,128,128]{4,3,2,1,0:T(8,128)}, f32[1,2,2,128,128]{4,3,2,1,0:T(8,128)}, f32[1,2,2,128,128]{4,3,2,1,0:T(8,128)}) custom-call(f32[4,256,256]{2,1,0:T(8,128)} %phase_ref.3, f32[4,256,256]{2,1,0:T(8,128)} %absorb_ref.3), custom_call_target="tpu_custom_call" | custom-call | flops 5242880 | bytes 2097152 | tf_op jit(solution)/shard_map/edge/pallas_call | solution.py:103
  2.8 2.5 %collective-permute-start = (f32[1,2,2,128,128]{4,3,2,1,0:T(8,128)}, f32[1,2,2,128,128]{4,3,2,1,0:T(8,128)S(1)}, u32[]{:S(2)}, u32[]{:S(2)}) collective-permute-start(f32[1,2,2,128,128]{4,3,2,1,0:T(8,128)} %get-tuple-element.19.refs_4_), channel_id=1, source_target_pairs={{0,7},{1,0},{2,1},{3,2},{4,3},{5,4},{6,5},{7,6},{8,15},{9,8},{10,9... | collective-permute-start | bytes 786440 | tf_op jit(solution)/shard_map/ppermute | solution.py:413
  5.3 0.7 %collective-permute-start.1 = (f32[1,2,2,128,128]{4,3,2,1,0:T(8,128)}, f32[1,2,2,128,128]{4,3,2,1,0:T(8,128)S(1)}, u32[]{:S(2)}, u32[]{:S(2)}) collective-permute-start(f32[1,2,2,128,128]{4,3,2,1,0:T(8,128)} %get-tuple-element.21.refs_4_), channel_id=1, source_target_pairs={{0,7},{1,0},{2,1},{3,2},{4,3},{5,4},{6,5},{7,6},{8,15},{9,8},{10,9... | collective-permute-start | bytes 786440 | tf_op jit(solution)/shard_map/ppermute | solution.py:413
  6.0 0.2 collective-permute-start.2
  6.1 0.7 %collective-permute-start.3 = (f32[1,2,2,128,128]{4,3,2,1,0:T(8,128)}, f32[1,2,2,128,128]{4,3,2,1,0:T(8,128)S(1)}, u32[]{:S(2)}, u32[]{:S(2)}) collective-permute-start(f32[1,2,2,128,128]{4,3,2,1,0:T(8,128)} %get-tuple-element.25.refs_4_), channel_id=1, source_target_pairs={{0,7},{1,0},{2,1},{3,2},{4,3},{5,4},{6,5},{7,6},{8,15},{9,8},{10,9... | collective-permute-start | bytes 786440 | tf_op jit(solution)/shard_map/ppermute | solution.py:413
  6.8 0.0 copy-done.11
  6.8 0.0 copy-done.10
  6.8 0.1 dynamic-slice_add_fusion
  6.9 0.1 copy.10
  7.0 0.1 broadcast_in_dim.10
  7.1 0.0 copy-done.2
  7.1 0.0 copy-start.3
  7.1 1.2 %copy-done.3 = f32[4,256,256]{2,1,0:T(8,128)S(1)} copy-done((f32[4,256,256]{2,1,0:T(8,128)S(1)}, f32[4,256,256]{2,1,0:T(8,128)}, u32[]{:S(2)}) %copy-start.3) | copy-done | bytes 1048600
  8.3 0.0 copy-start
  8.3 0.0 copy-start.1
  8.3 0.0 copy-start.4
  8.3 0.0 copy-start.8
  8.3 0.8 %rest.1.refs_5_ = f32[4,2,2,128,128]{4,3,2,1,0:T(8,128)S(1)} custom-call(f32[4,256,256]{2,1,0:T(8,128)S(1)} %copy-done.2, f32[4,256,256]{2,1,0:T(8,128)S(1)} %copy-done.3), custom_call_target="tpu_custom_call" | custom-call | flops 5242880 | bytes 2097152 | tf_op jit(solution)/shard_map/rest/pallas_call | solution.py:125
  9.2 0.0 copy-start.7
  9.2 0.3 collective-permute-done.refs_6_
  9.5 0.1 broadcast_in_dim.11.refs_0_
  9.6 0.0 copy-done
  9.6 0.0 copy-done.1
  9.6 0.0 copy-done.4
  9.6 0.0 copy-done.8
  9.6 1.2 %enter0.1 = (f32[4,2,128,128]{3,2,1,0:T(8,128)S(1)}, f32[2,2,384,128]{3,2,1,0:T(8,128)S(1)}) custom-call(s32[24,128]{1,0:T(8,128)S(1)} %broadcast_in_dim.11.refs_0_, f32[4,2,128,128]{3,2,1,0:T(8,128)S(1)} %bitcast.7, bf16[2,256,256]{2,1,0:T(8,128)(2,1)S(1)} %copy-done.1, bf16[2,256,256]{2,1,0:T(8,128)(2,1)S(1)} %copy-done, ...), custom_call_target="tpu_custom_call" | custom-call | flops 402653184 | bytes 786432 | tf_op jit(solution)/shard_map/enter0/pallas_call | solution.py:303
  10.8 0.0 copy-start.6
  10.8 1.5 %collective-permute-done.1.refs_6_ = f32[1,2,2,128,128]{4,3,2,1,0:T(8,128)S(1)} collective-permute-done((f32[1,2,2,128,128]{4,3,2,1,0:T(8,128)}, f32[1,2,2,128,128]{4,3,2,1,0:T(8,128)S(1)}, u32[]{:S(2)}, u32[]{:S(2)}) %collective-permute-start.1) | collective-permute-done | bytes 262176 | tf_op jit(solution)/shard_map/ppermute | solution.py:413
  12.3 0.0 copy-done.7
  12.3 1.1 %enter1.1 = (f32[4,2,128,128]{3,2,1,0:T(8,128)S(1)}, f32[2,2,384,128]{3,2,1,0:T(8,128)S(1)}) custom-call(s32[24,128]{1,0:T(8,128)S(1)} %broadcast_in_dim.11.refs_0_, f32[4,2,128,128]{3,2,1,0:T(8,128)S(1)} %get-tuple-element.20.refs_1_, bf16[2,256,256]{2,1,0:T(8,128)(2,1)S(1)} %copy-done.1, bf16[2,256,256]{2,1,0:T(8,128)(2,1)S(1)} %copy-done, ...), custom_call_target="tpu_custom_call" | custom-call | flops 402653184 | bytes 786432 | tf_op jit(solution)/shard_map/enter1/pallas_call | solution.py:303
  13.4 0.0 copy-start.5
  13.4 1.7 %collective-permute-done.2.refs_6_ = f32[1,2,2,128,128]{4,3,2,1,0:T(8,128)S(1)} collective-permute-done((f32[1,2,2,128,128]{4,3,2,1,0:T(8,128)}, f32[1,2,2,128,128]{4,3,2,1,0:T(8,128)S(1)}, u32[]{:S(2)}, u32[]{:S(2)}) %collective-permute-start.2) | collective-permute-done | bytes 262176 | tf_op jit(solution)/shard_map/ppermute | solution.py:413
  15.1 0.0 copy-done.6
  15.1 1.1 %enter2.1 = (f32[4,2,128,128]{3,2,1,0:T(8,128)S(1)}, f32[2,2,384,128]{3,2,1,0:T(8,128)S(1)}) custom-call(s32[24,128]{1,0:T(8,128)S(1)} %broadcast_in_dim.11.refs_0_, f32[4,2,128,128]{3,2,1,0:T(8,128)S(1)} %get-tuple-element.22.refs_1_, bf16[2,256,256]{2,1,0:T(8,128)(2,1)S(1)} %copy-done.1, bf16[2,256,256]{2,1,0:T(8,128)(2,1)S(1)} %copy-done, ...), custom_call_target="tpu_custom_call" | custom-call | flops 402653184 | bytes 786432 | tf_op jit(solution)/shard_map/enter2/pallas_call | solution.py:303
  16.2 1.7 %collective-permute-done.3.refs_6_ = f32[1,2,2,128,128]{4,3,2,1,0:T(8,128)S(1)} collective-permute-done((f32[1,2,2,128,128]{4,3,2,1,0:T(8,128)}, f32[1,2,2,128,128]{4,3,2,1,0:T(8,128)S(1)}, u32[]{:S(2)}, u32[]{:S(2)}) %collective-permute-start.3) | collective-permute-done | bytes 262176 | tf_op jit(solution)/shard_map/ppermute | solution.py:413
  17.9 0.0 copy-done.5
  17.9 0.8 %leave0.1 = (f32[2,2,128,128]{3,2,1,0:T(8,128)S(1)}, f32[2,2,384,128]{3,2,1,0:T(8,128)S(1)}) custom-call(s32[24,128]{1,0:T(8,128)S(1)} %broadcast_in_dim.11.refs_0_, f32[4,2,128,128]{3,2,1,0:T(8,128)S(1)} %get-tuple-element.24.refs_1_, bf16[2,256,256]{2,1,0:T(8,128)(2,1)S(1)} %copy-done.1, bf16[2,256,256]{2,1,0:T(8,128)(2,1)S(1)} %copy-done, ...), custom_call_target="tpu_custom_call" | custom-call | flops 201326592 | bytes 786432 | tf_op jit(solution)/shard_map/leave0/pallas_call | solution.py:303
  18.7 0.0 copy-start.9
  18.8 1.6 %collective-permute-start.6 = (f32[2,2,128,128]{3,2,1,0:T(8,128)S(1)}, f32[2,2,128,128]{3,2,1,0:T(8,128)S(1)}, u32[]{:S(2)}, u32[]{:S(2)}) collective-permute-start(f32[2,2,128,128]{3,2,1,0:T(8,128)S(1)} %get-tuple-element.30.refs_9_), channel_id=1, source_target_pairs={{0,8},{8,16},{16,24},{24,32},{32,40},{40,48},{48,56},{56,64},{64,7... | collective-permute-start | bytes 786440 | tf_op jit(solution)/shard_map/ppermute | solution.py:448
  20.3 0.8 %leave1.1.refs_8_.refs_10_ = f32[2,2,128,128]{3,2,1,0:T(8,128)S(1)} custom-call(s32[24,128]{1,0:T(8,128)S(1)} %broadcast_in_dim.11.refs_0_, f32[4,2,128,128]{3,2,1,0:T(8,128)S(1)} %get-tuple-element.24.refs_1_, bf16[2,256,256]{2,1,0:T(8,128)(2,1)S(1)} %copy-done.1, bf16[2,256,256]{2,1,0:T(8,128)(2,1)S(1)} %copy-done, ...), custom_call_target="tpu_custom_call" | custom-call | flops 201326592 | bytes 786432 | tf_op jit(solution)/shard_map/leave1/pallas_call | solution.py:303
  21.1 1.6 %collective-permute-start.4 = (f32[2,2,128,128]{3,2,1,0:T(8,128)S(1)}, f32[2,2,128,128]{3,2,1,0:T(8,128)S(1)}, u32[]{:S(2)}, u32[]{:S(2)}) collective-permute-start(f32[2,2,128,128]{3,2,1,0:T(8,128)S(1)} %leave1.1.refs_8_.refs_10_), channel_id=1, source_target_pairs={{0,8},{8,16},{16,24},{24,32},{32,40},{40,48},{48,56},{56,64},{64,7... | collective-permute-start | bytes 786440 | tf_op jit(solution)/shard_map/ppermute | solution.py:448
  22.7 0.0 copy-done.9
  22.7 7.5 %collective-permute-done.6.refs_1_ = f32[2,2,128,128]{3,2,1,0:T(8,128)S(1)} collective-permute-done((f32[2,2,128,128]{3,2,1,0:T(8,128)S(1)}, f32[2,2,128,128]{3,2,1,0:T(8,128)S(1)}, u32[]{:S(2)}, u32[]{:S(2)}) %collective-permute-start.6) | collective-permute-done | bytes 262176 | tf_op jit(solution)/shard_map/ppermute | solution.py:448
  30.2 3.0 %tick1_0.1.refs_11_ = f32[2,2,128,128]{3,2,1,0:T(8,128)S(1)} custom-call(s32[24,128]{1,0:T(8,128)S(1)} %broadcast_in_dim.11.refs_0_, f32[2,2,128,128]{3,2,1,0:T(8,128)S(1)} %collective-permute-done.6.refs_1_, bf16[2,256,256]{2,1,0:T(8,128)(2,1)S(1)} %copy-done.1, bf16[2,256,256]{2,1,0:T(8,128)(2,1)S(1)} %copy-done, ...), custom_call_target="tpu_custom_call" | custom-call | flops 805306368 | bytes 3145728 | tf_op jit(solution)/shard_map/tick1_0/pallas_call | solution.py:303
  33.2 0.1 collective-permute-start.7
  33.2 0.8 %collective-permute-done.4.refs_1_ = f32[2,2,128,128]{3,2,1,0:T(8,128)S(1)} collective-permute-done((f32[2,2,128,128]{3,2,1,0:T(8,128)S(1)}, f32[2,2,128,128]{3,2,1,0:T(8,128)S(1)}, u32[]{:S(2)}, u32[]{:S(2)}) %collective-permute-start.4) | collective-permute-done | bytes 262176 | tf_op jit(solution)/shard_map/ppermute | solution.py:448
  34.1 3.0 %tick1_1.1.refs_8_.refs_12_ = f32[2,2,128,128]{3,2,1,0:T(8,128)S(1)} custom-call(s32[24,128]{1,0:T(8,128)S(1)} %broadcast_in_dim.11.refs_0_, f32[2,2,128,128]{3,2,1,0:T(8,128)S(1)} %collective-permute-done.4.refs_1_, bf16[2,256,256]{2,1,0:T(8,128)(2,1)S(1)} %copy-done.1, bf16[2,256,256]{2,1,0:T(8,128)(2,1)S(1)} %copy-done, ...), custom_call_target="tpu_custom_call" | custom-call | flops 805306368 | bytes 3145728 | tf_op jit(solution)/shard_map/tick1_1/pallas_call | solution.py:303
  37.0 0.1 collective-permute-start.5
  37.2 6.0 %collective-permute-done.7.refs_1_ = f32[2,2,128,128]{3,2,1,0:T(8,128)S(1)} collective-permute-done((f32[2,2,128,128]{3,2,1,0:T(8,128)S(1)}, f32[2,2,128,128]{3,2,1,0:T(8,128)S(1)}, u32[]{:S(2)}, u32[]{:S(2)}) %collective-permute-start.7) | collective-permute-done | bytes 262176 | tf_op jit(solution)/shard_map/ppermute | solution.py:448
  43.2 3.0 %tick2_0.1 = (f32[2,2,128,128]{3,2,1,0:T(8,128)S(1)}, f32[3,4,2,128,128]{4,3,2,1,0:T(8,128)}) custom-call(s32[24,128]{1,0:T(8,128)S(1)} %broadcast_in_dim.11.refs_0_, f32[2,2,128,128]{3,2,1,0:T(8,128)S(1)} %collective-permute-done.7.refs_1_, bf16[2,256,256]{2,1,0:T(8,128)(2,1)S(1)} %copy-done.1, bf16[2,256,256]{2,1,0:T(8,128)(2,1)S(1)} %copy-done, ...), custom_call_target="tpu_custom_call" | custom-call | flops 805306368 | bytes 3145728 | tf_op jit(solution)/shard_map/tick2_0/pallas_call | solution.py:303
  46.2 1.1 %collective-permute-done.5.refs_1_ = f32[2,2,128,128]{3,2,1,0:T(8,128)S(1)} collective-permute-done((f32[2,2,128,128]{3,2,1,0:T(8,128)S(1)}, f32[2,2,128,128]{3,2,1,0:T(8,128)S(1)}, u32[]{:S(2)}, u32[]{:S(2)}) %collective-permute-start.5) | collective-permute-done | bytes 262176 | tf_op jit(solution)/shard_map/ppermute | solution.py:448
  47.3 3.7 %tick2_1.1 = f32[3,4,2,128,128]{4,3,2,1,0:T(8,128)} custom-call(s32[24,128]{1,0:T(8,128)S(1)} %broadcast_in_dim.11.refs_0_, f32[2,2,128,128]{3,2,1,0:T(8,128)S(1)} %collective-permute-done.5.refs_1_, bf16[2,256,256]{2,1,0:T(8,128)(2,1)S(1)} %copy-done.1, bf16[2,256,256]{2,1,0:T(8,128)(2,1)S(1)} %copy-done, ...), custom_call_target="tpu_custom_call", output_to_operand_aliasing={{}: (10, {})} | custom-call | flops 805306368 | bytes 3145728 | tf_op jit(solution)/shard_map/tick2_1/pallas_call | solution.py:303
  (3 shorter events, 0.0 us)
Async XLA Ops:
  0.0 7.1 %copy-start.2 = (f32[4,256,256]{2,1,0:T(8,128)S(1)}, f32[4,256,256]{2,1,0:T(8,128)}, u32[]{:S(2)}) copy-start(f32[4,256,256]{2,1,0:T(8,128)} %phase_ref.3) | copy-start | bytes 3145732
  0.0 6.8 %copy-start.11 = (s32[18,4]{0,1:T(4,128)S(1)}, s32[18,4]{0,1:T(4,128)}, u32[]{:S(2)}) copy-start(s32[18,4]{0,1:T(4,128)} %param.12) | copy-start | bytes 868
  0.0 6.8 %copy-start.10 = (s32[18,4]{0,1:T(4,128)S(1)}, s32[18,4]{0,1:T(4,128)}, u32[]{:S(2)}) copy-start(s32[18,4]{0,1:T(4,128)} %param.13) | copy-start | bytes 868
  2.8 6.7 %collective-permute-start = (f32[1,2,2,128,128]{4,3,2,1,0:T(8,128)}, f32[1,2,2,128,128]{4,3,2,1,0:T(8,128)S(1)}, u32[]{:S(2)}, u32[]{:S(2)}) collective-permute-start(f32[1,2,2,128,128]{4,3,2,1,0:T(8,128)} %get-tuple-element.19.refs_4_), channel_id=1, source_target_pairs={{0,7},{1,0},{2,1},{3,2},{4,3},{5,4},{6,5},{7,6},{8,15},{9,8},{10,9... | collective-permute-start | bytes 786440 | tf_op jit(solution)/shard_map/ppermute | solution.py:413
  5.3 7.0 %collective-permute-start.1 = (f32[1,2,2,128,128]{4,3,2,1,0:T(8,128)}, f32[1,2,2,128,128]{4,3,2,1,0:T(8,128)S(1)}, u32[]{:S(2)}, u32[]{:S(2)}) collective-permute-start(f32[1,2,2,128,128]{4,3,2,1,0:T(8,128)} %get-tuple-element.21.refs_4_), channel_id=1, source_target_pairs={{0,7},{1,0},{2,1},{3,2},{4,3},{5,4},{6,5},{7,6},{8,15},{9,8},{10,9... | collective-permute-start | bytes 786440 | tf_op jit(solution)/shard_map/ppermute | solution.py:413
  6.0 9.1 %collective-permute-start.2 = (f32[1,2,2,128,128]{4,3,2,1,0:T(8,128)}, f32[1,2,2,128,128]{4,3,2,1,0:T(8,128)S(1)}, u32[]{:S(2)}, u32[]{:S(2)}) collective-permute-start(f32[1,2,2,128,128]{4,3,2,1,0:T(8,128)} %get-tuple-element.23.refs_4_), channel_id=1, source_target_pairs={{0,7},{1,0},{2,1},{3,2},{4,3},{5,4},{6,5},{7,6},{8,15},{9,8},{10,9... | collective-permute-start | bytes 786440 | tf_op jit(solution)/shard_map/ppermute | solution.py:413
  6.1 11.8 %collective-permute-start.3 = (f32[1,2,2,128,128]{4,3,2,1,0:T(8,128)}, f32[1,2,2,128,128]{4,3,2,1,0:T(8,128)S(1)}, u32[]{:S(2)}, u32[]{:S(2)}) collective-permute-start(f32[1,2,2,128,128]{4,3,2,1,0:T(8,128)} %get-tuple-element.25.refs_4_), channel_id=1, source_target_pairs={{0,7},{1,0},{2,1},{3,2},{4,3},{5,4},{6,5},{7,6},{8,15},{9,8},{10,9... | collective-permute-start | bytes 786440 | tf_op jit(solution)/shard_map/ppermute | solution.py:413
  7.1 1.2 %copy-start.3 = (f32[4,256,256]{2,1,0:T(8,128)S(1)}, f32[4,256,256]{2,1,0:T(8,128)}, u32[]{:S(2)}) copy-start(f32[4,256,256]{2,1,0:T(8,128)} %absorb_ref.3) | copy-start | bytes 3145732
  8.3 1.2 %copy-start = (bf16[2,256,256]{2,1,0:T(8,128)(2,1)S(1)}, bf16[2,256,256]{2,1,0:T(8,128)(2,1)}, u32[]{:S(2)}) copy-start(bf16[2,256,256]{2,1,0:T(8,128)(2,1)} %constant.23.clone.refs_3_) | copy-start | bytes 786436
  8.3 1.2 %copy-start.1 = (bf16[2,256,256]{2,1,0:T(8,128)(2,1)S(1)}, bf16[2,256,256]{2,1,0:T(8,128)(2,1)}, u32[]{:S(2)}) copy-start(bf16[2,256,256]{2,1,0:T(8,128)(2,1)} %constant.22.clone.refs_2_) | copy-start | bytes 786436
  8.3 1.2 %copy-start.4 = (f32[1,4,2,128,128]{4,3,2,1,0:T(8,128)S(1)}, f32[1,4,2,128,128]{4,3,2,1,0:T(8,128)}, u32[]{:S(2)}) copy-start(f32[1,4,2,128,128]{4,3,2,1,0:T(8,128)} %param.11) | copy-start | bytes 1572868
  8.3 1.3 %copy-start.8 = (f32[1,2,2,128,128]{4,3,2,1,0:T(8,128)S(1)}, f32[1,2,2,128,128]{4,3,2,1,0:T(8,128)}, u32[]{:S(2)}) copy-start(f32[1,2,2,128,128]{4,3,2,1,0:T(8,128)} %get-tuple-element.19.refs_4_) | copy-start | bytes 786436
  9.2 3.1 %copy-start.7 = (f32[1,2,2,128,128]{4,3,2,1,0:T(8,128)S(1)}, f32[1,2,2,128,128]{4,3,2,1,0:T(8,128)}, u32[]{:S(2)}) copy-start(f32[1,2,2,128,128]{4,3,2,1,0:T(8,128)} %get-tuple-element.21.refs_4_) | copy-start | bytes 786436
  10.8 4.3 %copy-start.6 = (f32[1,2,2,128,128]{4,3,2,1,0:T(8,128)S(1)}, f32[1,2,2,128,128]{4,3,2,1,0:T(8,128)}, u32[]{:S(2)}) copy-start(f32[1,2,2,128,128]{4,3,2,1,0:T(8,128)} %get-tuple-element.23.refs_4_) | copy-start | bytes 786436
  13.4 4.5 %copy-start.5 = (f32[1,2,2,128,128]{4,3,2,1,0:T(8,128)S(1)}, f32[1,2,2,128,128]{4,3,2,1,0:T(8,128)}, u32[]{:S(2)}) copy-start(f32[1,2,2,128,128]{4,3,2,1,0:T(8,128)} %get-tuple-element.25.refs_4_) | copy-start | bytes 786436
  18.7 4.0 %copy-start.9 = (f32[2,128,128]{2,1,0:T(8,128)S(1)}, f32[2,128,128]{2,1,0:T(8,128)}, u32[]{:S(2)}) copy-start(f32[2,128,128]{2,1,0:T(8,128)} %refs_1_.3) | copy-start | bytes 393220
  18.8 11.4 %collective-permute-start.6 = (f32[2,2,128,128]{3,2,1,0:T(8,128)S(1)}, f32[2,2,128,128]{3,2,1,0:T(8,128)S(1)}, u32[]{:S(2)}, u32[]{:S(2)}) collective-permute-start(f32[2,2,128,128]{3,2,1,0:T(8,128)S(1)} %get-tuple-element.30.refs_9_), channel_id=1, source_target_pairs={{0,8},{8,16},{16,24},{24,32},{32,40},{40,48},{48,56},{56,64},{64,7... | collective-permute-start | bytes 786440 | tf_op jit(solution)/shard_map/ppermute | solution.py:448
  21.1 12.9 %collective-permute-start.4 = (f32[2,2,128,128]{3,2,1,0:T(8,128)S(1)}, f32[2,2,128,128]{3,2,1,0:T(8,128)S(1)}, u32[]{:S(2)}, u32[]{:S(2)}) collective-permute-start(f32[2,2,128,128]{3,2,1,0:T(8,128)S(1)} %leave1.1.refs_8_.refs_10_), channel_id=1, source_target_pairs={{0,8},{8,16},{16,24},{24,32},{32,40},{40,48},{48,56},{56,64},{64,7... | collective-permute-start | bytes 786440 | tf_op jit(solution)/shard_map/ppermute | solution.py:448
  33.2 10.0 %collective-permute-start.7 = (f32[2,2,128,128]{3,2,1,0:T(8,128)S(1)}, f32[2,2,128,128]{3,2,1,0:T(8,128)S(1)}, u32[]{:S(2)}, u32[]{:S(2)}) collective-permute-start(f32[2,2,128,128]{3,2,1,0:T(8,128)S(1)} %tick1_0.1.refs_11_), channel_id=1, source_target_pairs={{0,8},{8,16},{16,24},{24,32},{32,40},{40,48},{48,56},{56,64},{64,7... | collective-permute-start | bytes 786440 | tf_op jit(solution)/shard_map/ppermute | solution.py:448
  37.0 10.3 %collective-permute-start.5 = (f32[2,2,128,128]{3,2,1,0:T(8,128)S(1)}, f32[2,2,128,128]{3,2,1,0:T(8,128)S(1)}, u32[]{:S(2)}, u32[]{:S(2)}) collective-permute-start(f32[2,2,128,128]{3,2,1,0:T(8,128)S(1)} %tick1_1.1.refs_8_.refs_12_), channel_id=1, source_target_pairs={{0,8},{8,16},{16,24},{24,32},{32,40},{40,48},{48,56},{56,64},{64,7... | collective-permute-start | bytes 786440 | tf_op jit(solution)/shard_map/ppermute | solution.py:448

commit v5 on v4

--- a/solution.py
+++ b/solution.py
@@ -11,10 +11,11 @@
 from jax.sharding import PartitionSpec as P
 
 TICKS = 3
-CHUNKS = 2
+GROUPS = [[0], [1], [2], [3]]
 
 fresnel = 0.1
 VMEM_LIMIT = 24 * 1024 * 1024
+WEIGHT = 8
 WIDE_LIMIT = 62 * 1024 * 1024
 
 SIN_TERMS = [(-1.0) ** j / math.factorial(2 * j + 1) for j in range(7)]
@@ -203,24 +204,28 @@
     return [refs.pop(0) for _ in range(count)]
 
 
-def entry_kernel(layers, probes, with_pieces, starts, ends, *refs):
+def entry_kernel(layers, groups, base, with_pieces, starts, ends, with_after, *refs):
     refs = list(refs)
     anchors_ref, wave_ref, right_ref, left_ref = take(refs, 4)
     if with_pieces:
         piece_refs = take(refs, 3)
-        (out_ref,) = take(refs, 1)
+        take(refs, with_after)
+        out_refs = take(refs, len(groups))
         ext_refs = take(refs, len(layers))
     else:
         piece_refs = []
         ext_refs = take(refs, len(layers))
-        (out_ref,) = take(refs, 1)
+        take(refs, with_after)
+        out_refs = take(refs, len(groups))
+    places = [(g, at) for g, group in enumerate(groups) for at in range(len(group))]
 
     def put(n, part, wave):
-        out_ref[n, part] = wave
+        g, at = places[n]
+        out_refs[g][at, part] = wave
 
     advance(
-        0, layers, probes, starts, ends, piece_refs, ext_refs, anchors_ref,
-        lambda n, part: wave_ref[n, part], put, (right_ref, left_ref), refs,
+        0, layers, sum(groups, []), starts, ends, piece_refs, ext_refs, anchors_ref,
+        lambda n, part: wave_ref[base + n, part], put, (right_ref, left_ref), refs,
     )
 
 
@@ -243,20 +248,22 @@
         )
 
 
-def tick_kernel(tick, layers, probes, stores, own_store, *refs):
+def tick_kernel(tick, layers, probes, stores, own_store, with_after, *refs):
     refs = list(refs)
     anchors_ref, wave_ref, right_ref, left_ref = take(refs, 4)
     ext_refs = take(refs, len(layers))
     (first_ref,) = take(refs, 1)
     stored_refs = take(refs, len(stores))
     if own_store:
-        take(refs, 1)
+        take(refs, 1 + with_after)
         (final_ref,) = take(refs, 1)
         sem, out_ref = refs.pop(), refs.pop()
     elif stores:
+        take(refs, with_after)
         out_ref, final_ref = take(refs, 2)
         sem = refs.pop()
     else:
+        take(refs, with_after)
         (out_ref,) = take(refs, 1)
 
     copies = []
@@ -272,7 +279,7 @@
 
     @pl.when(depth == 0)
     def _():
-        out_ref[...] = first_ref[...]
+        out_ref[...] = first_ref[probes[0] : probes[0] + len(probes)]
 
     @pl.when(depth != 0)
     def _():
@@ -299,7 +306,11 @@
 
 def call(kernel, operands, specs, out_shape, out_specs, n, size, layers, name, **rest):
     grid = rest.pop("grid", (1,))
-    flops = grid[0] * layers * n * 2 * 3 * 2 * size * (2 * size) ** 2
+    flops = WEIGHT * grid[0] * layers * n * 2 * 3 * 2 * size * (2 * size) ** 2
+    after = rest.pop("after", None)
+    if after is not None:
+        operands.append(after)
+        specs.append(pl.BlockSpec(memory_space=pl.ANY))
     return pl.pallas_call(
         kernel,
         grid=grid,
@@ -323,16 +334,17 @@
     )(*operands)
 
 
-def entry(layers, probes, anchors, tables, wave, pieces, exts, starts, ends, tile_rows, name):
+def entry(
+    layers, groups, anchors, tables, wave, pieces, exts, starts, ends, tile_rows, name, after=None
+):
     size = wave.shape[-1]
-    count, n = len(layers), len(probes)
-    first = probes[0] // n if wave.shape[0] != n else 0
+    count, n = len(layers), sum(map(len, groups))
+    base = groups[0][0] if wave.shape[0] != n else 0
     operands = [anchors, wave, *tables]
-    specs = [
-        vmem(), pl.BlockSpec((n, 2, size, size), lambda i: (first, 0, 0, 0)),
-        vmem(), vmem(),
+    specs = [vmem()] * 4
+    out_shape = [
+        jax.ShapeDtypeStruct((len(group), 2, size, size), jnp.float32) for group in groups
     ]
-    out_shape = [jax.ShapeDtypeStruct((n, 2, size, size), jnp.float32)]
     if pieces is not None:
         operands += [piece for piece, _ in pieces]
         for _, at in pieces:
@@ -346,10 +358,11 @@
         operands += exts
         specs += [vmem()] * count
     kernel = functools.partial(
-        entry_kernel, layers, probes, pieces is not None, starts, ends
+        entry_kernel, layers, groups, base, pieces is not None, starts, ends, after is not None
     )
     return call(
-        kernel, operands, specs, out_shape, [vmem()] * len(out_shape), n, size, count, name
+        kernel, operands, specs, out_shape, [vmem()] * len(out_shape), n, size, count, name,
+        after=after,
     )
 
 
@@ -367,18 +380,15 @@
 
 
 def tick_section(
-    tick, c, n, anchors, tables, wave, exts, first, stored=(), out_shape=None, out=None
+    tick, probes, anchors, tables, wave, exts, first, after, stored=(), out_shape=None, out=None
 ):
     size = wave.shape[-1]
-    count = len(exts)
-    probes = list(range(c * n, (c + 1) * n))
+    count, n = len(exts), len(probes)
     operands = [anchors, wave, *tables, *exts, first, *(part for _, part in stored)]
-    specs = [vmem()] * (4 + count)
-    specs.append(pl.BlockSpec((n, 2, size, size), lambda i: (c, 0, 0, 0)))
-    specs += [vmem()] * len(stored)
+    specs = [vmem()] * (5 + count + len(stored))
     shape = [jax.ShapeDtypeStruct((n, 2, size, size), jnp.float32)]
     out_specs = [vmem()]
-    rest = {}
+    rest = {"after": after}
     if out is not None:
         rest["input_output_aliases"] = {len(operands): 0}
         operands.append(out)
@@ -394,10 +404,10 @@
         rest["scratch"] = [pltpu.SemaphoreType.DMA((len(stored),))]
     kernel = functools.partial(
         tick_kernel, tick, list(range(count)), probes, [to for to, _ in stored],
-        out is not None,
+        out is not None, after is not None,
     )
     return call(
-        kernel, operands, specs, shape, out_specs, n, size, count, f"tick{tick}_{c}", **rest
+        kernel, operands, specs, shape, out_specs, n, size, count, f"tick{tick}_{probes[0]}", **rest
     )
 
 
@@ -420,8 +430,6 @@
     anchors = jnp.broadcast_to(anchors.reshape(-1, 1), (anchors.size, size))
     held = waves_in[0]
     count = held.shape[0]
-    per_chunk = count // CHUNKS
-    groups = [list(range(c * per_chunk, (c + 1) * per_chunk)) for c in range(CHUNKS)]
     exts = []
     done = []
     for r in range(slices):
@@ -430,40 +438,39 @@
         edges = (r == 0, r == slices - 1, tile_rows)
         if r < slices - 1:
             held, *made = entry(
-                layers, list(range(count)), anchors, tables, held, pieces, None, *edges, f"enter{r}"
+                layers, [list(range(count))], anchors, tables, held, pieces, None, *edges, f"enter{r}"
             )
             exts += made
             continue
-        for c, group in enumerate(groups):
-            sources = (pieces, None) if c == 0 else (None, exts[-1:])
-            left, *made = entry(
-                layers, group, anchors, tables, held, *sources, *edges, f"leave{c}"
-            )
-            exts += made
-            done.append(left)
+        left, *made = entry(
+            layers, GROUPS[:1], anchors, tables, held, pieces, None, *edges, "leave0"
+        )
+        exts += made
+        done = [left]
+        done += entry(
+            layers, GROUPS[1:], anchors, tables, held, None, exts[-1:], *edges, "leave1", left
+        )
 
     stored = []
     for tick in range(1, TICKS):
-        stored += [((tick - 1, c * per_chunk), part) for c, part in enumerate(done)]
+        stored += [((tick - 1, group[0]), part) for group, part in zip(GROUPS, done)]
         arrived = [lax.ppermute(left, "depth", onward) for left in done]
-        first = first_section(
-            tick, per_chunk, anchors, tables, probe_wave, exts, done[-1], CHUNKS
-        )
+        first = first_section(tick, 1, anchors, tables, probe_wave, exts, done[-1], count)
         done = []
-        out = None
-        for c in range(CHUNKS):
+        for c, group in enumerate(GROUPS):
             last = {}
-            if tick == TICKS - 1:
+            if tick == TICKS - 1 and c == 0:
                 shape = jax.ShapeDtypeStruct((TICKS, count, *held.shape[1:]), held.dtype)
                 last = dict(stored=stored, out_shape=shape)
-                if c == CHUNKS - 1:
-                    last = dict(stored=stored, out=out)
+            elif tick == TICKS - 1 and c == len(GROUPS) - 1:
+                stored = [((tick, other[0]), part) for other, part in zip(GROUPS, done)]
+                last = dict(stored=stored, out=out)
             left, *made = tick_section(
-                tick, c, per_chunk, anchors, tables, arrived[c], exts, first, **last
+                tick, group, anchors, tables, arrived[c], exts, first,
+                done[-1] if done else None, **last
             )
             if made:
                 out = made[0]
-                stored = [((tick, c * per_chunk), left)]
             done.append(left)
     out = done[-1]
     return out[:, None]

time: 51.3 us -> 54.8 us (1.068)
  waiting for transfers between devices: 20.5 us -> 11.5 us
  starting transfers between devices: 7.31 us -> 14 us
  Pallas kernels: 21.4 us -> 27.3 us
    ppermute x4 -> x8, waiting for transfers between devices: 15.4 us -> 6.33 us  [shards(): arrived = [lax.ppermute(left, 'depth', onward) for left in done]]
    ppermute x4 -> x8, starting transfers between devices: 3.31 us -> 10 us  [shards(): arrived = [lax.ppermute(left, 'depth', onward) for left in done]]
    pallas_call x11 -> x15, Pallas kernels: 17.8 us -> 23.6 us  [call(): pl.pallas_call(kernel, grid=grid, in_specs=specs, out_specs=out_specs, ou...]
  transfers between devices with their start and end apart: 8 -> 12, of which waited for: 8 -> 6; matrix products, arithmetic and copies ran while one was open for 1% -> 1% of each run, Pallas kernels for 28% -> 38%
where the time goes in v5:
time: 54.8 us; the launch traced here: 54.6 us
  Pallas kernels  27.3 us (50%)
  starting transfers between devices  14 us (26%)
  waiting for transfers between devices  11.5 us (21%)
  local copies, waits for them, and re-layouts  1.54 us (3%)
    pallas_call x15, Pallas kernels, call(): pl.pallas_call(kernel, grid=grid, in_specs=specs, out_specs=out_specs, ou...  23.6 us
    ppermute x8, starting transfers between devices, shards(): arrived = [lax.ppermute(left, 'depth', onward) for left in done]  10 us
    ppermute x8, waiting for transfers between devices, shards(): arrived = [lax.ppermute(left, 'depth', onward) for left in done]  6.33 us
    ppermute x4, waiting for transfers between devices, shards(): rims = [lax.ppermute(first, 'tile', back) for first in firsts]  5.12 us
    ppermute x4, starting transfers between devices, shards(): rims = [lax.ppermute(first, 'tile', back) for first in firsts]  4 us
    pallas_call x1, Pallas kernels, edge_rows(): pl.pallas_call(edge_kernel, out_shape=[shape] * count, in_specs=[hbm()] *...  2.82 us
    unnamed x24, local copies, waits for them, and re-layouts  1.28 us
  transfers between devices with their start and end apart: 12, of which 6 were waited for; matrix products, arithmetic and copies ran while one was open for 1% of the time, Pallas kernels for 38%

profile of v5, /device:TPU:96, one launch (start us, length us, event | category | flops | bytes accessed | tf_op | source)
XLA Modules:
  0.0 54.6 jit_solution(11611691835518948380)
XLA Ops:
  0.0 0.0 copy-start
  0.0 0.0 copy-start.11
  0.0 2.8 %edge.1 = (f32[1,2,2,128,128]{4,3,2,1,0:T(8,128)}, f32[1,2,2,128,128]{4,3,2,1,0:T(8,128)}, f32[1,2,2,128,128]{4,3,2,1,0:T(8,128)}, f32[1,2,2,128,128]{4,3,2,1,0:T(8,128)}) custom-call(f32[4,256,256]{2,1,0:T(8,128)} %phase_ref.3, f32[4,256,256]{2,1,0:T(8,128)} %absorb_ref.3), custom_call_target="tpu_custom_call" | custom-call | flops 5242880 | bytes 2097152 | tf_op jit(solution)/shard_map/edge/pallas_call | solution.py:104
  2.8 2.5 %collective-permute-start = (f32[1,2,2,128,128]{4,3,2,1,0:T(8,128)}, f32[1,2,2,128,128]{4,3,2,1,0:T(8,128)S(1)}, u32[]{:S(2)}, u32[]{:S(2)}) collective-permute-start(f32[1,2,2,128,128]{4,3,2,1,0:T(8,128)} %get-tuple-element.22.refs_4_), channel_id=1, source_target_pairs={{0,7},{1,0},{2,1},{3,2},{4,3},{5,4},{6,5},{7,6},{8,15},{9,8},{10,9... | collective-permute-start | bytes 786440 | tf_op jit(solution)/shard_map/ppermute | solution.py:423
  5.3 0.7 %collective-permute-start.1 = (f32[1,2,2,128,128]{4,3,2,1,0:T(8,128)}, f32[1,2,2,128,128]{4,3,2,1,0:T(8,128)S(1)}, u32[]{:S(2)}, u32[]{:S(2)}) collective-permute-start(f32[1,2,2,128,128]{4,3,2,1,0:T(8,128)} %get-tuple-element.24.refs_4_), channel_id=1, source_target_pairs={{0,7},{1,0},{2,1},{3,2},{4,3},{5,4},{6,5},{7,6},{8,15},{9,8},{10,9... | collective-permute-start | bytes 786440 | tf_op jit(solution)/shard_map/ppermute | solution.py:423
  6.0 0.2 collective-permute-start.2
  6.2 0.7 %collective-permute-start.3 = (f32[1,2,2,128,128]{4,3,2,1,0:T(8,128)}, f32[1,2,2,128,128]{4,3,2,1,0:T(8,128)S(1)}, u32[]{:S(2)}, u32[]{:S(2)}) collective-permute-start(f32[1,2,2,128,128]{4,3,2,1,0:T(8,128)} %get-tuple-element.28.refs_4_), channel_id=1, source_target_pairs={{0,7},{1,0},{2,1},{3,2},{4,3},{5,4},{6,5},{7,6},{8,15},{9,8},{10,9... | collective-permute-start | bytes 786440 | tf_op jit(solution)/shard_map/ppermute | solution.py:423
  6.8 0.0 copy-done.11
  6.8 0.0 copy-done.10
  6.8 0.1 dynamic-slice_add_fusion
  6.9 0.1 copy.10
  7.0 0.1 broadcast_in_dim.10
  7.1 0.0 copy-done
  7.1 0.0 copy-start.1
  7.1 1.2 %copy-done.1 = f32[4,256,256]{2,1,0:T(8,128)S(1)} copy-done((f32[4,256,256]{2,1,0:T(8,128)S(1)}, f32[4,256,256]{2,1,0:T(8,128)}, u32[]{:S(2)}) %copy-start.1) | copy-done | bytes 1048600
  8.3 0.0 copy-start.6
  8.3 0.0 copy-start.8
  8.4 0.0 copy-start.9
  8.4 0.8 %rest.1.refs_5_ = f32[4,2,2,128,128]{4,3,2,1,0:T(8,128)S(1)} custom-call(f32[4,256,256]{2,1,0:T(8,128)S(1)} %copy-done, f32[4,256,256]{2,1,0:T(8,128)S(1)} %copy-done.1), custom_call_target="tpu_custom_call" | custom-call | flops 5242880 | bytes 2097152 | tf_op jit(solution)/shard_map/rest/pallas_call | solution.py:126
  9.2 0.3 collective-permute-done.refs_6_
  9.5 0.1 broadcast_in_dim.11.refs_0_
  9.6 0.0 copy-done.2
  9.6 0.0 copy-done.6
  9.6 0.0 copy-done.8
  9.6 0.0 copy-done.9
  9.6 0.0 copy-start.5
  9.6 1.2 %enter0.1 = (f32[4,2,128,128]{3,2,1,0:T(8,128)S(1)}, f32[2,2,384,128]{3,2,1,0:T(8,128)S(1)}) custom-call(s32[24,128]{1,0:T(8,128)S(1)} %broadcast_in_dim.11.refs_0_, f32[4,2,128,128]{3,2,1,0:T(8,128)S(1)} %bitcast.7, bf16[2,256,256]{2,1,0:T(8,128)(2,1)S(1)} %copy-done.9, bf16[2,256,256]{2,1,0:T(8,128)(2,1)S(1)} %copy-done.8, ...), custom_call_target="tpu_custom_call" | custom-call | flops 3221225472 | bytes 786432 | tf_op jit(solution)/shard_map/enter0/pallas_call | solution.py:314
  10.8 1.5 %collective-permute-done.1.refs_6_ = f32[1,2,2,128,128]{4,3,2,1,0:T(8,128)S(1)} collective-permute-done((f32[1,2,2,128,128]{4,3,2,1,0:T(8,128)}, f32[1,2,2,128,128]{4,3,2,1,0:T(8,128)S(1)}, u32[]{:S(2)}, u32[]{:S(2)}) %collective-permute-start.1) | collective-permute-done | bytes 262176 | tf_op jit(solution)/shard_map/ppermute | solution.py:423
  12.3 0.0 copy-done.5
  12.3 0.0 copy-start.4
  12.3 1.1 %enter1.1 = (f32[4,2,128,128]{3,2,1,0:T(8,128)S(1)}, f32[2,2,384,128]{3,2,1,0:T(8,128)S(1)}) custom-call(s32[24,128]{1,0:T(8,128)S(1)} %broadcast_in_dim.11.refs_0_, f32[4,2,128,128]{3,2,1,0:T(8,128)S(1)} %get-tuple-element.23.refs_1_, bf16[2,256,256]{2,1,0:T(8,128)(2,1)S(1)} %copy-done.9, bf16[2,256,256]{2,1,0:T(8,128)(2,1)S(1)} %copy-done.8, ...), custom_call_target="tpu_custom_call" | custom-call | flops 3221225472 | bytes 786432 | tf_op jit(solution)/shard_map/enter1/pallas_call | solution.py:314
  13.5 1.7 %collective-permute-done.2.refs_6_ = f32[1,2,2,128,128]{4,3,2,1,0:T(8,128)S(1)} collective-permute-done((f32[1,2,2,128,128]{4,3,2,1,0:T(8,128)}, f32[1,2,2,128,128]{4,3,2,1,0:T(8,128)S(1)}, u32[]{:S(2)}, u32[]{:S(2)}) %collective-permute-start.2) | collective-permute-done | bytes 262176 | tf_op jit(solution)/shard_map/ppermute | solution.py:423
  15.1 0.0 copy-done.4
  15.1 0.0 copy-start.3
  15.1 1.1 %enter2.1 = (f32[4,2,128,128]{3,2,1,0:T(8,128)S(1)}, f32[2,2,384,128]{3,2,1,0:T(8,128)S(1)}) custom-call(s32[24,128]{1,0:T(8,128)S(1)} %broadcast_in_dim.11.refs_0_, f32[4,2,128,128]{3,2,1,0:T(8,128)S(1)} %get-tuple-element.25.refs_1_, bf16[2,256,256]{2,1,0:T(8,128)(2,1)S(1)} %copy-done.9, bf16[2,256,256]{2,1,0:T(8,128)(2,1)S(1)} %copy-done.8, ...), custom_call_target="tpu_custom_call" | custom-call | flops 3221225472 | bytes 786432 | tf_op jit(solution)/shard_map/enter2/pallas_call | solution.py:314
  16.3 1.7 %collective-permute-done.3.refs_6_ = f32[1,2,2,128,128]{4,3,2,1,0:T(8,128)S(1)} collective-permute-done((f32[1,2,2,128,128]{4,3,2,1,0:T(8,128)}, f32[1,2,2,128,128]{4,3,2,1,0:T(8,128)S(1)}, u32[]{:S(2)}, u32[]{:S(2)}) %collective-permute-start.3) | collective-permute-done | bytes 262176 | tf_op jit(solution)/shard_map/ppermute | solution.py:423
  17.9 0.0 copy-done.3
  17.9 0.7 %leave0.1 = (f32[1,2,128,128]{3,2,1,0:T(8,128)S(1)}, f32[2,2,384,128]{3,2,1,0:T(8,128)S(1)}) custom-call(s32[24,128]{1,0:T(8,128)S(1)} %broadcast_in_dim.11.refs_0_, f32[4,2,128,128]{3,2,1,0:T(8,128)S(1)} %get-tuple-element.27.refs_1_, bf16[2,256,256]{2,1,0:T(8,128)(2,1)S(1)} %copy-done.9, bf16[2,256,256]{2,1,0:T(8,128)(2,1)S(1)} %copy-done.8, ...), custom_call_target="tpu_custom_call" | custom-call | flops 805306368 | bytes 786432 | tf_op jit(solution)/shard_map/leave0/pallas_call | solution.py:314
  18.6 1.6 %collective-permute-start.7 = (f32[1,2,128,128]{3,2,1,0:T(8,128)S(1)}, f32[1,2,128,128]{3,2,1,0:T(8,128)S(1)}, u32[]{:S(2)}, u32[]{:S(2)}) collective-permute-start(f32[1,2,128,128]{3,2,1,0:T(8,128)S(1)} %get-tuple-element.30.refs_5_.refs_9_), channel_id=1, source_target_pairs={{0,8},{8,16},{16,24},{24,32},{32,40},{40,48},{48,56},{56,64},{64,7... | collective-permute-start | bytes 393224 | tf_op jit(solution)/shard_map/ppermute | solution.py:457
  20.2 1.1 %leave1.1 = (f32[1,2,128,128]{3,2,1,0:T(8,128)S(1)}, f32[1,2,128,128]{3,2,1,0:T(8,128)S(1)}, f32[1,2,128,128]{3,2,1,0:T(8,128)S(1)}) custom-call(s32[24,128]{1,0:T(8,128)S(1)} %broadcast_in_dim.11.refs_0_, f32[4,2,128,128]{3,2,1,0:T(8,128)S(1)} %get-tuple-element.27.refs_1_, bf16[2,256,256]{2,1,0:T(8,128)(2,1)S(1)} %copy-done.9, ...), custom_call_target="tpu_custom_call" | custom-call | flops 2415919104 | bytes 786432 | tf_op jit(solution)/shard_map/leave1/pallas_call | solution.py:314
  21.2 1.6 %collective-permute-start.5 = (f32[1,2,128,128]{3,2,1,0:T(8,128)S(1)}, f32[1,2,128,128]{3,2,1,0:T(8,128)S(1)}, u32[]{:S(2)}, u32[]{:S(2)}) collective-permute-start(f32[1,2,128,128]{3,2,1,0:T(8,128)S(1)} %get-tuple-element.35.refs_11_), channel_id=1, source_target_pairs={{0,8},{8,16},{16,24},{24,32},{32,40},{40,48},{48,56},{56,64},{64,7... | collective-permute-start | bytes 393224 | tf_op jit(solution)/shard_map/ppermute | solution.py:457
  22.8 1.2 %collective-permute-start.6 = (f32[1,2,128,128]{3,2,1,0:T(8,128)S(1)}, f32[1,2,128,128]{3,2,1,0:T(8,128)S(1)}, u32[]{:S(2)}, u32[]{:S(2)}) collective-permute-start(f32[1,2,128,128]{3,2,1,0:T(8,128)S(1)} %get-tuple-element.36.refs_10_), channel_id=1, source_target_pairs={{0,8},{8,16},{16,24},{24,32},{32,40},{40,48},{48,56},{56,64},{64,7... | collective-permute-start | bytes 393224 | tf_op jit(solution)/shard_map/ppermute | solution.py:457
  24.0 0.1 collective-permute-start.4
  24.1 0.0 copy-done.7
  24.1 2.5 %collective-permute-done.7.refs_1_ = f32[1,2,128,128]{3,2,1,0:T(8,128)S(1)} collective-permute-done((f32[1,2,128,128]{3,2,1,0:T(8,128)S(1)}, f32[1,2,128,128]{3,2,1,0:T(8,128)S(1)}, u32[]{:S(2)}, u32[]{:S(2)}) %collective-permute-start.7) | collective-permute-done | bytes 131104 | tf_op jit(solution)/shard_map/ppermute | solution.py:457
  26.5 2.2 %tick1_0.1.refs_9_.refs_13_ = f32[1,2,128,128]{3,2,1,0:T(8,128)S(1)} custom-call(s32[24,128]{1,0:T(8,128)S(1)} %broadcast_in_dim.11.refs_0_, f32[1,2,128,128]{3,2,1,0:T(8,128)S(1)} %collective-permute-done.7.refs_1_, bf16[2,256,256]{2,1,0:T(8,128)(2,1)S(1)} %copy-done.9, bf16[2,256,256]{2,1,0:T(8,128)(2,1)S(1)} %copy-done.8, ...), custom_call_target="tpu_custom_call" | custom-call | flops 3221225472 | bytes 3145728 | tf_op jit(solution)/shard_map/tick1_0/pallas_call | solution.py:314
  28.7 0.1 collective-permute-start.9
  28.8 3.8 %collective-permute-done.6.refs_1_ = f32[1,2,128,128]{3,2,1,0:T(8,128)S(1)} collective-permute-done((f32[1,2,128,128]{3,2,1,0:T(8,128)S(1)}, f32[1,2,128,128]{3,2,1,0:T(8,128)S(1)}, u32[]{:S(2)}, u32[]{:S(2)}) %collective-permute-start.6) | collective-permute-done | bytes 131104 | tf_op jit(solution)/shard_map/ppermute | solution.py:457
  32.7 2.2 %tick1_1.1.refs_9_.refs_14_ = f32[1,2,128,128]{3,2,1,0:T(8,128)S(1)} custom-call(s32[24,128]{1,0:T(8,128)S(1)} %broadcast_in_dim.11.refs_0_, f32[1,2,128,128]{3,2,1,0:T(8,128)S(1)} %collective-permute-done.6.refs_1_, bf16[2,256,256]{2,1,0:T(8,128)(2,1)S(1)} %copy-done.9, bf16[2,256,256]{2,1,0:T(8,128)(2,1)S(1)} %copy-done.8, ...), custom_call_target="tpu_custom_call" | custom-call | flops 3221225472 | bytes 3145728 | tf_op jit(solution)/shard_map/tick1_1/pallas_call | solution.py:314
  34.9 0.1 collective-permute-start.10
  34.9 0.0 collective-permute-done.5.refs_1_
  34.9 2.2 %tick1_2.1.refs_9_.refs_15_ = f32[1,2,128,128]{3,2,1,0:T(8,128)S(1)} custom-call(s32[24,128]{1,0:T(8,128)S(1)} %broadcast_in_dim.11.refs_0_, f32[1,2,128,128]{3,2,1,0:T(8,128)S(1)} %collective-permute-done.5.refs_1_, bf16[2,256,256]{2,1,0:T(8,128)(2,1)S(1)} %copy-done.9, bf16[2,256,256]{2,1,0:T(8,128)(2,1)S(1)} %copy-done.8, ...), custom_call_target="tpu_custom_call" | custom-call | flops 3221225472 | bytes 3145728 | tf_op jit(solution)/shard_map/tick1_2/pallas_call | solution.py:314
  37.1 0.7 %collective-permute-start.11 = (f32[1,2,128,128]{3,2,1,0:T(8,128)S(1)}, f32[1,2,128,128]{3,2,1,0:T(8,128)S(1)}, u32[]{:S(2)}, u32[]{:S(2)}) collective-permute-start(f32[1,2,128,128]{3,2,1,0:T(8,128)S(1)} %tick1_2.1.refs_9_.refs_15_), channel_id=1, source_target_pairs={{0,8},{8,16},{16,24},{24,32},{32,40},{40,48},{48,56},{56,64},{64,7... | collective-permute-start | bytes 393224 | tf_op jit(solution)/shard_map/ppermute | solution.py:457
  37.9 0.0 collective-permute-done.4.refs_1_
  37.9 2.2 %tick1_3.1.refs_8_.refs_16_ = f32[1,2,128,128]{3,2,1,0:T(8,128)S(1)} custom-call(s32[24,128]{1,0:T(8,128)S(1)} %broadcast_in_dim.11.refs_0_, f32[1,2,128,128]{3,2,1,0:T(8,128)S(1)} %collective-permute-done.4.refs_1_, bf16[2,256,256]{2,1,0:T(8,128)(2,1)S(1)} %copy-done.9, bf16[2,256,256]{2,1,0:T(8,128)(2,1)S(1)} %copy-done.8, ...), custom_call_target="tpu_custom_call" | custom-call | flops 3221225472 | bytes 3145728 | tf_op jit(solution)/shard_map/tick1_3/pallas_call | solution.py:314
  40.1 4.8 %collective-permute-start.8 = (f32[1,2,128,128]{3,2,1,0:T(8,128)S(1)}, f32[1,2,128,128]{3,2,1,0:T(8,128)S(1)}, u32[]{:S(2)}, u32[]{:S(2)}) collective-permute-start(f32[1,2,128,128]{3,2,1,0:T(8,128)S(1)} %tick1_3.1.refs_8_.refs_16_), channel_id=1, source_target_pairs={{0,8},{8,16},{16,24},{24,32},{32,40},{40,48},{48,56},{56,64},{64,7... | collective-permute-start | bytes 393224 | tf_op jit(solution)/shard_map/ppermute | solution.py:457
  44.8 0.0 collective-permute-done.9.refs_1_
  44.8 2.3 %tick2_0.1 = (f32[1,2,128,128]{3,2,1,0:T(8,128)S(1)}, f32[3,4,2,128,128]{4,3,2,1,0:T(8,128)}) custom-call(s32[24,128]{1,0:T(8,128)S(1)} %broadcast_in_dim.11.refs_0_, f32[1,2,128,128]{3,2,1,0:T(8,128)S(1)} %collective-permute-done.9.refs_1_, bf16[2,256,256]{2,1,0:T(8,128)(2,1)S(1)} %copy-done.9, bf16[2,256,256]{2,1,0:T(8,128)(2,1)S(1)} %copy-done.8, ...), custom_call_target="tpu_custom_call" | custom-call | flops 3221225472 | bytes 3145728 | tf_op jit(solution)/shard_map/tick2_0/pallas_call | solution.py:314
  47.1 0.0 collective-permute-done.10.refs_1_
  47.1 2.2 %tick2_1.1.refs_9_.refs_10_ = f32[1,2,128,128]{3,2,1,0:T(8,128)S(1)} custom-call(s32[24,128]{1,0:T(8,128)S(1)} %broadcast_in_dim.11.refs_0_, f32[1,2,128,128]{3,2,1,0:T(8,128)S(1)} %collective-permute-done.10.refs_1_, bf16[2,256,256]{2,1,0:T(8,128)(2,1)S(1)} %copy-done.9, bf16[2,256,256]{2,1,0:T(8,128)(2,1)S(1)} %copy-done.8, ...), custom_call_target="tpu_custom_call" | custom-call | flops 3221225472 | bytes 3145728 | tf_op jit(solution)/shard_map/tick2_1/pallas_call | solution.py:314
  49.3 0.0 collective-permute-done.11.refs_1_
  49.3 2.2 %tick2_2.1.refs_11_.refs_13_ = f32[1,2,128,128]{3,2,1,0:T(8,128)S(1)} custom-call(s32[24,128]{1,0:T(8,128)S(1)} %broadcast_in_dim.11.refs_0_, f32[1,2,128,128]{3,2,1,0:T(8,128)S(1)} %collective-permute-done.11.refs_1_, bf16[2,256,256]{2,1,0:T(8,128)(2,1)S(1)} %copy-done.9, bf16[2,256,256]{2,1,0:T(8,128)(2,1)S(1)} %copy-done.8, ...), custom_call_target="tpu_custom_call" | custom-call | flops 3221225472 | bytes 3145728 | tf_op jit(solution)/shard_map/tick2_2/pallas_call | solution.py:314
  51.5 0.0 collective-permute-done.8.refs_1_
  51.5 2.9 %tick2_3.1 = f32[3,4,2,128,128]{4,3,2,1,0:T(8,128)} custom-call(s32[24,128]{1,0:T(8,128)S(1)} %broadcast_in_dim.11.refs_0_, f32[1,2,128,128]{3,2,1,0:T(8,128)S(1)} %collective-permute-done.8.refs_1_, bf16[2,256,256]{2,1,0:T(8,128)(2,1)S(1)} %copy-done.9, bf16[2,256,256]{2,1,0:T(8,128)(2,1)S(1)} %copy-done.8, ...), custom_call_target="tpu_custom_call", output_to_operand_aliasing={{}: (12, {})} | custom-call | flops 3221225472 | bytes 3145728 | tf_op jit(solution)/shard_map/tick2_3/pallas_call | solution.py:314
  (6 shorter events, 0.0 us)
Async XLA Ops:
  0.0 7.1 %copy-start = (f32[4,256,256]{2,1,0:T(8,128)S(1)}, f32[4,256,256]{2,1,0:T(8,128)}, u32[]{:S(2)}) copy-start(f32[4,256,256]{2,1,0:T(8,128)} %phase_ref.3) | copy-start | bytes 3145732
  0.0 6.8 %copy-start.11 = (s32[18,4]{0,1:T(4,128)S(1)}, s32[18,4]{0,1:T(4,128)}, u32[]{:S(2)}) copy-start(s32[18,4]{0,1:T(4,128)} %param.12) | copy-start | bytes 868
  0.0 6.8 %copy-start.10 = (s32[18,4]{0,1:T(4,128)S(1)}, s32[18,4]{0,1:T(4,128)}, u32[]{:S(2)}) copy-start(s32[18,4]{0,1:T(4,128)} %param.13) | copy-start | bytes 868
  2.8 6.7 %collective-permute-start = (f32[1,2,2,128,128]{4,3,2,1,0:T(8,128)}, f32[1,2,2,128,128]{4,3,2,1,0:T(8,128)S(1)}, u32[]{:S(2)}, u32[]{:S(2)}) collective-permute-start(f32[1,2,2,128,128]{4,3,2,1,0:T(8,128)} %get-tuple-element.22.refs_4_), channel_id=1, source_target_pairs={{0,7},{1,0},{2,1},{3,2},{4,3},{5,4},{6,5},{7,6},{8,15},{9,8},{10,9... | collective-permute-start | bytes 786440 | tf_op jit(solution)/shard_map/ppermute | solution.py:423
  5.3 7.0 %collective-permute-start.1 = (f32[1,2,2,128,128]{4,3,2,1,0:T(8,128)}, f32[1,2,2,128,128]{4,3,2,1,0:T(8,128)S(1)}, u32[]{:S(2)}, u32[]{:S(2)}) collective-permute-start(f32[1,2,2,128,128]{4,3,2,1,0:T(8,128)} %get-tuple-element.24.refs_4_), channel_id=1, source_target_pairs={{0,7},{1,0},{2,1},{3,2},{4,3},{5,4},{6,5},{7,6},{8,15},{9,8},{10,9... | collective-permute-start | bytes 786440 | tf_op jit(solution)/shard_map/ppermute | solution.py:423
  6.0 9.1 %collective-permute-start.2 = (f32[1,2,2,128,128]{4,3,2,1,0:T(8,128)}, f32[1,2,2,128,128]{4,3,2,1,0:T(8,128)S(1)}, u32[]{:S(2)}, u32[]{:S(2)}) collective-permute-start(f32[1,2,2,128,128]{4,3,2,1,0:T(8,128)} %get-tuple-element.26.refs_4_), channel_id=1, source_target_pairs={{0,7},{1,0},{2,1},{3,2},{4,3},{5,4},{6,5},{7,6},{8,15},{9,8},{10,9... | collective-permute-start | bytes 786440 | tf_op jit(solution)/shard_map/ppermute | solution.py:423
  6.2 11.8 %collective-permute-start.3 = (f32[1,2,2,128,128]{4,3,2,1,0:T(8,128)}, f32[1,2,2,128,128]{4,3,2,1,0:T(8,128)S(1)}, u32[]{:S(2)}, u32[]{:S(2)}) collective-permute-start(f32[1,2,2,128,128]{4,3,2,1,0:T(8,128)} %get-tuple-element.28.refs_4_), channel_id=1, source_target_pairs={{0,7},{1,0},{2,1},{3,2},{4,3},{5,4},{6,5},{7,6},{8,15},{9,8},{10,9... | collective-permute-start | bytes 786440 | tf_op jit(solution)/shard_map/ppermute | solution.py:423
  7.1 1.2 %copy-start.1 = (f32[4,256,256]{2,1,0:T(8,128)S(1)}, f32[4,256,256]{2,1,0:T(8,128)}, u32[]{:S(2)}) copy-start(f32[4,256,256]{2,1,0:T(8,128)} %absorb_ref.3) | copy-start | bytes 3145732
  8.3 1.2 %copy-start.2 = (f32[1,4,2,128,128]{4,3,2,1,0:T(8,128)S(1)}, f32[1,4,2,128,128]{4,3,2,1,0:T(8,128)}, u32[]{:S(2)}) copy-start(f32[1,4,2,128,128]{4,3,2,1,0:T(8,128)} %param.11) | copy-start | bytes 1572868
  8.3 1.2 %copy-start.6 = (f32[1,2,2,128,128]{4,3,2,1,0:T(8,128)S(1)}, f32[1,2,2,128,128]{4,3,2,1,0:T(8,128)}, u32[]{:S(2)}) copy-start(f32[1,2,2,128,128]{4,3,2,1,0:T(8,128)} %get-tuple-element.22.refs_4_) | copy-start | bytes 786436
  8.3 1.2 %copy-start.8 = (bf16[2,256,256]{2,1,0:T(8,128)(2,1)S(1)}, bf16[2,256,256]{2,1,0:T(8,128)(2,1)}, u32[]{:S(2)}) copy-start(bf16[2,256,256]{2,1,0:T(8,128)(2,1)} %constant.23.clone.refs_3_) | copy-start | bytes 786436
  8.4 1.3 %copy-start.9 = (bf16[2,256,256]{2,1,0:T(8,128)(2,1)S(1)}, bf16[2,256,256]{2,1,0:T(8,128)(2,1)}, u32[]{:S(2)}) copy-start(bf16[2,256,256]{2,1,0:T(8,128)(2,1)} %constant.22.clone.refs_2_) | copy-start | bytes 786436
  9.6 2.7 %copy-start.5 = (f32[1,2,2,128,128]{4,3,2,1,0:T(8,128)S(1)}, f32[1,2,2,128,128]{4,3,2,1,0:T(8,128)}, u32[]{:S(2)}) copy-start(f32[1,2,2,128,128]{4,3,2,1,0:T(8,128)} %get-tuple-element.24.refs_4_) | copy-start | bytes 786436
  12.3 2.8 %copy-start.4 = (f32[1,2,2,128,128]{4,3,2,1,0:T(8,128)S(1)}, f32[1,2,2,128,128]{4,3,2,1,0:T(8,128)}, u32[]{:S(2)}) copy-start(f32[1,2,2,128,128]{4,3,2,1,0:T(8,128)} %get-tuple-element.26.refs_4_) | copy-start | bytes 786436
  15.1 2.8 %copy-start.3 = (f32[1,2,2,128,128]{4,3,2,1,0:T(8,128)S(1)}, f32[1,2,2,128,128]{4,3,2,1,0:T(8,128)}, u32[]{:S(2)}) copy-start(f32[1,2,2,128,128]{4,3,2,1,0:T(8,128)} %get-tuple-element.28.refs_4_) | copy-start | bytes 786436
  18.6 7.9 %collective-permute-start.7 = (f32[1,2,128,128]{3,2,1,0:T(8,128)S(1)}, f32[1,2,128,128]{3,2,1,0:T(8,128)S(1)}, u32[]{:S(2)}, u32[]{:S(2)}) collective-permute-start(f32[1,2,128,128]{3,2,1,0:T(8,128)S(1)} %get-tuple-element.30.refs_5_.refs_9_), channel_id=1, source_target_pairs={{0,8},{8,16},{16,24},{24,32},{32,40},{40,48},{48,56},{56,64},{64,7... | collective-permute-start | bytes 393224 | tf_op jit(solution)/shard_map/ppermute | solution.py:457
  20.2 3.9 %copy-start.7 = (f32[2,128,128]{2,1,0:T(8,128)S(1)}, f32[2,128,128]{2,1,0:T(8,128)}, u32[]{:S(2)}) copy-start(f32[2,128,128]{2,1,0:T(8,128)} %refs_1_.3) | copy-start | bytes 393220
  21.2 13.7 %collective-permute-start.5 = (f32[1,2,128,128]{3,2,1,0:T(8,128)S(1)}, f32[1,2,128,128]{3,2,1,0:T(8,128)S(1)}, u32[]{:S(2)}, u32[]{:S(2)}) collective-permute-start(f32[1,2,128,128]{3,2,1,0:T(8,128)S(1)} %get-tuple-element.35.refs_11_), channel_id=1, source_target_pairs={{0,8},{8,16},{16,24},{24,32},{32,40},{40,48},{48,56},{56,64},{64,7... | collective-permute-start | bytes 393224 | tf_op jit(solution)/shard_map/ppermute | solution.py:457
  22.8 9.9 %collective-permute-start.6 = (f32[1,2,128,128]{3,2,1,0:T(8,128)S(1)}, f32[1,2,128,128]{3,2,1,0:T(8,128)S(1)}, u32[]{:S(2)}, u32[]{:S(2)}) collective-permute-start(f32[1,2,128,128]{3,2,1,0:T(8,128)S(1)} %get-tuple-element.36.refs_10_), channel_id=1, source_target_pairs={{0,8},{8,16},{16,24},{24,32},{32,40},{40,48},{48,56},{56,64},{64,7... | collective-permute-start | bytes 393224 | tf_op jit(solution)/shard_map/ppermute | solution.py:457
  24.0 13.9 %collective-permute-start.4 = (f32[1,2,128,128]{3,2,1,0:T(8,128)S(1)}, f32[1,2,128,128]{3,2,1,0:T(8,128)S(1)}, u32[]{:S(2)}, u32[]{:S(2)}) collective-permute-start(f32[1,2,128,128]{3,2,1,0:T(8,128)S(1)} %get-tuple-element.31.refs_8_.refs_12_), channel_id=1, source_target_pairs={{0,8},{8,16},{16,24},{24,32},{32,40},{40,48},{48,56},{56,64},{64,7... | collective-permute-start | bytes 393224 | tf_op jit(solution)/shard_map/ppermute | solution.py:457
  28.7 16.1 %collective-permute-start.9 = (f32[1,2,128,128]{3,2,1,0:T(8,128)S(1)}, f32[1,2,128,128]{3,2,1,0:T(8,128)S(1)}, u32[]{:S(2)}, u32[]{:S(2)}) collective-permute-start(f32[1,2,128,128]{3,2,1,0:T(8,128)S(1)} %tick1_0.1.refs_9_.refs_13_), channel_id=1, source_target_pairs={{0,8},{8,16},{16,24},{24,32},{32,40},{40,48},{48,56},{56,64},{64,7... | collective-permute-start | bytes 393224 | tf_op jit(solution)/shard_map/ppermute | solution.py:457
  34.9 12.3 %collective-permute-start.10 = (f32[1,2,128,128]{3,2,1,0:T(8,128)S(1)}, f32[1,2,128,128]{3,2,1,0:T(8,128)S(1)}, u32[]{:S(2)}, u32[]{:S(2)}) collective-permute-start(f32[1,2,128,128]{3,2,1,0:T(8,128)S(1)} %tick1_1.1.refs_9_.refs_14_), channel_id=1, source_target_pairs={{0,8},{8,16},{16,24},{24,32},{32,40},{40,48},{48,56},{56,64},{64,7... | collective-permute-start | bytes 393224 | tf_op jit(solution)/shard_map/ppermute | solution.py:457
  37.1 12.2 %collective-permute-start.11 = (f32[1,2,128,128]{3,2,1,0:T(8,128)S(1)}, f32[1,2,128,128]{3,2,1,0:T(8,128)S(1)}, u32[]{:S(2)}, u32[]{:S(2)}) collective-permute-start(f32[1,2,128,128]{3,2,1,0:T(8,128)S(1)} %tick1_2.1.refs_9_.refs_15_), channel_id=1, source_target_pairs={{0,8},{8,16},{16,24},{24,32},{32,40},{40,48},{48,56},{56,64},{64,7... | collective-permute-start | bytes 393224 | tf_op jit(solution)/shard_map/ppermute | solution.py:457
  40.1 11.5 %collective-permute-start.8 = (f32[1,2,128,128]{3,2,1,0:T(8,128)S(1)}, f32[1,2,128,128]{3,2,1,0:T(8,128)S(1)}, u32[]{:S(2)}, u32[]{:S(2)}) collective-permute-start(f32[1,2,128,128]{3,2,1,0:T(8,128)S(1)} %tick1_3.1.refs_8_.refs_16_), channel_id=1, source_target_pairs={{0,8},{8,16},{16,24},{24,32},{32,40},{40,48},{48,56},{56,64},{64,7... | collective-permute-start | bytes 393224 | tf_op jit(solution)/shard_map/ppermute | solution.py:457

commit v6 on v5

--- a/solution.py
+++ b/solution.py
@@ -11,12 +11,12 @@
 from jax.sharding import PartitionSpec as P
 
 TICKS = 3
-GROUPS = [[0], [1], [2], [3]]
+GROUPS = [[0, 1], [2], [3]]
 
 fresnel = 0.1
 VMEM_LIMIT = 24 * 1024 * 1024
 WEIGHT = 8
-WIDE_LIMIT = 62 * 1024 * 1024
+EDGE_LIMIT = VMEM_LIMIT
 
 SIN_TERMS = [(-1.0) ** j / math.factorial(2 * j + 1) for j in range(7)]
 COS_TERMS = [(-1.0) ** j / math.factorial(2 * j) for j in range(8)]
@@ -77,13 +77,13 @@
     lax.fori_loop(0, rows // step, body, 0)
 
 
-def edge_kernel(phase_ref, absorb_ref, *refs):
+def edge_kernel(first, phase_ref, absorb_ref, *refs):
     *out_refs, phase_buf, absorb_buf, sem = refs
     count, rows = phase_buf.shape[:2]
     copies = []
     for layer in range(count):
         for n, (ref, buf) in enumerate([(phase_ref, phase_buf), (absorb_ref, absorb_buf)]):
-            source = ref.at[layer, pl.ds(0, rows)]
+            source = ref.at[first + layer, pl.ds(0, rows)]
             copies.append(pltpu.make_async_copy(source, buf.at[layer], sem.at[2 * layer + n]))
             copies[-1].start()
     for layer in range(count):
@@ -97,12 +97,12 @@
         trans_layer(phase_ref.at[layer], absorb_ref.at[layer], out_ref.at[layer])
 
 
-def edge_rows(phase_map, absorb, size):
-    count, _, columns = phase_map.shape
+def edge_rows(phase_map, absorb, size, layers):
+    count, columns = len(layers), phase_map.shape[2]
     shape = jax.ShapeDtypeStruct((1, 2, columns // size, size, size), jnp.float32)
     values = count * size * columns
     return pl.pallas_call(
-        edge_kernel,
+        functools.partial(edge_kernel, layers[0]),
         out_shape=[shape] * count,
         in_specs=[hbm()] * 2,
         out_specs=[vmem()] * count,
@@ -111,12 +111,12 @@
             pltpu.VMEM((count, size, columns), jnp.float32),
             pltpu.SemaphoreType.DMA((2 * count,)),
         ],
-        compiler_params=pltpu.CompilerParams(vmem_limit_bytes=WIDE_LIMIT),
+        compiler_params=pltpu.CompilerParams(vmem_limit_bytes=EDGE_LIMIT),
         cost_estimate=pl.CostEstimate(
             flops=values * 40, bytes_accessed=values * 16, transcendentals=values
         ),
-        name="edge",
-    )(phase_map, absorb)
+        name=f"edge{layers[0]}",
+    )(*(pltpu.with_memory_space_constraint(x, pltpu.HBM) for x in (phase_map, absorb)))
 
 
 def rest_rows(phase_map, absorb, size):
@@ -419,7 +419,8 @@
     back = [(i, (i - 1) % tiles) for i in range(tiles)]
     onward = [(i, (i + 1) % depth_count) for i in range(depth_count)]
 
-    firsts = edge_rows(phase_map, absorb, size)
+    firsts = edge_rows(phase_map, absorb, size, [0])
+    firsts += edge_rows(phase_map, absorb, size, list(range(1, slices)))
     rims = [lax.ppermute(first, "tile", back) for first in firsts]
     rest = rest_rows(phase_map, absorb, size)
 
@@ -455,7 +456,9 @@
     for tick in range(1, TICKS):
         stored += [((tick - 1, group[0]), part) for group, part in zip(GROUPS, done)]
         arrived = [lax.ppermute(left, "depth", onward) for left in done]
-        first = first_section(tick, 1, anchors, tables, probe_wave, exts, done[-1], count)
+        first = first_section(
+            tick, 2, anchors, tables, probe_wave, exts, done[-1], count // 2
+        )
         done = []
         for c, group in enumerate(GROUPS):
             last = {}

time: 54.8 us -> 50 us (0.912)
  starting transfers between devices: 14 us -> 10.7 us
  local copies, waits for them, and re-layouts: 1.54 us -> 0.54 us
  waiting for transfers between devices: 11.5 us -> 10.9 us
    ppermute x4, waiting for transfers between devices: 5.12 us -> 1.34 us  [shards(): rims = [lax.ppermute(first, 'tile', back) for first in firsts]]
    ppermute x8 -> x6, starting transfers between devices: 10 us -> 6.7 us  [shards(): arrived = [lax.ppermute(left, 'depth', onward) for left in done]]
    ppermute x8 -> x6, waiting for transfers between devices: 6.33 us -> 9.53 us  [shards(): arrived = [lax.ppermute(left, 'depth', onward) for left in done]]
    unnamed x24 -> x16, local copies, waits for them, and re-layouts: 1.28 us -> 0.28 us
    pallas_call x15 -> x13, Pallas kernels: 23.6 us -> 23.5 us  [call(): pl.pallas_call(kernel, grid=grid, in_specs=specs, out_specs=out_specs, ou...]
    pallas_call x1 -> x2, Pallas kernels: 2.82 us -> 2.75 us  [edge_rows(): pl.pallas_call(functools.partial(edge_kernel, layers[0]), out_shape=[shap...]
  transfers between devices with their start and end apart: 12 -> 10, of which waited for: 6 -> 4; matrix products, arithmetic and copies ran while one was open for 1% -> 1% of each run, Pallas kernels for 38% -> 45%
where the time goes in v6:
time: 50 us; the launch traced here: 49.6 us
  Pallas kernels  27.1 us (54%)
  waiting for transfers between devices  10.9 us (22%)
  starting transfers between devices  10.7 us (21%)
  local copies, waits for them, and re-layouts  0.54 us (1%)
    pallas_call x13, Pallas kernels, call(): pl.pallas_call(kernel, grid=grid, in_specs=specs, out_specs=out_specs, ou...  23.5 us
    ppermute x6, waiting for transfers between devices, shards(): arrived = [lax.ppermute(left, 'depth', onward) for left in done]  9.53 us
    ppermute x6, starting transfers between devices, shards(): arrived = [lax.ppermute(left, 'depth', onward) for left in done]  6.7 us
    ppermute x4, starting transfers between devices, shards(): rims = [lax.ppermute(first, 'tile', back) for first in firsts]  4.01 us
    pallas_call x2, Pallas kernels, edge_rows(): pl.pallas_call(functools.partial(edge_kernel, layers[0]), out_shape=[shap...  2.75 us
    ppermute x4, waiting for transfers between devices, shards(): rims = [lax.ppermute(first, 'tile', back) for first in firsts]  1.34 us
  transfers between devices with their start and end apart: 10, of which 4 were waited for; matrix products, arithmetic and copies ran while one was open for 1% of the time, Pallas kernels for 45%

profile of v6, /device:TPU:96, one launch (start us, length us, event | category | flops | bytes accessed | tf_op | source)
XLA Modules:
  0.0 49.6 jit_solution(2288923807709735176)
XLA Ops:
  0.0 1.2 %edge0.1.refs_4_ = f32[1,2,2,128,128]{4,3,2,1,0:T(8,128)S(1)} custom-call(f32[4,256,256]{2,1,0:T(8,128)} %phase_ref.5, f32[4,256,256]{2,1,0:T(8,128)} %absorb_ref.5), custom_call_target="tpu_custom_call" | custom-call | flops 1310720 | bytes 524288 | tf_op jit(solution)/shard_map/edge0/pallas_call | solution.py:104
  1.2 0.0 copy-start.7
  1.2 0.0 copy-start.6
  1.2 0.0 copy-start
  1.2 0.0 copy-start.1
  1.2 2.5 %collective-permute-start = (f32[1,2,2,128,128]{4,3,2,1,0:T(8,128)S(1)}, f32[1,2,2,128,128]{4,3,2,1,0:T(8,128)}, u32[]{:S(2)}, u32[]{:S(2)}) collective-permute-start(f32[1,2,2,128,128]{4,3,2,1,0:T(8,128)S(1)} %edge0.1.refs_4_), channel_id=1, source_target_pairs={{0,7},{1,0},{2,1},{3,2},{4,3},{5,4},{6,5},{7,6},{8,15},{9,8},{10,9... | collective-permute-start | bytes 786440 | tf_op jit(solution)/shard_map/ppermute | solution.py:424
  3.7 1.6 %edge1.1 = (f32[1,2,2,128,128]{4,3,2,1,0:T(8,128)S(1)}, f32[1,2,2,128,128]{4,3,2,1,0:T(8,128)S(1)}, f32[1,2,2,128,128]{4,3,2,1,0:T(8,128)S(1)}) custom-call(f32[4,256,256]{2,1,0:T(8,128)} %phase_ref.5, f32[4,256,256]{2,1,0:T(8,128)} %absorb_ref.5), custom_call_target="tpu_custom_call" | custom-call | flops 3932160 | bytes 1572864 | tf_op jit(solution)/shard_map/edge1/pallas_call | solution.py:104
  5.3 0.7 %collective-permute-start.1 = (f32[1,2,2,128,128]{4,3,2,1,0:T(8,128)S(1)}, f32[1,2,2,128,128]{4,3,2,1,0:T(8,128)}, u32[]{:S(2)}, u32[]{:S(2)}) collective-permute-start(f32[1,2,2,128,128]{4,3,2,1,0:T(8,128)S(1)} %get-tuple-element.21.refs_4_), channel_id=1, source_target_pairs={{0,7},{1,0},{2,1},{3,2},{4,3},{5,4},{6,5},{7,6},{8,15},{9,8},{10,9... | collective-permute-start | bytes 786440 | tf_op jit(solution)/shard_map/ppermute | solution.py:424
  6.0 0.3 collective-permute-start.2
  6.3 0.6 %collective-permute-start.3 = (f32[1,2,2,128,128]{4,3,2,1,0:T(8,128)S(1)}, f32[1,2,2,128,128]{4,3,2,1,0:T(8,128)S(1)}, u32[]{:S(2)}, u32[]{:S(2)}) collective-permute-start(f32[1,2,2,128,128]{4,3,2,1,0:T(8,128)S(1)} %get-tuple-element.25.refs_4_), channel_id=1, source_target_pairs={{0,7},{1,0},{2,1},{3,2},{4,3},{5,4},{6,5},{7,6},{8,15},{9,8},{10,9... | collective-permute-start | bytes 786440 | tf_op jit(solution)/shard_map/ppermute | solution.py:424
  6.8 0.0 copy-done.7
  6.8 0.0 copy-done.6
  6.8 0.1 dynamic-slice_add_fusion
  6.9 0.1 copy.10
  7.0 0.1 broadcast_in_dim.10
  7.1 0.0 copy-done
  7.1 0.0 copy-done.1
  7.1 0.0 copy-start.2
  7.1 0.0 copy-start.4
  7.1 0.0 copy-start.5
  7.1 0.8 %rest.1.refs_5_ = f32[4,2,2,128,128]{4,3,2,1,0:T(8,128)S(1)} custom-call(f32[4,256,256]{2,1,0:T(8,128)S(1)} %copy-done, f32[4,256,256]{2,1,0:T(8,128)S(1)} %copy-done.1), custom_call_target="tpu_custom_call" | custom-call | flops 5242880 | bytes 2097152 | tf_op jit(solution)/shard_map/rest/pallas_call | solution.py:126
  8.0 0.0 collective-permute-done.refs_6_
  8.0 0.1 broadcast_in_dim.11.refs_0_
  8.1 0.1 copy-done.2
  8.2 0.1 copy-done.4
  8.2 0.1 copy-done.5
  8.3 2.2 %enter0.1 = (f32[4,2,128,128]{3,2,1,0:T(8,128)S(1)}, f32[2,2,384,128]{3,2,1,0:T(8,128)S(1)}) custom-call(s32[24,128]{1,0:T(8,128)S(1)} %broadcast_in_dim.11.refs_0_, f32[4,2,128,128]{3,2,1,0:T(8,128)S(1)} %bitcast.7, bf16[2,256,256]{2,1,0:T(8,128)(2,1)S(1)} %copy-done.5, bf16[2,256,256]{2,1,0:T(8,128)(2,1)S(1)} %copy-done.4, ...), custom_call_target="tpu_custom_call" | custom-call | flops 3221225472 | bytes 786432 | tf_op jit(solution)/shard_map/enter0/pallas_call | solution.py:314
  10.5 0.0 collective-permute-done.1.refs_6_
  10.5 2.1 %enter1.1 = (f32[4,2,128,128]{3,2,1,0:T(8,128)S(1)}, f32[2,2,384,128]{3,2,1,0:T(8,128)S(1)}) custom-call(s32[24,128]{1,0:T(8,128)S(1)} %broadcast_in_dim.11.refs_0_, f32[4,2,128,128]{3,2,1,0:T(8,128)S(1)} %get-tuple-element.20.refs_1_, bf16[2,256,256]{2,1,0:T(8,128)(2,1)S(1)} %copy-done.5, bf16[2,256,256]{2,1,0:T(8,128)(2,1)S(1)} %copy-done.4, ...), custom_call_target="tpu_custom_call" | custom-call | flops 3221225472 | bytes 786432 | tf_op jit(solution)/shard_map/enter1/pallas_call | solution.py:314
  12.6 0.6 %collective-permute-done.2.refs_6_ = f32[1,2,2,128,128]{4,3,2,1,0:T(8,128)} collective-permute-done((f32[1,2,2,128,128]{4,3,2,1,0:T(8,128)S(1)}, f32[1,2,2,128,128]{4,3,2,1,0:T(8,128)}, u32[]{:S(2)}, u32[]{:S(2)}) %collective-permute-start.2) | collective-permute-done | bytes 262176 | tf_op jit(solution)/shard_map/ppermute | solution.py:424
  13.2 2.1 %enter2.1 = (f32[4,2,128,128]{3,2,1,0:T(8,128)S(1)}, f32[2,2,384,128]{3,2,1,0:T(8,128)S(1)}) custom-call(s32[24,128]{1,0:T(8,128)S(1)} %broadcast_in_dim.11.refs_0_, f32[4,2,128,128]{3,2,1,0:T(8,128)S(1)} %get-tuple-element.22.refs_1_, bf16[2,256,256]{2,1,0:T(8,128)(2,1)S(1)} %copy-done.5, bf16[2,256,256]{2,1,0:T(8,128)(2,1)S(1)} %copy-done.4, ...), custom_call_target="tpu_custom_call" | custom-call | flops 3221225472 | bytes 786432 | tf_op jit(solution)/shard_map/enter2/pallas_call | solution.py:314
  15.3 0.7 %collective-permute-done.3.refs_6_ = f32[1,2,2,128,128]{4,3,2,1,0:T(8,128)S(1)} collective-permute-done((f32[1,2,2,128,128]{4,3,2,1,0:T(8,128)S(1)}, f32[1,2,2,128,128]{4,3,2,1,0:T(8,128)S(1)}, u32[]{:S(2)}, u32[]{:S(2)}) %collective-permute-start.3) | collective-permute-done | bytes 262176 | tf_op jit(solution)/shard_map/ppermute | solution.py:424
  16.0 0.8 %leave0.1 = (f32[2,2,128,128]{3,2,1,0:T(8,128)S(1)}, f32[2,2,384,128]{3,2,1,0:T(8,128)S(1)}) custom-call(s32[24,128]{1,0:T(8,128)S(1)} %broadcast_in_dim.11.refs_0_, f32[4,2,128,128]{3,2,1,0:T(8,128)S(1)} %get-tuple-element.24.refs_1_, bf16[2,256,256]{2,1,0:T(8,128)(2,1)S(1)} %copy-done.5, bf16[2,256,256]{2,1,0:T(8,128)(2,1)S(1)} %copy-done.4, ...), custom_call_target="tpu_custom_call" | custom-call | flops 1610612736 | bytes 786432 | tf_op jit(solution)/shard_map/leave0/pallas_call | solution.py:314
  16.8 1.6 %collective-permute-start.6 = (f32[2,2,128,128]{3,2,1,0:T(8,128)S(1)}, f32[2,2,128,128]{3,2,1,0:T(8,128)S(1)}, u32[]{:S(2)}, u32[]{:S(2)}) collective-permute-start(f32[2,2,128,128]{3,2,1,0:T(8,128)S(1)} %get-tuple-element.27.refs_5_.refs_9_), channel_id=1, source_target_pairs={{0,8},{8,16},{16,24},{24,32},{32,40},{40,48},{48,56},{56,64},{64,7... | collective-permute-start | bytes 786440 | tf_op jit(solution)/shard_map/ppermute | solution.py:458
  18.4 0.0 copy-start.3
  18.4 0.8 %leave1.1 = (f32[1,2,128,128]{3,2,1,0:T(8,128)S(1)}, f32[1,2,128,128]{3,2,1,0:T(8,128)S(1)}) custom-call(s32[24,128]{1,0:T(8,128)S(1)} %broadcast_in_dim.11.refs_0_, f32[4,2,128,128]{3,2,1,0:T(8,128)S(1)} %get-tuple-element.24.refs_1_, bf16[2,256,256]{2,1,0:T(8,128)(2,1)S(1)} %copy-done.5, bf16[2,256,256]{2,1,0:T(8,128)(2,1)S(1)} %copy-done.4, ...), custom_call_target="tpu_custom_call" | custom-call | flops 1610612736 | bytes 786432 | tf_op jit(solution)/shard_map/leave1/pallas_call | solution.py:314
  19.2 1.6 %collective-permute-start.5 = (f32[1,2,128,128]{3,2,1,0:T(8,128)S(1)}, f32[1,2,128,128]{3,2,1,0:T(8,128)S(1)}, u32[]{:S(2)}, u32[]{:S(2)}) collective-permute-start(f32[1,2,128,128]{3,2,1,0:T(8,128)S(1)} %get-tuple-element.32.refs_10_), channel_id=1, source_target_pairs={{0,8},{8,16},{16,24},{24,32},{32,40},{40,48},{48,56},{56,64},{64,7... | collective-permute-start | bytes 393224 | tf_op jit(solution)/shard_map/ppermute | solution.py:458
  20.8 1.2 %collective-permute-start.4 = (f32[1,2,128,128]{3,2,1,0:T(8,128)S(1)}, f32[1,2,128,128]{3,2,1,0:T(8,128)S(1)}, u32[]{:S(2)}, u32[]{:S(2)}) collective-permute-start(f32[1,2,128,128]{3,2,1,0:T(8,128)S(1)} %get-tuple-element.28.refs_8_.refs_11_), channel_id=1, source_target_pairs={{0,8},{8,16},{16,24},{24,32},{32,40},{40,48},{48,56},{56,64},{64,7... | collective-permute-start | bytes 393224 | tf_op jit(solution)/shard_map/ppermute | solution.py:458
  22.0 0.0 copy-done.3
  22.0 6.3 %collective-permute-done.6.refs_1_ = f32[2,2,128,128]{3,2,1,0:T(8,128)S(1)} collective-permute-done((f32[2,2,128,128]{3,2,1,0:T(8,128)S(1)}, f32[2,2,128,128]{3,2,1,0:T(8,128)S(1)}, u32[]{:S(2)}, u32[]{:S(2)}) %collective-permute-start.6) | collective-permute-done | bytes 262176 | tf_op jit(solution)/shard_map/ppermute | solution.py:458
  28.3 3.0 %tick1_0.1.refs_9_.refs_12_ = f32[2,2,128,128]{3,2,1,0:T(8,128)S(1)} custom-call(s32[24,128]{1,0:T(8,128)S(1)} %broadcast_in_dim.11.refs_0_, f32[2,2,128,128]{3,2,1,0:T(8,128)S(1)} %collective-permute-done.6.refs_1_, bf16[2,256,256]{2,1,0:T(8,128)(2,1)S(1)} %copy-done.5, bf16[2,256,256]{2,1,0:T(8,128)(2,1)S(1)} %copy-done.4, ...), custom_call_target="tpu_custom_call" | custom-call | flops 6442450944 | bytes 3145728 | tf_op jit(solution)/shard_map/tick1_0/pallas_call | solution.py:314
  31.2 0.1 collective-permute-start.8
  31.3 0.0 collective-permute-done.5.refs_1_
  31.3 2.2 %tick1_2.1.refs_9_.refs_13_ = f32[1,2,128,128]{3,2,1,0:T(8,128)S(1)} custom-call(s32[24,128]{1,0:T(8,128)S(1)} %broadcast_in_dim.11.refs_0_, f32[1,2,128,128]{3,2,1,0:T(8,128)S(1)} %collective-permute-done.5.refs_1_, bf16[2,256,256]{2,1,0:T(8,128)(2,1)S(1)} %copy-done.5, bf16[2,256,256]{2,1,0:T(8,128)(2,1)S(1)} %copy-done.4, ...), custom_call_target="tpu_custom_call" | custom-call | flops 3221225472 | bytes 3145728 | tf_op jit(solution)/shard_map/tick1_2/pallas_call | solution.py:314
  33.6 0.9 %collective-permute-start.9 = (f32[1,2,128,128]{3,2,1,0:T(8,128)S(1)}, f32[1,2,128,128]{3,2,1,0:T(8,128)S(1)}, u32[]{:S(2)}, u32[]{:S(2)}) collective-permute-start(f32[1,2,128,128]{3,2,1,0:T(8,128)S(1)} %tick1_2.1.refs_9_.refs_13_), channel_id=1, source_target_pairs={{0,8},{8,16},{16,24},{24,32},{32,40},{40,48},{48,56},{56,64},{64,7... | collective-permute-start | bytes 393224 | tf_op jit(solution)/shard_map/ppermute | solution.py:458
  34.4 0.0 collective-permute-done.4.refs_1_
  34.4 2.2 %tick1_3.1.refs_8_.refs_14_ = f32[1,2,128,128]{3,2,1,0:T(8,128)S(1)} custom-call(s32[24,128]{1,0:T(8,128)S(1)} %broadcast_in_dim.11.refs_0_, f32[1,2,128,128]{3,2,1,0:T(8,128)S(1)} %collective-permute-done.4.refs_1_, bf16[2,256,256]{2,1,0:T(8,128)(2,1)S(1)} %copy-done.5, bf16[2,256,256]{2,1,0:T(8,128)(2,1)S(1)} %copy-done.4, ...), custom_call_target="tpu_custom_call" | custom-call | flops 3221225472 | bytes 3145728 | tf_op jit(solution)/shard_map/tick1_3/pallas_call | solution.py:314
  36.6 1.4 %collective-permute-start.7 = (f32[1,2,128,128]{3,2,1,0:T(8,128)S(1)}, f32[1,2,128,128]{3,2,1,0:T(8,128)S(1)}, u32[]{:S(2)}, u32[]{:S(2)}) collective-permute-start(f32[1,2,128,128]{3,2,1,0:T(8,128)S(1)} %tick1_3.1.refs_8_.refs_14_), channel_id=1, source_target_pairs={{0,8},{8,16},{16,24},{24,32},{32,40},{40,48},{48,56},{56,64},{64,7... | collective-permute-start | bytes 393224 | tf_op jit(solution)/shard_map/ppermute | solution.py:458
  38.1 3.2 %collective-permute-done.8.refs_1_ = f32[2,2,128,128]{3,2,1,0:T(8,128)S(1)} collective-permute-done((f32[2,2,128,128]{3,2,1,0:T(8,128)S(1)}, f32[2,2,128,128]{3,2,1,0:T(8,128)S(1)}, u32[]{:S(2)}, u32[]{:S(2)}) %collective-permute-start.8) | collective-permute-done | bytes 262176 | tf_op jit(solution)/shard_map/ppermute | solution.py:458
  41.3 3.0 %tick2_0.1 = (f32[2,2,128,128]{3,2,1,0:T(8,128)S(1)}, f32[3,4,2,128,128]{4,3,2,1,0:T(8,128)}) custom-call(s32[24,128]{1,0:T(8,128)S(1)} %broadcast_in_dim.11.refs_0_, f32[2,2,128,128]{3,2,1,0:T(8,128)S(1)} %collective-permute-done.8.refs_1_, bf16[2,256,256]{2,1,0:T(8,128)(2,1)S(1)} %copy-done.5, bf16[2,256,256]{2,1,0:T(8,128)(2,1)S(1)} %copy-done.4, ...), custom_call_target="tpu_custom_call" | custom-call | flops 6442450944 | bytes 3145728 | tf_op jit(solution)/shard_map/tick2_0/pallas_call | solution.py:314
  44.3 0.0 collective-permute-done.9.refs_1_
  44.4 2.2 %tick2_2.1.refs_10_.refs_12_ = f32[1,2,128,128]{3,2,1,0:T(8,128)S(1)} custom-call(s32[24,128]{1,0:T(8,128)S(1)} %broadcast_in_dim.11.refs_0_, f32[1,2,128,128]{3,2,1,0:T(8,128)S(1)} %collective-permute-done.9.refs_1_, bf16[2,256,256]{2,1,0:T(8,128)(2,1)S(1)} %copy-done.5, bf16[2,256,256]{2,1,0:T(8,128)(2,1)S(1)} %copy-done.4, ...), custom_call_target="tpu_custom_call" | custom-call | flops 3221225472 | bytes 3145728 | tf_op jit(solution)/shard_map/tick2_2/pallas_call | solution.py:314
  46.6 0.0 collective-permute-done.7.refs_1_
  46.6 2.9 %tick2_3.1 = f32[3,4,2,128,128]{4,3,2,1,0:T(8,128)} custom-call(s32[24,128]{1,0:T(8,128)S(1)} %broadcast_in_dim.11.refs_0_, f32[1,2,128,128]{3,2,1,0:T(8,128)S(1)} %collective-permute-done.7.refs_1_, bf16[2,256,256]{2,1,0:T(8,128)(2,1)S(1)} %copy-done.5, bf16[2,256,256]{2,1,0:T(8,128)(2,1)S(1)} %copy-done.4, ...), custom_call_target="tpu_custom_call", output_to_operand_aliasing={{}: (11, {})} | custom-call | flops 3221225472 | bytes 3145728 | tf_op jit(solution)/shard_map/tick2_3/pallas_call | solution.py:314
  (3 shorter events, 0.0 us)
Async XLA Ops:
  1.2 5.7 %copy-start.7 = (s32[18,4]{0,1:T(4,128)S(1)}, s32[18,4]{0,1:T(4,128)}, u32[]{:S(2)}) copy-start(s32[18,4]{0,1:T(4,128)} %param.12) | copy-start | bytes 868
  1.2 5.7 %copy-start.6 = (s32[18,4]{0,1:T(4,128)S(1)}, s32[18,4]{0,1:T(4,128)}, u32[]{:S(2)}) copy-start(s32[18,4]{0,1:T(4,128)} %param.13) | copy-start | bytes 868
  1.2 5.9 %copy-start = (f32[4,256,256]{2,1,0:T(8,128)S(1)}, f32[4,256,256]{2,1,0:T(8,128)}, u32[]{:S(2)}) copy-start(f32[4,256,256]{2,1,0:T(8,128)} %phase_ref.5) | copy-start | bytes 3145732
  1.2 5.9 %copy-start.1 = (f32[4,256,256]{2,1,0:T(8,128)S(1)}, f32[4,256,256]{2,1,0:T(8,128)}, u32[]{:S(2)}) copy-start(f32[4,256,256]{2,1,0:T(8,128)} %absorb_ref.5) | copy-start | bytes 3145732
  1.2 6.8 %collective-permute-start = (f32[1,2,2,128,128]{4,3,2,1,0:T(8,128)S(1)}, f32[1,2,2,128,128]{4,3,2,1,0:T(8,128)}, u32[]{:S(2)}, u32[]{:S(2)}) collective-permute-start(f32[1,2,2,128,128]{4,3,2,1,0:T(8,128)S(1)} %edge0.1.refs_4_), channel_id=1, source_target_pairs={{0,7},{1,0},{2,1},{3,2},{4,3},{5,4},{6,5},{7,6},{8,15},{9,8},{10,9... | collective-permute-start | bytes 786440 | tf_op jit(solution)/shard_map/ppermute | solution.py:424
  5.3 5.2 %collective-permute-start.1 = (f32[1,2,2,128,128]{4,3,2,1,0:T(8,128)S(1)}, f32[1,2,2,128,128]{4,3,2,1,0:T(8,128)}, u32[]{:S(2)}, u32[]{:S(2)}) collective-permute-start(f32[1,2,2,128,128]{4,3,2,1,0:T(8,128)S(1)} %get-tuple-element.21.refs_4_), channel_id=1, source_target_pairs={{0,7},{1,0},{2,1},{3,2},{4,3},{5,4},{6,5},{7,6},{8,15},{9,8},{10,9... | collective-permute-start | bytes 786440 | tf_op jit(solution)/shard_map/ppermute | solution.py:424
  6.0 7.2 %collective-permute-start.2 = (f32[1,2,2,128,128]{4,3,2,1,0:T(8,128)S(1)}, f32[1,2,2,128,128]{4,3,2,1,0:T(8,128)}, u32[]{:S(2)}, u32[]{:S(2)}) collective-permute-start(f32[1,2,2,128,128]{4,3,2,1,0:T(8,128)S(1)} %get-tuple-element.23.refs_4_), channel_id=1, source_target_pairs={{0,7},{1,0},{2,1},{3,2},{4,3},{5,4},{6,5},{7,6},{8,15},{9,8},{10,9... | collective-permute-start | bytes 786440 | tf_op jit(solution)/shard_map/ppermute | solution.py:424
  6.3 9.7 %collective-permute-start.3 = (f32[1,2,2,128,128]{4,3,2,1,0:T(8,128)S(1)}, f32[1,2,2,128,128]{4,3,2,1,0:T(8,128)S(1)}, u32[]{:S(2)}, u32[]{:S(2)}) collective-permute-start(f32[1,2,2,128,128]{4,3,2,1,0:T(8,128)S(1)} %get-tuple-element.25.refs_4_), channel_id=1, source_target_pairs={{0,7},{1,0},{2,1},{3,2},{4,3},{5,4},{6,5},{7,6},{8,15},{9,8},{10,9... | collective-permute-start | bytes 786440 | tf_op jit(solution)/shard_map/ppermute | solution.py:424
  7.1 1.0 %copy-start.2 = (f32[1,4,2,128,128]{4,3,2,1,0:T(8,128)S(1)}, f32[1,4,2,128,128]{4,3,2,1,0:T(8,128)}, u32[]{:S(2)}) copy-start(f32[1,4,2,128,128]{4,3,2,1,0:T(8,128)} %param.11) | copy-start | bytes 1572868
  7.1 1.1 %copy-start.4 = (bf16[2,256,256]{2,1,0:T(8,128)(2,1)S(1)}, bf16[2,256,256]{2,1,0:T(8,128)(2,1)}, u32[]{:S(2)}) copy-start(bf16[2,256,256]{2,1,0:T(8,128)(2,1)} %constant.23.clone.refs_3_) | copy-start | bytes 786436
  7.1 1.2 %copy-start.5 = (bf16[2,256,256]{2,1,0:T(8,128)(2,1)S(1)}, bf16[2,256,256]{2,1,0:T(8,128)(2,1)}, u32[]{:S(2)}) copy-start(bf16[2,256,256]{2,1,0:T(8,128)(2,1)} %constant.22.clone.refs_2_) | copy-start | bytes 786436
  16.8 11.4 %collective-permute-start.6 = (f32[2,2,128,128]{3,2,1,0:T(8,128)S(1)}, f32[2,2,128,128]{3,2,1,0:T(8,128)S(1)}, u32[]{:S(2)}, u32[]{:S(2)}) collective-permute-start(f32[2,2,128,128]{3,2,1,0:T(8,128)S(1)} %get-tuple-element.27.refs_5_.refs_9_), channel_id=1, source_target_pairs={{0,8},{8,16},{16,24},{24,32},{32,40},{40,48},{48,56},{56,64},{64,7... | collective-permute-start | bytes 786440 | tf_op jit(solution)/shard_map/ppermute | solution.py:458
  18.4 3.6 %copy-start.3 = (f32[2,128,128]{2,1,0:T(8,128)S(1)}, f32[2,128,128]{2,1,0:T(8,128)}, u32[]{:S(2)}) copy-start(f32[2,128,128]{2,1,0:T(8,128)} %refs_1_.3) | copy-start | bytes 393220
  19.2 12.1 %collective-permute-start.5 = (f32[1,2,128,128]{3,2,1,0:T(8,128)S(1)}, f32[1,2,128,128]{3,2,1,0:T(8,128)S(1)}, u32[]{:S(2)}, u32[]{:S(2)}) collective-permute-start(f32[1,2,128,128]{3,2,1,0:T(8,128)S(1)} %get-tuple-element.32.refs_10_), channel_id=1, source_target_pairs={{0,8},{8,16},{16,24},{24,32},{32,40},{40,48},{48,56},{56,64},{64,7... | collective-permute-start | bytes 393224 | tf_op jit(solution)/shard_map/ppermute | solution.py:458
  20.8 13.7 %collective-permute-start.4 = (f32[1,2,128,128]{3,2,1,0:T(8,128)S(1)}, f32[1,2,128,128]{3,2,1,0:T(8,128)S(1)}, u32[]{:S(2)}, u32[]{:S(2)}) collective-permute-start(f32[1,2,128,128]{3,2,1,0:T(8,128)S(1)} %get-tuple-element.28.refs_8_.refs_11_), channel_id=1, source_target_pairs={{0,8},{8,16},{16,24},{24,32},{32,40},{40,48},{48,56},{56,64},{64,7... | collective-permute-start | bytes 393224 | tf_op jit(solution)/shard_map/ppermute | solution.py:458
  31.2 10.0 %collective-permute-start.8 = (f32[2,2,128,128]{3,2,1,0:T(8,128)S(1)}, f32[2,2,128,128]{3,2,1,0:T(8,128)S(1)}, u32[]{:S(2)}, u32[]{:S(2)}) collective-permute-start(f32[2,2,128,128]{3,2,1,0:T(8,128)S(1)} %tick1_0.1.refs_9_.refs_12_), channel_id=1, source_target_pairs={{0,8},{8,16},{16,24},{24,32},{32,40},{40,48},{48,56},{56,64},{64,7... | collective-permute-start | bytes 786440 | tf_op jit(solution)/shard_map/ppermute | solution.py:458
  33.6 10.8 %collective-permute-start.9 = (f32[1,2,128,128]{3,2,1,0:T(8,128)S(1)}, f32[1,2,128,128]{3,2,1,0:T(8,128)S(1)}, u32[]{:S(2)}, u32[]{:S(2)}) collective-permute-start(f32[1,2,128,128]{3,2,1,0:T(8,128)S(1)} %tick1_2.1.refs_9_.refs_13_), channel_id=1, source_target_pairs={{0,8},{8,16},{16,24},{24,32},{32,40},{40,48},{48,56},{56,64},{64,7... | collective-permute-start | bytes 393224 | tf_op jit(solution)/shard_map/ppermute | solution.py:458
  36.6 9.9 %collective-permute-start.7 = (f32[1,2,128,128]{3,2,1,0:T(8,128)S(1)}, f32[1,2,128,128]{3,2,1,0:T(8,128)S(1)}, u32[]{:S(2)}, u32[]{:S(2)}) collective-permute-start(f32[1,2,128,128]{3,2,1,0:T(8,128)S(1)} %tick1_3.1.refs_8_.refs_14_), channel_id=1, source_target_pairs={{0,8},{8,16},{16,24},{24,32},{32,40},{40,48},{48,56},{56,64},{64,7... | collective-permute-start | bytes 393224 | tf_op jit(solution)/shard_map/ppermute | solution.py:458

commit v7 on v6

--- a/solution.py
+++ b/solution.py
@@ -32,7 +32,10 @@
     high = right.astype(ml_dtypes.bfloat16)
     low = (right - high.astype(np.float64)).astype(ml_dtypes.bfloat16)
     right = np.stack([high, low])
-    return right, np.ascontiguousarray(right.transpose(0, 2, 1))
+    left = right.transpose(0, 2, 1)
+    columns = left[:, :, :size]
+    single = np.concatenate([columns[0], columns[0], columns[1]], 1)
+    return right, left.reshape(4 * size, 2 * size), single
 
 
 def series(z, terms):
@@ -141,7 +144,7 @@
     tick, layers, probes, starts, ends, piece_refs, ext_refs, anchors_ref, waves, put, tables, scratch
 ):
     right_ref, left_ref = tables
-    state, x_high, x_low, r_high, r_low = scratch
+    state, x_all, r_high, r_low = scratch
     size = state.shape[-1]
     each = anchors_ref.shape[0] // (2 * TICKS)
     row_at, col_at = [
@@ -149,7 +152,7 @@
         for axis in range(2)
     ]
     lane = lax.broadcasted_iota(jnp.int32, (size, size), 1)
-    count = len(layers)
+    count, total = len(layers), len(probes) * size
 
     for n in range(len(probes)):
         for part in range(2):
@@ -157,6 +160,14 @@
             if starts:
                 wave = pltpu.roll(wave, col_at[n] & (size - 1), 1)
             state[n, part] = wave
+
+    def leave(n, part, j, wave):
+        if j < count - 1:
+            state[n, part] = wave
+            return
+        if ends:
+            wave = pltpu.roll(wave, (size - col_at[n]) & (size - 1), 1)
+        put(n, part, wave)
 
     for j in range(count):
         ext = ext_refs[j]
@@ -172,32 +183,30 @@
             t_imag = jnp.where(inside, ext[1, 0, at, :], ext[1, 1, at, :])
             real, imag = state[n, 0], state[n, 1]
             rows = slice(n * size, (n + 1) * size)
-            x_high[rows, :size], x_low[rows, :size] = split(real * t_real - imag * t_imag)
-            x_high[rows, size:], x_low[rows, size:] = split(real * t_imag + imag * t_real)
-        y = (
-            product(x_high[...], right_ref[0])
-            + product(x_high[...], right_ref[1])
-            + product(x_low[...], right_ref[0])
-        )
+            lows = slice(total + n * size, total + (n + 1) * size)
+            x_all[rows, :size], x_all[lows, :size] = split(real * t_real - imag * t_imag)
+            x_all[rows, size:], x_all[lows, size:] = split(real * t_imag + imag * t_real)
+        both = product(x_all[...], right_ref[0])
+        y = both[:total] + (both[total:] + product(x_all[:total], right_ref[1]))
+        if len(probes) == 1:
+            high, low = split(y)
+            r_high[:size], r_high[size : 2 * size], r_high[2 * size :] = high, low, high
+            s = product(left_ref[...], r_high[...])
+            parts = (s[:size, :size] - s[size:, size:], s[size:, :size] + s[:size, size:])
+            for part in range(2):
+                leave(0, part, j, parts[part])
+            continue
         for n in range(len(probes)):
             rows = slice(n * size, (n + 1) * size)
             r_high[:size, rows], r_low[:size, rows] = split(y[rows, :size])
             r_high[size:, rows], r_low[size:, rows] = split(y[rows, size:])
-        z = (
-            product(left_ref[0], r_high[...])
-            + product(left_ref[1], r_high[...])
-            + product(left_ref[0], r_low[...])
-        )
+        both = product(left_ref[...], r_high[...])
+        width = 2 * size
+        z = both[:width] + (both[width:] + product(left_ref[:width], r_low[...]))
         for n in range(len(probes)):
             rows = slice(n * size, (n + 1) * size)
             for part in range(2):
-                wave = z[part * size : (part + 1) * size, rows]
-                if j < count - 1:
-                    state[n, part] = wave
-                    continue
-                if ends:
-                    wave = pltpu.roll(wave, (size - col_at[n]) & (size - 1), 1)
-                put(n, part, wave)
+                leave(n, part, j, z[part * size : (part + 1) * size, rows])
 
 
 def take(refs, count):
@@ -304,6 +313,11 @@
     return pl.BlockSpec(memory_space=pltpu.HBM)
 
 
+def pick(tables, n):
+    right, left, single = tables
+    return right, single if n == 1 else left
+
+
 def call(kernel, operands, specs, out_shape, out_specs, n, size, layers, name, **rest):
     grid = rest.pop("grid", (1,))
     flops = WEIGHT * grid[0] * layers * n * 2 * 3 * 2 * size * (2 * size) ** 2
@@ -319,9 +333,8 @@
         out_shape=out_shape,
         scratch_shapes=[
             pltpu.VMEM((n, 2, size, size), jnp.float32),
-            pltpu.VMEM((n * size, 2 * size), jnp.bfloat16),
-            pltpu.VMEM((n * size, 2 * size), jnp.bfloat16),
-            pltpu.VMEM((2 * size, n * size), jnp.bfloat16),
+            pltpu.VMEM((2 * n * size, 2 * size), jnp.bfloat16),
+            pltpu.VMEM((3 * size, 2 * size) if n == 1 else (2 * size, n * size), jnp.bfloat16),
             pltpu.VMEM((2 * size, n * size), jnp.bfloat16),
             *rest.pop("scratch", []),
         ],
@@ -340,7 +353,7 @@
     size = wave.shape[-1]
     count, n = len(layers), sum(map(len, groups))
     base = groups[0][0] if wave.shape[0] != n else 0
-    operands = [anchors, wave, *tables]
+    operands = [anchors, wave, *pick(tables, n)]
     specs = [vmem()] * 4
     out_shape = [
         jax.ShapeDtypeStruct((len(group), 2, size, size), jnp.float32) for group in groups
@@ -371,7 +384,7 @@
     layers = list(range(len(exts)))
     return call(
         functools.partial(first_kernel, tick, layers),
-        [anchors, probe_wave, *tables, *exts, after],
+        [anchors, probe_wave, *pick(tables, n), *exts, after],
         [vmem()] * (4 + len(exts)) + [pl.BlockSpec(memory_space=pl.ANY)],
         jax.ShapeDtypeStruct((chunks * n, 2, size, size), jnp.float32),
         pl.BlockSpec((n, 2, size, size), lambda i: (i, 0, 0, 0)),
@@ -384,7 +397,7 @@
 ):
     size = wave.shape[-1]
     count, n = len(exts), len(probes)
-    operands = [anchors, wave, *tables, *exts, first, *(part for _, part in stored)]
+    operands = [anchors, wave, *pick(tables, n), *exts, first, *(part for _, part in stored)]
     specs = [vmem()] * (5 + count + len(stored))
     shape = [jax.ShapeDtypeStruct((n, 2, size, size), jnp.float32)]
     out_specs = [vmem()]

time: 50 us -> 49.7 us (level)
  Pallas kernels: 27.1 us -> 26.6 us
  transfers between devices with their start and end apart: 10 -> 10, of which waited for: 4 -> 4; matrix products, arithmetic and copies ran while one was open for 1% -> 1% of each run, Pallas kernels for 45% -> 44%
where the time goes in v7:
time: 49.7 us; the launch traced here: 49.4 us
  Pallas kernels  26.6 us (54%)
  waiting for transfers between devices  11 us (22%)
  starting transfers between devices  10.8 us (22%)
  local copies, waits for them, and re-layouts  0.54 us (1%)
    pallas_call x13, Pallas kernels, call(): pl.pallas_call(kernel, grid=grid, in_specs=specs, out_specs=out_specs, ou...  23.1 us
    ppermute x6, waiting for transfers between devices, shards(): arrived = [lax.ppermute(left, 'depth', onward) for left in done]  9.66 us
    ppermute x6, starting transfers between devices, shards(): arrived = [lax.ppermute(left, 'depth', onward) for left in done]  6.76 us
    ppermute x4, starting transfers between devices, shards(): rims = [lax.ppermute(first, 'tile', back) for first in firsts]  4.01 us
    pallas_call x2, Pallas kernels, edge_rows(): pl.pallas_call(functools.partial(edge_kernel, layers[0]), out_shape=[shap...  2.75 us
    ppermute x4, waiting for transfers between devices, shards(): rims = [lax.ppermute(first, 'tile', back) for first in firsts]  1.35 us
  transfers between devices with their start and end apart: 10, of which 4 were waited for; matrix products, arithmetic and copies ran while one was open for 1% of the time, Pallas kernels for 44%

profile of v7, /device:TPU:96, one launch (start us, length us, event | category | flops | bytes accessed | tf_op | source)
XLA Modules:
  0.0 49.4 jit_solution(8029143852846355361)
XLA Ops:
  0.0 1.2 %edge0.1.refs_4_ = f32[1,2,2,128,128]{4,3,2,1,0:T(8,128)S(1)} custom-call(f32[4,256,256]{2,1,0:T(8,128)} %phase_ref.5, f32[4,256,256]{2,1,0:T(8,128)} %absorb_ref.5), custom_call_target="tpu_custom_call" | custom-call | flops 1310720 | bytes 524288 | tf_op jit(solution)/shard_map/edge0/pallas_call | solution.py:107
  1.2 0.0 copy-start.8
  1.2 0.0 copy-start.7
  1.2 0.0 copy-start
  1.2 0.0 copy-start.1
  1.2 2.5 %collective-permute-start = (f32[1,2,2,128,128]{4,3,2,1,0:T(8,128)S(1)}, f32[1,2,2,128,128]{4,3,2,1,0:T(8,128)}, u32[]{:S(2)}, u32[]{:S(2)}) collective-permute-start(f32[1,2,2,128,128]{4,3,2,1,0:T(8,128)S(1)} %edge0.1.refs_4_), channel_id=1, source_target_pairs={{0,7},{1,0},{2,1},{3,2},{4,3},{5,4},{6,5},{7,6},{8,15},{9,8},{10,9... | collective-permute-start | bytes 786440 | tf_op jit(solution)/shard_map/ppermute | solution.py:437
  3.7 1.6 %edge1.1 = (f32[1,2,2,128,128]{4,3,2,1,0:T(8,128)S(1)}, f32[1,2,2,128,128]{4,3,2,1,0:T(8,128)S(1)}, f32[1,2,2,128,128]{4,3,2,1,0:T(8,128)S(1)}) custom-call(f32[4,256,256]{2,1,0:T(8,128)} %phase_ref.5, f32[4,256,256]{2,1,0:T(8,128)} %absorb_ref.5), custom_call_target="tpu_custom_call" | custom-call | flops 3932160 | bytes 1572864 | tf_op jit(solution)/shard_map/edge1/pallas_call | solution.py:107
  5.3 0.7 %collective-permute-start.1 = (f32[1,2,2,128,128]{4,3,2,1,0:T(8,128)S(1)}, f32[1,2,2,128,128]{4,3,2,1,0:T(8,128)}, u32[]{:S(2)}, u32[]{:S(2)}) collective-permute-start(f32[1,2,2,128,128]{4,3,2,1,0:T(8,128)S(1)} %get-tuple-element.21.refs_4_), channel_id=1, source_target_pairs={{0,7},{1,0},{2,1},{3,2},{4,3},{5,4},{6,5},{7,6},{8,15},{9,8},{10,9... | collective-permute-start | bytes 786440 | tf_op jit(solution)/shard_map/ppermute | solution.py:437
  6.0 0.3 collective-permute-start.2
  6.3 0.6 %collective-permute-start.3 = (f32[1,2,2,128,128]{4,3,2,1,0:T(8,128)S(1)}, f32[1,2,2,128,128]{4,3,2,1,0:T(8,128)S(1)}, u32[]{:S(2)}, u32[]{:S(2)}) collective-permute-start(f32[1,2,2,128,128]{4,3,2,1,0:T(8,128)S(1)} %get-tuple-element.25.refs_4_), channel_id=1, source_target_pairs={{0,7},{1,0},{2,1},{3,2},{4,3},{5,4},{6,5},{7,6},{8,15},{9,8},{10,9... | collective-permute-start | bytes 786440 | tf_op jit(solution)/shard_map/ppermute | solution.py:437
  6.8 0.0 copy-done.8
  6.8 0.0 copy-done.7
  6.8 0.1 dynamic-slice_add_fusion
  6.9 0.1 copy.11
  7.0 0.1 broadcast_in_dim.10
  7.1 0.0 copy-done
  7.1 0.0 copy-done.1
  7.1 0.0 copy-start.2
  7.1 0.0 copy-start.4
  7.1 0.0 copy-start.5
  7.1 0.8 %rest.1.refs_5_ = f32[4,2,2,128,128]{4,3,2,1,0:T(8,128)S(1)} custom-call(f32[4,256,256]{2,1,0:T(8,128)S(1)} %copy-done, f32[4,256,256]{2,1,0:T(8,128)S(1)} %copy-done.1), custom_call_target="tpu_custom_call" | custom-call | flops 5242880 | bytes 2097152 | tf_op jit(solution)/shard_map/rest/pallas_call | solution.py:129
  8.0 0.0 collective-permute-done.refs_6_
  8.0 0.1 broadcast_in_dim.11.refs_0_
  8.1 0.1 copy-done.2
  8.2 0.1 copy-done.4
  8.2 0.1 copy-done.5
  8.3 2.2 %enter0.1 = (f32[4,2,128,128]{3,2,1,0:T(8,128)S(1)}, f32[2,2,384,128]{3,2,1,0:T(8,128)S(1)}) custom-call(s32[24,128]{1,0:T(8,128)S(1)} %broadcast_in_dim.11.refs_0_, f32[4,2,128,128]{3,2,1,0:T(8,128)S(1)} %bitcast.7, bf16[2,256,256]{2,1,0:T(8,128)(2,1)S(1)} %copy-done.4, bf16[512,256]{1,0:T(8,128)(2,1)S(1)} %copy-done.5, ...), custom_call_target="tpu_custom_call" | custom-call | flops 3221225472 | bytes 786432 | tf_op jit(solution)/shard_map/enter0/pallas_call | solution.py:328
  10.5 0.0 collective-permute-done.1.refs_6_
  10.5 2.1 %enter1.1 = (f32[4,2,128,128]{3,2,1,0:T(8,128)S(1)}, f32[2,2,384,128]{3,2,1,0:T(8,128)S(1)}) custom-call(s32[24,128]{1,0:T(8,128)S(1)} %broadcast_in_dim.11.refs_0_, f32[4,2,128,128]{3,2,1,0:T(8,128)S(1)} %get-tuple-element.20.refs_1_, bf16[2,256,256]{2,1,0:T(8,128)(2,1)S(1)} %copy-done.4, bf16[512,256]{1,0:T(8,128)(2,1)S(1)} %copy-done.5, ...), custom_call_target="tpu_custom_call" | custom-call | flops 3221225472 | bytes 786432 | tf_op jit(solution)/shard_map/enter1/pallas_call | solution.py:328
  12.6 0.6 %collective-permute-done.2.refs_6_ = f32[1,2,2,128,128]{4,3,2,1,0:T(8,128)} collective-permute-done((f32[1,2,2,128,128]{4,3,2,1,0:T(8,128)S(1)}, f32[1,2,2,128,128]{4,3,2,1,0:T(8,128)}, u32[]{:S(2)}, u32[]{:S(2)}) %collective-permute-start.2) | collective-permute-done | bytes 262176 | tf_op jit(solution)/shard_map/ppermute | solution.py:437
  13.2 2.1 %enter2.1 = (f32[4,2,128,128]{3,2,1,0:T(8,128)S(1)}, f32[2,2,384,128]{3,2,1,0:T(8,128)S(1)}) custom-call(s32[24,128]{1,0:T(8,128)S(1)} %broadcast_in_dim.11.refs_0_, f32[4,2,128,128]{3,2,1,0:T(8,128)S(1)} %get-tuple-element.22.refs_1_, bf16[2,256,256]{2,1,0:T(8,128)(2,1)S(1)} %copy-done.4, bf16[512,256]{1,0:T(8,128)(2,1)S(1)} %copy-done.5, ...), custom_call_target="tpu_custom_call" | custom-call | flops 3221225472 | bytes 786432 | tf_op jit(solution)/shard_map/enter2/pallas_call | solution.py:328
  15.3 0.7 %collective-permute-done.3.refs_6_ = f32[1,2,2,128,128]{4,3,2,1,0:T(8,128)S(1)} collective-permute-done((f32[1,2,2,128,128]{4,3,2,1,0:T(8,128)S(1)}, f32[1,2,2,128,128]{4,3,2,1,0:T(8,128)S(1)}, u32[]{:S(2)}, u32[]{:S(2)}) %collective-permute-start.3) | collective-permute-done | bytes 262176 | tf_op jit(solution)/shard_map/ppermute | solution.py:437
  16.0 0.8 %leave0.1 = (f32[2,2,128,128]{3,2,1,0:T(8,128)S(1)}, f32[2,2,384,128]{3,2,1,0:T(8,128)S(1)}) custom-call(s32[24,128]{1,0:T(8,128)S(1)} %broadcast_in_dim.11.refs_0_, f32[4,2,128,128]{3,2,1,0:T(8,128)S(1)} %get-tuple-element.24.refs_1_, bf16[2,256,256]{2,1,0:T(8,128)(2,1)S(1)} %copy-done.4, bf16[512,256]{1,0:T(8,128)(2,1)S(1)} %copy-done.5, ...), custom_call_target="tpu_custom_call" | custom-call | flops 1610612736 | bytes 786432 | tf_op jit(solution)/shard_map/leave0/pallas_call | solution.py:328
  16.8 1.6 %collective-permute-start.6 = (f32[2,2,128,128]{3,2,1,0:T(8,128)S(1)}, f32[2,2,128,128]{3,2,1,0:T(8,128)S(1)}, u32[]{:S(2)}, u32[]{:S(2)}) collective-permute-start(f32[2,2,128,128]{3,2,1,0:T(8,128)S(1)} %get-tuple-element.27.refs_5_.refs_9_), channel_id=1, source_target_pairs={{0,8},{8,16},{16,24},{24,32},{32,40},{40,48},{48,56},{56,64},{64,7... | collective-permute-start | bytes 786440 | tf_op jit(solution)/shard_map/ppermute | solution.py:471
  18.4 0.0 copy-start.3
  18.4 0.8 %leave1.1 = (f32[1,2,128,128]{3,2,1,0:T(8,128)S(1)}, f32[1,2,128,128]{3,2,1,0:T(8,128)S(1)}) custom-call(s32[24,128]{1,0:T(8,128)S(1)} %broadcast_in_dim.11.refs_0_, f32[4,2,128,128]{3,2,1,0:T(8,128)S(1)} %get-tuple-element.24.refs_1_, bf16[2,256,256]{2,1,0:T(8,128)(2,1)S(1)} %copy-done.4, bf16[512,256]{1,0:T(8,128)(2,1)S(1)} %copy-done.5, ...), custom_call_target="tpu_custom_call" | custom-call | flops 1610612736 | bytes 786432 | tf_op jit(solution)/shard_map/leave1/pallas_call | solution.py:328
  19.2 1.6 %collective-permute-start.5 = (f32[1,2,128,128]{3,2,1,0:T(8,128)S(1)}, f32[1,2,128,128]{3,2,1,0:T(8,128)S(1)}, u32[]{:S(2)}, u32[]{:S(2)}) collective-permute-start(f32[1,2,128,128]{3,2,1,0:T(8,128)S(1)} %get-tuple-element.32.refs_10_), channel_id=1, source_target_pairs={{0,8},{8,16},{16,24},{24,32},{32,40},{40,48},{48,56},{56,64},{64,7... | collective-permute-start | bytes 393224 | tf_op jit(solution)/shard_map/ppermute | solution.py:471
  20.8 1.2 %collective-permute-start.4 = (f32[1,2,128,128]{3,2,1,0:T(8,128)S(1)}, f32[1,2,128,128]{3,2,1,0:T(8,128)S(1)}, u32[]{:S(2)}, u32[]{:S(2)}) collective-permute-start(f32[1,2,128,128]{3,2,1,0:T(8,128)S(1)} %get-tuple-element.28.refs_8_.refs_11_), channel_id=1, source_target_pairs={{0,8},{8,16},{16,24},{24,32},{32,40},{40,48},{48,56},{56,64},{64,7... | collective-permute-start | bytes 393224 | tf_op jit(solution)/shard_map/ppermute | solution.py:471
  22.0 0.0 copy-done.3
  22.0 0.0 copy-start.6
  22.0 6.3 %collective-permute-done.6.refs_1_ = f32[2,2,128,128]{3,2,1,0:T(8,128)S(1)} collective-permute-done((f32[2,2,128,128]{3,2,1,0:T(8,128)S(1)}, f32[2,2,128,128]{3,2,1,0:T(8,128)S(1)}, u32[]{:S(2)}, u32[]{:S(2)}) %collective-permute-start.6) | collective-permute-done | bytes 262176 | tf_op jit(solution)/shard_map/ppermute | solution.py:471
  28.3 3.0 %tick1_0.1.refs_9_.refs_12_ = f32[2,2,128,128]{3,2,1,0:T(8,128)S(1)} custom-call(s32[24,128]{1,0:T(8,128)S(1)} %broadcast_in_dim.11.refs_0_, f32[2,2,128,128]{3,2,1,0:T(8,128)S(1)} %collective-permute-done.6.refs_1_, bf16[2,256,256]{2,1,0:T(8,128)(2,1)S(1)} %copy-done.4, bf16[512,256]{1,0:T(8,128)(2,1)S(1)} %copy-done.5, ...), custom_call_target="tpu_custom_call" | custom-call | flops 6442450944 | bytes 3145728 | tf_op jit(solution)/shard_map/tick1_0/pallas_call | solution.py:328
  31.2 0.1 collective-permute-start.8
  31.3 0.0 collective-permute-done.5.refs_1_
  31.3 0.0 copy-done.6
  31.3 2.1 %tick1_2.1.refs_9_.refs_13_ = f32[1,2,128,128]{3,2,1,0:T(8,128)S(1)} custom-call(s32[24,128]{1,0:T(8,128)S(1)} %broadcast_in_dim.11.refs_0_, f32[1,2,128,128]{3,2,1,0:T(8,128)S(1)} %collective-permute-done.5.refs_1_, bf16[2,256,256]{2,1,0:T(8,128)(2,1)S(1)} %copy-done.4, bf16[256,384]{1,0:T(8,128)(2,1)S(1)} %copy-done.6, ...), custom_call_target="tpu_custom_call" | custom-call | flops 3221225472 | bytes 3145728 | tf_op jit(solution)/shard_map/tick1_2/pallas_call | solution.py:328
  33.5 0.9 %collective-permute-start.9 = (f32[1,2,128,128]{3,2,1,0:T(8,128)S(1)}, f32[1,2,128,128]{3,2,1,0:T(8,128)S(1)}, u32[]{:S(2)}, u32[]{:S(2)}) collective-permute-start(f32[1,2,128,128]{3,2,1,0:T(8,128)S(1)} %tick1_2.1.refs_9_.refs_13_), channel_id=1, source_target_pairs={{0,8},{8,16},{16,24},{24,32},{32,40},{40,48},{48,56},{56,64},{64,7... | collective-permute-start | bytes 393224 | tf_op jit(solution)/shard_map/ppermute | solution.py:471
  34.3 0.0 collective-permute-done.4.refs_1_
  34.3 2.1 %tick1_3.1.refs_8_.refs_14_ = f32[1,2,128,128]{3,2,1,0:T(8,128)S(1)} custom-call(s32[24,128]{1,0:T(8,128)S(1)} %broadcast_in_dim.11.refs_0_, f32[1,2,128,128]{3,2,1,0:T(8,128)S(1)} %collective-permute-done.4.refs_1_, bf16[2,256,256]{2,1,0:T(8,128)(2,1)S(1)} %copy-done.4, bf16[256,384]{1,0:T(8,128)(2,1)S(1)} %copy-done.6, ...), custom_call_target="tpu_custom_call" | custom-call | flops 3221225472 | bytes 3145728 | tf_op jit(solution)/shard_map/tick1_3/pallas_call | solution.py:328
  36.4 1.5 %collective-permute-start.7 = (f32[1,2,128,128]{3,2,1,0:T(8,128)S(1)}, f32[1,2,128,128]{3,2,1,0:T(8,128)S(1)}, u32[]{:S(2)}, u32[]{:S(2)}) collective-permute-start(f32[1,2,128,128]{3,2,1,0:T(8,128)S(1)} %tick1_3.1.refs_8_.refs_14_), channel_id=1, source_target_pairs={{0,8},{8,16},{16,24},{24,32},{32,40},{40,48},{48,56},{56,64},{64,7... | collective-permute-start | bytes 393224 | tf_op jit(solution)/shard_map/ppermute | solution.py:471
  37.9 3.4 %collective-permute-done.8.refs_1_ = f32[2,2,128,128]{3,2,1,0:T(8,128)S(1)} collective-permute-done((f32[2,2,128,128]{3,2,1,0:T(8,128)S(1)}, f32[2,2,128,128]{3,2,1,0:T(8,128)S(1)}, u32[]{:S(2)}, u32[]{:S(2)}) %collective-permute-start.8) | collective-permute-done | bytes 262176 | tf_op jit(solution)/shard_map/ppermute | solution.py:471
  41.3 3.0 %tick2_0.1 = (f32[2,2,128,128]{3,2,1,0:T(8,128)S(1)}, f32[3,4,2,128,128]{4,3,2,1,0:T(8,128)}) custom-call(s32[24,128]{1,0:T(8,128)S(1)} %broadcast_in_dim.11.refs_0_, f32[2,2,128,128]{3,2,1,0:T(8,128)S(1)} %collective-permute-done.8.refs_1_, bf16[2,256,256]{2,1,0:T(8,128)(2,1)S(1)} %copy-done.4, bf16[512,256]{1,0:T(8,128)(2,1)S(1)} %copy-done.5, ...), custom_call_target="tpu_custom_call" | custom-call | flops 6442450944 | bytes 3145728 | tf_op jit(solution)/shard_map/tick2_0/pallas_call | solution.py:328
  44.3 0.0 collective-permute-done.9.refs_1_
  44.3 2.1 %tick2_2.1.refs_10_.refs_12_ = f32[1,2,128,128]{3,2,1,0:T(8,128)S(1)} custom-call(s32[24,128]{1,0:T(8,128)S(1)} %broadcast_in_dim.11.refs_0_, f32[1,2,128,128]{3,2,1,0:T(8,128)S(1)} %collective-permute-done.9.refs_1_, bf16[2,256,256]{2,1,0:T(8,128)(2,1)S(1)} %copy-done.4, bf16[256,384]{1,0:T(8,128)(2,1)S(1)} %copy-done.6, ...), custom_call_target="tpu_custom_call" | custom-call | flops 3221225472 | bytes 3145728 | tf_op jit(solution)/shard_map/tick2_2/pallas_call | solution.py:328
  46.5 0.0 collective-permute-done.7.refs_1_
  46.5 2.8 %tick2_3.1 = f32[3,4,2,128,128]{4,3,2,1,0:T(8,128)} custom-call(s32[24,128]{1,0:T(8,128)S(1)} %broadcast_in_dim.11.refs_0_, f32[1,2,128,128]{3,2,1,0:T(8,128)S(1)} %collective-permute-done.7.refs_1_, bf16[2,256,256]{2,1,0:T(8,128)(2,1)S(1)} %copy-done.4, bf16[256,384]{1,0:T(8,128)(2,1)S(1)} %copy-done.6, ...), custom_call_target="tpu_custom_call", output_to_operand_aliasing={{}: (11, {})} | custom-call | flops 3221225472 | bytes 3145728 | tf_op jit(solution)/shard_map/tick2_3/pallas_call | solution.py:328
  (3 shorter events, 0.0 us)
Async XLA Ops:
  1.2 5.7 %copy-start.8 = (s32[18,4]{0,1:T(4,128)S(1)}, s32[18,4]{0,1:T(4,128)}, u32[]{:S(2)}) copy-start(s32[18,4]{0,1:T(4,128)} %param.13) | copy-start | bytes 868
  1.2 5.7 %copy-start.7 = (s32[18,4]{0,1:T(4,128)S(1)}, s32[18,4]{0,1:T(4,128)}, u32[]{:S(2)}) copy-start(s32[18,4]{0,1:T(4,128)} %param.14) | copy-start | bytes 868
  1.2 5.9 %copy-start = (f32[4,256,256]{2,1,0:T(8,128)S(1)}, f32[4,256,256]{2,1,0:T(8,128)}, u32[]{:S(2)}) copy-start(f32[4,256,256]{2,1,0:T(8,128)} %phase_ref.5) | copy-start | bytes 3145732
  1.2 5.9 %copy-start.1 = (f32[4,256,256]{2,1,0:T(8,128)S(1)}, f32[4,256,256]{2,1,0:T(8,128)}, u32[]{:S(2)}) copy-start(f32[4,256,256]{2,1,0:T(8,128)} %absorb_ref.5) | copy-start | bytes 3145732
  1.2 6.8 %collective-permute-start = (f32[1,2,2,128,128]{4,3,2,1,0:T(8,128)S(1)}, f32[1,2,2,128,128]{4,3,2,1,0:T(8,128)}, u32[]{:S(2)}, u32[]{:S(2)}) collective-permute-start(f32[1,2,2,128,128]{4,3,2,1,0:T(8,128)S(1)} %edge0.1.refs_4_), channel_id=1, source_target_pairs={{0,7},{1,0},{2,1},{3,2},{4,3},{5,4},{6,5},{7,6},{8,15},{9,8},{10,9... | collective-permute-start | bytes 786440 | tf_op jit(solution)/shard_map/ppermute | solution.py:437
  5.3 5.2 %collective-permute-start.1 = (f32[1,2,2,128,128]{4,3,2,1,0:T(8,128)S(1)}, f32[1,2,2,128,128]{4,3,2,1,0:T(8,128)}, u32[]{:S(2)}, u32[]{:S(2)}) collective-permute-start(f32[1,2,2,128,128]{4,3,2,1,0:T(8,128)S(1)} %get-tuple-element.21.refs_4_), channel_id=1, source_target_pairs={{0,7},{1,0},{2,1},{3,2},{4,3},{5,4},{6,5},{7,6},{8,15},{9,8},{10,9... | collective-permute-start | bytes 786440 | tf_op jit(solution)/shard_map/ppermute | solution.py:437
  6.0 7.2 %collective-permute-start.2 = (f32[1,2,2,128,128]{4,3,2,1,0:T(8,128)S(1)}, f32[1,2,2,128,128]{4,3,2,1,0:T(8,128)}, u32[]{:S(2)}, u32[]{:S(2)}) collective-permute-start(f32[1,2,2,128,128]{4,3,2,1,0:T(8,128)S(1)} %get-tuple-element.23.refs_4_), channel_id=1, source_target_pairs={{0,7},{1,0},{2,1},{3,2},{4,3},{5,4},{6,5},{7,6},{8,15},{9,8},{10,9... | collective-permute-start | bytes 786440 | tf_op jit(solution)/shard_map/ppermute | solution.py:437
  6.3 9.7 %collective-permute-start.3 = (f32[1,2,2,128,128]{4,3,2,1,0:T(8,128)S(1)}, f32[1,2,2,128,128]{4,3,2,1,0:T(8,128)S(1)}, u32[]{:S(2)}, u32[]{:S(2)}) collective-permute-start(f32[1,2,2,128,128]{4,3,2,1,0:T(8,128)S(1)} %get-tuple-element.25.refs_4_), channel_id=1, source_target_pairs={{0,7},{1,0},{2,1},{3,2},{4,3},{5,4},{6,5},{7,6},{8,15},{9,8},{10,9... | collective-permute-start | bytes 786440 | tf_op jit(solution)/shard_map/ppermute | solution.py:437
  7.1 1.0 %copy-start.2 = (f32[1,4,2,128,128]{4,3,2,1,0:T(8,128)S(1)}, f32[1,4,2,128,128]{4,3,2,1,0:T(8,128)}, u32[]{:S(2)}) copy-start(f32[1,4,2,128,128]{4,3,2,1,0:T(8,128)} %param.12) | copy-start | bytes 1572868
  7.1 1.1 %copy-start.4 = (bf16[2,256,256]{2,1,0:T(8,128)(2,1)S(1)}, bf16[2,256,256]{2,1,0:T(8,128)(2,1)}, u32[]{:S(2)}) copy-start(bf16[2,256,256]{2,1,0:T(8,128)(2,1)} %constant.24.clone.refs_2_) | copy-start | bytes 786436
  7.1 1.2 %copy-start.5 = (bf16[512,256]{1,0:T(8,128)(2,1)S(1)}, bf16[512,256]{1,0:T(8,128)(2,1)}, u32[]{:S(2)}) copy-start(bf16[512,256]{1,0:T(8,128)(2,1)} %constant.25.clone.refs_3_) | copy-start | bytes 786436
  16.8 11.4 %collective-permute-start.6 = (f32[2,2,128,128]{3,2,1,0:T(8,128)S(1)}, f32[2,2,128,128]{3,2,1,0:T(8,128)S(1)}, u32[]{:S(2)}, u32[]{:S(2)}) collective-permute-start(f32[2,2,128,128]{3,2,1,0:T(8,128)S(1)} %get-tuple-element.27.refs_5_.refs_9_), channel_id=1, source_target_pairs={{0,8},{8,16},{16,24},{24,32},{32,40},{40,48},{48,56},{56,64},{64,7... | collective-permute-start | bytes 786440 | tf_op jit(solution)/shard_map/ppermute | solution.py:471
  18.4 3.6 %copy-start.3 = (f32[2,128,128]{2,1,0:T(8,128)S(1)}, f32[2,128,128]{2,1,0:T(8,128)}, u32[]{:S(2)}) copy-start(f32[2,128,128]{2,1,0:T(8,128)} %refs_1_.3) | copy-start | bytes 393220
  19.2 12.1 %collective-permute-start.5 = (f32[1,2,128,128]{3,2,1,0:T(8,128)S(1)}, f32[1,2,128,128]{3,2,1,0:T(8,128)S(1)}, u32[]{:S(2)}, u32[]{:S(2)}) collective-permute-start(f32[1,2,128,128]{3,2,1,0:T(8,128)S(1)} %get-tuple-element.32.refs_10_), channel_id=1, source_target_pairs={{0,8},{8,16},{16,24},{24,32},{32,40},{40,48},{48,56},{56,64},{64,7... | collective-permute-start | bytes 393224 | tf_op jit(solution)/shard_map/ppermute | solution.py:471
  20.8 13.6 %collective-permute-start.4 = (f32[1,2,128,128]{3,2,1,0:T(8,128)S(1)}, f32[1,2,128,128]{3,2,1,0:T(8,128)S(1)}, u32[]{:S(2)}, u32[]{:S(2)}) collective-permute-start(f32[1,2,128,128]{3,2,1,0:T(8,128)S(1)} %get-tuple-element.28.refs_8_.refs_11_), channel_id=1, source_target_pairs={{0,8},{8,16},{16,24},{24,32},{32,40},{40,48},{48,56},{56,64},{64,7... | collective-permute-start | bytes 393224 | tf_op jit(solution)/shard_map/ppermute | solution.py:471
  22.0 9.3 %copy-start.6 = (bf16[256,384]{1,0:T(8,128)(2,1)S(1)}, bf16[256,384]{1,0:T(8,128)(2,1)}, u32[]{:S(2)}) copy-start(bf16[256,384]{1,0:T(8,128)(2,1)} %constant.26.clone.refs_3_) | copy-start | bytes 589828
  31.2 10.0 %collective-permute-start.8 = (f32[2,2,128,128]{3,2,1,0:T(8,128)S(1)}, f32[2,2,128,128]{3,2,1,0:T(8,128)S(1)}, u32[]{:S(2)}, u32[]{:S(2)}) collective-permute-start(f32[2,2,128,128]{3,2,1,0:T(8,128)S(1)} %tick1_0.1.refs_9_.refs_12_), channel_id=1, source_target_pairs={{0,8},{8,16},{16,24},{24,32},{32,40},{40,48},{48,56},{56,64},{64,7... | collective-permute-start | bytes 786440 | tf_op jit(solution)/shard_map/ppermute | solution.py:471
  33.5 10.9 %collective-permute-start.9 = (f32[1,2,128,128]{3,2,1,0:T(8,128)S(1)}, f32[1,2,128,128]{3,2,1,0:T(8,128)S(1)}, u32[]{:S(2)}, u32[]{:S(2)}) collective-permute-start(f32[1,2,128,128]{3,2,1,0:T(8,128)S(1)} %tick1_2.1.refs_9_.refs_13_), channel_id=1, source_target_pairs={{0,8},{8,16},{16,24},{24,32},{32,40},{40,48},{48,56},{56,64},{64,7... | collective-permute-start | bytes 393224 | tf_op jit(solution)/shard_map/ppermute | solution.py:471
  36.4 10.0 %collective-permute-start.7 = (f32[1,2,128,128]{3,2,1,0:T(8,128)S(1)}, f32[1,2,128,128]{3,2,1,0:T(8,128)S(1)}, u32[]{:S(2)}, u32[]{:S(2)}) collective-permute-start(f32[1,2,128,128]{3,2,1,0:T(8,128)S(1)} %tick1_3.1.refs_8_.refs_14_), channel_id=1, source_target_pairs={{0,8},{8,16},{16,24},{24,32},{32,40},{40,48},{48,56},{56,64},{64,7... | collective-permute-start | bytes 393224 | tf_op jit(solution)/shard_map/ppermute | solution.py:471

commit v8 on v7

--- a/solution.py
+++ b/solution.py
@@ -432,8 +432,7 @@
     back = [(i, (i - 1) % tiles) for i in range(tiles)]
     onward = [(i, (i + 1) % depth_count) for i in range(depth_count)]
 
-    firsts = edge_rows(phase_map, absorb, size, [0])
-    firsts += edge_rows(phase_map, absorb, size, list(range(1, slices)))
+    firsts = edge_rows(phase_map, absorb, size, list(range(slices)))
     rims = [lax.ppermute(first, "tile", back) for first in firsts]
     rest = rest_rows(phase_map, absorb, size)
 

time: 49.7 us -> 51.2 us (1.030)
  waiting for transfers between devices: 11 us -> 14 us
  Pallas kernels: 26.6 us -> 25.7 us
    ppermute x4, waiting for transfers between devices: 1.35 us -> 4.27 us  [shards(): rims = [lax.ppermute(first, 'tile', back) for first in firsts]]
    pallas_call x13, Pallas kernels: 23.1 us -> 22.2 us  [call(): pl.pallas_call(kernel, grid=grid, in_specs=specs, out_specs=out_specs, ou...]
    pallas_call x2 -> x1, Pallas kernels: 2.75 us -> 2.6 us  [edge_rows(): pl.pallas_call(functools.partial(edge_kernel, layers[0]), out_shape=[shap...]
  transfers between devices with their start and end apart: 10 -> 10, of which waited for: 4 -> 6; matrix products, arithmetic and copies ran while one was open for 1% -> 1% of each run, Pallas kernels for 44% -> 38%
where the time goes in v8:
time: 51.2 us; the launch traced here: 51.1 us
  Pallas kernels  25.7 us (50%)
  waiting for transfers between devices  14 us (27%)
  starting transfers between devices  10.7 us (21%)
    pallas_call x13, Pallas kernels, call(): pl.pallas_call(kernel, grid=grid, in_specs=specs, out_specs=out_specs, ou...  22.2 us
    ppermute x6, waiting for transfers between devices, shards(): arrived = [lax.ppermute(left, 'depth', onward) for left in done]  9.71 us
    ppermute x6, starting transfers between devices, shards(): arrived = [lax.ppermute(left, 'depth', onward) for left in done]  6.72 us
    ppermute x4, waiting for transfers between devices, shards(): rims = [lax.ppermute(first, 'tile', back) for first in firsts]  4.27 us
    ppermute x4, starting transfers between devices, shards(): rims = [lax.ppermute(first, 'tile', back) for first in firsts]  4 us
    pallas_call x1, Pallas kernels, edge_rows(): pl.pallas_call(functools.partial(edge_kernel, layers[0]), out_shape=[shap...  2.6 us
  transfers between devices with their start and end apart: 10, of which 6 were waited for; matrix products, arithmetic and copies ran while one was open for 1% of the time, Pallas kernels for 38%

profile of v8, /device:TPU:96, one launch (start us, length us, event | category | flops | bytes accessed | tf_op | source)
XLA Modules:
  0.0 51.1 jit_solution(12192956492656035927)
XLA Ops:
  0.0 0.0 copy-start.1
  0.0 0.0 copy-start
  0.0 0.0 copy-start.8
  0.0 0.0 copy-start.7
  0.0 2.6 %edge0.1 = (f32[1,2,2,128,128]{4,3,2,1,0:T(8,128)}, f32[1,2,2,128,128]{4,3,2,1,0:T(8,128)S(1)}, f32[1,2,2,128,128]{4,3,2,1,0:T(8,128)S(1)}, f32[1,2,2,128,128]{4,3,2,1,0:T(8,128)S(1)}) custom-call(f32[4,256,256]{2,1,0:T(8,128)} %phase_ref.3, f32[4,256,256]{2,1,0:T(8,128)} %absorb_ref.3), custom_call_target="tpu_custom_call" | custom-call | flops 5242880 | bytes 2097152 | tf_op jit(solution)/shard_map/edge0/pallas_call | solution.py:107
  2.6 2.5 %collective-permute-start = (f32[1,2,2,128,128]{4,3,2,1,0:T(8,128)}, f32[1,2,2,128,128]{4,3,2,1,0:T(8,128)}, u32[]{:S(2)}, u32[]{:S(2)}) collective-permute-start(f32[1,2,2,128,128]{4,3,2,1,0:T(8,128)} %get-tuple-element.21.refs_4_), channel_id=1, source_target_pairs={{0,7},{1,0},{2,1},{3,2},{4,3},{5,4},{6,5},{7,6},{8,15},{9,8},{10,9... | collective-permute-start | bytes 786440 | tf_op jit(solution)/shard_map/ppermute | solution.py:436
  5.1 0.7 %collective-permute-start.1 = (f32[1,2,2,128,128]{4,3,2,1,0:T(8,128)S(1)}, f32[1,2,2,128,128]{4,3,2,1,0:T(8,128)}, u32[]{:S(2)}, u32[]{:S(2)}) collective-permute-start(f32[1,2,2,128,128]{4,3,2,1,0:T(8,128)S(1)} %get-tuple-element.23.refs_4_), channel_id=1, source_target_pairs={{0,7},{1,0},{2,1},{3,2},{4,3},{5,4},{6,5},{7,6},{8,15},{9,8},{10,9... | collective-permute-start | bytes 786440 | tf_op jit(solution)/shard_map/ppermute | solution.py:436
  5.8 0.2 collective-permute-start.2
  6.0 0.7 %collective-permute-start.3 = (f32[1,2,2,128,128]{4,3,2,1,0:T(8,128)S(1)}, f32[1,2,2,128,128]{4,3,2,1,0:T(8,128)S(1)}, u32[]{:S(2)}, u32[]{:S(2)}) collective-permute-start(f32[1,2,2,128,128]{4,3,2,1,0:T(8,128)S(1)} %get-tuple-element.27.refs_4_), channel_id=1, source_target_pairs={{0,7},{1,0},{2,1},{3,2},{4,3},{5,4},{6,5},{7,6},{8,15},{9,8},{10,9... | collective-permute-start | bytes 786440 | tf_op jit(solution)/shard_map/ppermute | solution.py:436
  6.6 0.0 copy-done.8
  6.6 0.0 copy-done.7
  6.6 0.1 dynamic-slice_add_fusion
  6.7 0.1 copy.11
  6.8 0.1 broadcast_in_dim.10
  6.9 0.0 copy-done.1
  6.9 0.0 copy-done
  6.9 0.0 copy-start.2
  6.9 0.0 copy-start.4
  6.9 0.0 copy-start.5
  6.9 0.8 %rest.1.refs_5_ = f32[4,2,2,128,128]{4,3,2,1,0:T(8,128)S(1)} custom-call(f32[4,256,256]{2,1,0:T(8,128)S(1)} %copy-done, f32[4,256,256]{2,1,0:T(8,128)S(1)} %copy-done.1), custom_call_target="tpu_custom_call" | custom-call | flops 5242880 | bytes 2097152 | tf_op jit(solution)/shard_map/rest/pallas_call | solution.py:129
  7.8 1.5 %collective-permute-done.refs_6_ = f32[1,2,2,128,128]{4,3,2,1,0:T(8,128)} collective-permute-done((f32[1,2,2,128,128]{4,3,2,1,0:T(8,128)}, f32[1,2,2,128,128]{4,3,2,1,0:T(8,128)}, u32[]{:S(2)}, u32[]{:S(2)}) %collective-permute-start) | collective-permute-done | bytes 262176 | tf_op jit(solution)/shard_map/ppermute | solution.py:436
  9.3 0.1 broadcast_in_dim.11.refs_0_
  9.4 0.0 copy-done.2
  9.4 0.0 copy-done.4
  9.4 0.0 copy-done.5
  9.4 2.2 %enter0.1 = (f32[4,2,128,128]{3,2,1,0:T(8,128)S(1)}, f32[2,2,384,128]{3,2,1,0:T(8,128)S(1)}) custom-call(s32[24,128]{1,0:T(8,128)S(1)} %broadcast_in_dim.11.refs_0_, f32[4,2,128,128]{3,2,1,0:T(8,128)S(1)} %bitcast.7, bf16[2,256,256]{2,1,0:T(8,128)(2,1)S(1)} %copy-done.4, bf16[512,256]{1,0:T(8,128)(2,1)S(1)} %copy-done.5, ...), custom_call_target="tpu_custom_call" | custom-call | flops 3221225472 | bytes 786432 | tf_op jit(solution)/shard_map/enter0/pallas_call | solution.py:328
  11.6 0.4 collective-permute-done.1.refs_6_
  12.0 2.1 %enter1.1 = (f32[4,2,128,128]{3,2,1,0:T(8,128)S(1)}, f32[2,2,384,128]{3,2,1,0:T(8,128)S(1)}) custom-call(s32[24,128]{1,0:T(8,128)S(1)} %broadcast_in_dim.11.refs_0_, f32[4,2,128,128]{3,2,1,0:T(8,128)S(1)} %get-tuple-element.22.refs_1_, bf16[2,256,256]{2,1,0:T(8,128)(2,1)S(1)} %copy-done.4, bf16[512,256]{1,0:T(8,128)(2,1)S(1)} %copy-done.5, ...), custom_call_target="tpu_custom_call" | custom-call | flops 3221225472 | bytes 786432 | tf_op jit(solution)/shard_map/enter1/pallas_call | solution.py:328
  14.1 0.7 %collective-permute-done.2.refs_6_ = f32[1,2,2,128,128]{4,3,2,1,0:T(8,128)S(1)} collective-permute-done((f32[1,2,2,128,128]{4,3,2,1,0:T(8,128)S(1)}, f32[1,2,2,128,128]{4,3,2,1,0:T(8,128)S(1)}, u32[]{:S(2)}, u32[]{:S(2)}) %collective-permute-start.2) | collective-permute-done | bytes 262176 | tf_op jit(solution)/shard_map/ppermute | solution.py:436
  14.8 1.1 %enter2.1 = (f32[4,2,128,128]{3,2,1,0:T(8,128)S(1)}, f32[2,2,384,128]{3,2,1,0:T(8,128)S(1)}) custom-call(s32[24,128]{1,0:T(8,128)S(1)} %broadcast_in_dim.11.refs_0_, f32[4,2,128,128]{3,2,1,0:T(8,128)S(1)} %get-tuple-element.24.refs_1_, bf16[2,256,256]{2,1,0:T(8,128)(2,1)S(1)} %copy-done.4, bf16[512,256]{1,0:T(8,128)(2,1)S(1)} %copy-done.5, ...), custom_call_target="tpu_custom_call" | custom-call | flops 3221225472 | bytes 786432 | tf_op jit(solution)/shard_map/enter2/pallas_call | solution.py:328
  16.0 1.7 %collective-permute-done.3.refs_6_ = f32[1,2,2,128,128]{4,3,2,1,0:T(8,128)S(1)} collective-permute-done((f32[1,2,2,128,128]{4,3,2,1,0:T(8,128)S(1)}, f32[1,2,2,128,128]{4,3,2,1,0:T(8,128)S(1)}, u32[]{:S(2)}, u32[]{:S(2)}) %collective-permute-start.3) | collective-permute-done | bytes 262176 | tf_op jit(solution)/shard_map/ppermute | solution.py:436
  17.6 0.8 %leave0.1 = (f32[2,2,128,128]{3,2,1,0:T(8,128)S(1)}, f32[2,2,384,128]{3,2,1,0:T(8,128)S(1)}) custom-call(s32[24,128]{1,0:T(8,128)S(1)} %broadcast_in_dim.11.refs_0_, f32[4,2,128,128]{3,2,1,0:T(8,128)S(1)} %get-tuple-element.26.refs_1_, bf16[2,256,256]{2,1,0:T(8,128)(2,1)S(1)} %copy-done.4, bf16[512,256]{1,0:T(8,128)(2,1)S(1)} %copy-done.5, ...), custom_call_target="tpu_custom_call" | custom-call | flops 1610612736 | bytes 786432 | tf_op jit(solution)/shard_map/leave0/pallas_call | solution.py:328
  18.5 1.6 %collective-permute-start.6 = (f32[2,2,128,128]{3,2,1,0:T(8,128)S(1)}, f32[2,2,128,128]{3,2,1,0:T(8,128)S(1)}, u32[]{:S(2)}, u32[]{:S(2)}) collective-permute-start(f32[2,2,128,128]{3,2,1,0:T(8,128)S(1)} %get-tuple-element.29.refs_5_.refs_9_), channel_id=1, source_target_pairs={{0,8},{8,16},{16,24},{24,32},{32,40},{40,48},{48,56},{56,64},{64,7... | collective-permute-start | bytes 786440 | tf_op jit(solution)/shard_map/ppermute | solution.py:470
  20.0 0.0 copy-start.3
  20.0 0.8 %leave1.1 = (f32[1,2,128,128]{3,2,1,0:T(8,128)S(1)}, f32[1,2,128,128]{3,2,1,0:T(8,128)S(1)}) custom-call(s32[24,128]{1,0:T(8,128)S(1)} %broadcast_in_dim.11.refs_0_, f32[4,2,128,128]{3,2,1,0:T(8,128)S(1)} %get-tuple-element.26.refs_1_, bf16[2,256,256]{2,1,0:T(8,128)(2,1)S(1)} %copy-done.4, bf16[512,256]{1,0:T(8,128)(2,1)S(1)} %copy-done.5, ...), custom_call_target="tpu_custom_call" | custom-call | flops 1610612736 | bytes 786432 | tf_op jit(solution)/shard_map/leave1/pallas_call | solution.py:328
  20.8 1.6 %collective-permute-start.5 = (f32[1,2,128,128]{3,2,1,0:T(8,128)S(1)}, f32[1,2,128,128]{3,2,1,0:T(8,128)S(1)}, u32[]{:S(2)}, u32[]{:S(2)}) collective-permute-start(f32[1,2,128,128]{3,2,1,0:T(8,128)S(1)} %get-tuple-element.34.refs_10_), channel_id=1, source_target_pairs={{0,8},{8,16},{16,24},{24,32},{32,40},{40,48},{48,56},{56,64},{64,7... | collective-permute-start | bytes 393224 | tf_op jit(solution)/shard_map/ppermute | solution.py:470
  22.4 1.2 %collective-permute-start.4 = (f32[1,2,128,128]{3,2,1,0:T(8,128)S(1)}, f32[1,2,128,128]{3,2,1,0:T(8,128)S(1)}, u32[]{:S(2)}, u32[]{:S(2)}) collective-permute-start(f32[1,2,128,128]{3,2,1,0:T(8,128)S(1)} %get-tuple-element.30.refs_8_.refs_11_), channel_id=1, source_target_pairs={{0,8},{8,16},{16,24},{24,32},{32,40},{40,48},{48,56},{56,64},{64,7... | collective-permute-start | bytes 393224 | tf_op jit(solution)/shard_map/ppermute | solution.py:470
  23.6 0.0 copy-done.3
  23.6 0.0 copy-start.6
  23.6 6.3 %collective-permute-done.6.refs_1_ = f32[2,2,128,128]{3,2,1,0:T(8,128)S(1)} collective-permute-done((f32[2,2,128,128]{3,2,1,0:T(8,128)S(1)}, f32[2,2,128,128]{3,2,1,0:T(8,128)S(1)}, u32[]{:S(2)}, u32[]{:S(2)}) %collective-permute-start.6) | collective-permute-done | bytes 262176 | tf_op jit(solution)/shard_map/ppermute | solution.py:470
  29.9 3.0 %tick1_0.1.refs_9_.refs_12_ = f32[2,2,128,128]{3,2,1,0:T(8,128)S(1)} custom-call(s32[24,128]{1,0:T(8,128)S(1)} %broadcast_in_dim.11.refs_0_, f32[2,2,128,128]{3,2,1,0:T(8,128)S(1)} %collective-permute-done.6.refs_1_, bf16[2,256,256]{2,1,0:T(8,128)(2,1)S(1)} %copy-done.4, bf16[512,256]{1,0:T(8,128)(2,1)S(1)} %copy-done.5, ...), custom_call_target="tpu_custom_call" | custom-call | flops 6442450944 | bytes 3145728 | tf_op jit(solution)/shard_map/tick1_0/pallas_call | solution.py:328
  32.9 0.1 collective-permute-start.8
  32.9 0.0 collective-permute-done.5.refs_1_
  33.0 0.0 copy-done.6
  33.0 2.1 %tick1_2.1.refs_9_.refs_13_ = f32[1,2,128,128]{3,2,1,0:T(8,128)S(1)} custom-call(s32[24,128]{1,0:T(8,128)S(1)} %broadcast_in_dim.11.refs_0_, f32[1,2,128,128]{3,2,1,0:T(8,128)S(1)} %collective-permute-done.5.refs_1_, bf16[2,256,256]{2,1,0:T(8,128)(2,1)S(1)} %copy-done.4, bf16[256,384]{1,0:T(8,128)(2,1)S(1)} %copy-done.6, ...), custom_call_target="tpu_custom_call" | custom-call | flops 3221225472 | bytes 3145728 | tf_op jit(solution)/shard_map/tick1_2/pallas_call | solution.py:328
  35.1 0.9 %collective-permute-start.9 = (f32[1,2,128,128]{3,2,1,0:T(8,128)S(1)}, f32[1,2,128,128]{3,2,1,0:T(8,128)S(1)}, u32[]{:S(2)}, u32[]{:S(2)}) collective-permute-start(f32[1,2,128,128]{3,2,1,0:T(8,128)S(1)} %tick1_2.1.refs_9_.refs_13_), channel_id=1, source_target_pairs={{0,8},{8,16},{16,24},{24,32},{32,40},{40,48},{48,56},{56,64},{64,7... | collective-permute-start | bytes 393224 | tf_op jit(solution)/shard_map/ppermute | solution.py:470
  36.0 0.0 collective-permute-done.4.refs_1_
  36.0 2.1 %tick1_3.1.refs_8_.refs_14_ = f32[1,2,128,128]{3,2,1,0:T(8,128)S(1)} custom-call(s32[24,128]{1,0:T(8,128)S(1)} %broadcast_in_dim.11.refs_0_, f32[1,2,128,128]{3,2,1,0:T(8,128)S(1)} %collective-permute-done.4.refs_1_, bf16[2,256,256]{2,1,0:T(8,128)(2,1)S(1)} %copy-done.4, bf16[256,384]{1,0:T(8,128)(2,1)S(1)} %copy-done.6, ...), custom_call_target="tpu_custom_call" | custom-call | flops 3221225472 | bytes 3145728 | tf_op jit(solution)/shard_map/tick1_3/pallas_call | solution.py:328
  38.1 1.4 %collective-permute-start.7 = (f32[1,2,128,128]{3,2,1,0:T(8,128)S(1)}, f32[1,2,128,128]{3,2,1,0:T(8,128)S(1)}, u32[]{:S(2)}, u32[]{:S(2)}) collective-permute-start(f32[1,2,128,128]{3,2,1,0:T(8,128)S(1)} %tick1_3.1.refs_8_.refs_14_), channel_id=1, source_target_pairs={{0,8},{8,16},{16,24},{24,32},{32,40},{40,48},{48,56},{56,64},{64,7... | collective-permute-start | bytes 393224 | tf_op jit(solution)/shard_map/ppermute | solution.py:470
  39.5 3.4 %collective-permute-done.8.refs_1_ = f32[2,2,128,128]{3,2,1,0:T(8,128)S(1)} collective-permute-done((f32[2,2,128,128]{3,2,1,0:T(8,128)S(1)}, f32[2,2,128,128]{3,2,1,0:T(8,128)S(1)}, u32[]{:S(2)}, u32[]{:S(2)}) %collective-permute-start.8) | collective-permute-done | bytes 262176 | tf_op jit(solution)/shard_map/ppermute | solution.py:470
  42.9 3.0 %tick2_0.1 = (f32[2,2,128,128]{3,2,1,0:T(8,128)S(1)}, f32[3,4,2,128,128]{4,3,2,1,0:T(8,128)}) custom-call(s32[24,128]{1,0:T(8,128)S(1)} %broadcast_in_dim.11.refs_0_, f32[2,2,128,128]{3,2,1,0:T(8,128)S(1)} %collective-permute-done.8.refs_1_, bf16[2,256,256]{2,1,0:T(8,128)(2,1)S(1)} %copy-done.4, bf16[512,256]{1,0:T(8,128)(2,1)S(1)} %copy-done.5, ...), custom_call_target="tpu_custom_call" | custom-call | flops 6442450944 | bytes 3145728 | tf_op jit(solution)/shard_map/tick2_0/pallas_call | solution.py:328
  46.0 0.0 collective-permute-done.9.refs_1_
  46.0 2.1 %tick2_2.1.refs_10_.refs_12_ = f32[1,2,128,128]{3,2,1,0:T(8,128)S(1)} custom-call(s32[24,128]{1,0:T(8,128)S(1)} %broadcast_in_dim.11.refs_0_, f32[1,2,128,128]{3,2,1,0:T(8,128)S(1)} %collective-permute-done.9.refs_1_, bf16[2,256,256]{2,1,0:T(8,128)(2,1)S(1)} %copy-done.4, bf16[256,384]{1,0:T(8,128)(2,1)S(1)} %copy-done.6, ...), custom_call_target="tpu_custom_call" | custom-call | flops 3221225472 | bytes 3145728 | tf_op jit(solution)/shard_map/tick2_2/pallas_call | solution.py:328
  48.1 0.0 collective-permute-done.7.refs_1_
  48.1 2.8 %tick2_3.1 = f32[3,4,2,128,128]{4,3,2,1,0:T(8,128)} custom-call(s32[24,128]{1,0:T(8,128)S(1)} %broadcast_in_dim.11.refs_0_, f32[1,2,128,128]{3,2,1,0:T(8,128)S(1)} %collective-permute-done.7.refs_1_, bf16[2,256,256]{2,1,0:T(8,128)(2,1)S(1)} %copy-done.4, bf16[256,384]{1,0:T(8,128)(2,1)S(1)} %copy-done.6, ...), custom_call_target="tpu_custom_call", output_to_operand_aliasing={{}: (11, {})} | custom-call | flops 3221225472 | bytes 3145728 | tf_op jit(solution)/shard_map/tick2_3/pallas_call | solution.py:328
  (3 shorter events, 0.0 us)
Async XLA Ops:
  0.0 6.9 %copy-start.1 = (f32[4,256,256]{2,1,0:T(8,128)S(1)}, f32[4,256,256]{2,1,0:T(8,128)}, u32[]{:S(2)}) copy-start(f32[4,256,256]{2,1,0:T(8,128)} %absorb_ref.3) | copy-start | bytes 3145732
  0.0 6.9 %copy-start = (f32[4,256,256]{2,1,0:T(8,128)S(1)}, f32[4,256,256]{2,1,0:T(8,128)}, u32[]{:S(2)}) copy-start(f32[4,256,256]{2,1,0:T(8,128)} %phase_ref.3) | copy-start | bytes 3145732
  0.0 6.6 %copy-start.8 = (s32[18,4]{0,1:T(4,128)S(1)}, s32[18,4]{0,1:T(4,128)}, u32[]{:S(2)}) copy-start(s32[18,4]{0,1:T(4,128)} %param.13) | copy-start | bytes 868
  0.0 6.6 %copy-start.7 = (s32[18,4]{0,1:T(4,128)S(1)}, s32[18,4]{0,1:T(4,128)}, u32[]{:S(2)}) copy-start(s32[18,4]{0,1:T(4,128)} %param.14) | copy-start | bytes 868
  2.6 6.7 %collective-permute-start = (f32[1,2,2,128,128]{4,3,2,1,0:T(8,128)}, f32[1,2,2,128,128]{4,3,2,1,0:T(8,128)}, u32[]{:S(2)}, u32[]{:S(2)}) collective-permute-start(f32[1,2,2,128,128]{4,3,2,1,0:T(8,128)} %get-tuple-element.21.refs_4_), channel_id=1, source_target_pairs={{0,7},{1,0},{2,1},{3,2},{4,3},{5,4},{6,5},{7,6},{8,15},{9,8},{10,9... | collective-permute-start | bytes 786440 | tf_op jit(solution)/shard_map/ppermute | solution.py:436
  5.1 6.9 %collective-permute-start.1 = (f32[1,2,2,128,128]{4,3,2,1,0:T(8,128)S(1)}, f32[1,2,2,128,128]{4,3,2,1,0:T(8,128)}, u32[]{:S(2)}, u32[]{:S(2)}) collective-permute-start(f32[1,2,2,128,128]{4,3,2,1,0:T(8,128)S(1)} %get-tuple-element.23.refs_4_), channel_id=1, source_target_pairs={{0,7},{1,0},{2,1},{3,2},{4,3},{5,4},{6,5},{7,6},{8,15},{9,8},{10,9... | collective-permute-start | bytes 786440 | tf_op jit(solution)/shard_map/ppermute | solution.py:436
  5.8 9.0 %collective-permute-start.2 = (f32[1,2,2,128,128]{4,3,2,1,0:T(8,128)S(1)}, f32[1,2,2,128,128]{4,3,2,1,0:T(8,128)S(1)}, u32[]{:S(2)}, u32[]{:S(2)}) collective-permute-start(f32[1,2,2,128,128]{4,3,2,1,0:T(8,128)S(1)} %get-tuple-element.25.refs_4_), channel_id=1, source_target_pairs={{0,7},{1,0},{2,1},{3,2},{4,3},{5,4},{6,5},{7,6},{8,15},{9,8},{10,9... | collective-permute-start | bytes 786440 | tf_op jit(solution)/shard_map/ppermute | solution.py:436
  6.0 11.7 %collective-permute-start.3 = (f32[1,2,2,128,128]{4,3,2,1,0:T(8,128)S(1)}, f32[1,2,2,128,128]{4,3,2,1,0:T(8,128)S(1)}, u32[]{:S(2)}, u32[]{:S(2)}) collective-permute-start(f32[1,2,2,128,128]{4,3,2,1,0:T(8,128)S(1)} %get-tuple-element.27.refs_4_), channel_id=1, source_target_pairs={{0,7},{1,0},{2,1},{3,2},{4,3},{5,4},{6,5},{7,6},{8,15},{9,8},{10,9... | collective-permute-start | bytes 786440 | tf_op jit(solution)/shard_map/ppermute | solution.py:436
  6.9 2.5 %copy-start.2 = (f32[1,4,2,128,128]{4,3,2,1,0:T(8,128)S(1)}, f32[1,4,2,128,128]{4,3,2,1,0:T(8,128)}, u32[]{:S(2)}) copy-start(f32[1,4,2,128,128]{4,3,2,1,0:T(8,128)} %param.12) | copy-start | bytes 1572868
  6.9 2.5 %copy-start.4 = (bf16[2,256,256]{2,1,0:T(8,128)(2,1)S(1)}, bf16[2,256,256]{2,1,0:T(8,128)(2,1)}, u32[]{:S(2)}) copy-start(bf16[2,256,256]{2,1,0:T(8,128)(2,1)} %constant.24.clone.refs_2_) | copy-start | bytes 786436
  6.9 2.4 %copy-start.5 = (bf16[512,256]{1,0:T(8,128)(2,1)S(1)}, bf16[512,256]{1,0:T(8,128)(2,1)}, u32[]{:S(2)}) copy-start(bf16[512,256]{1,0:T(8,128)(2,1)} %constant.25.clone.refs_3_) | copy-start | bytes 786436
  18.5 11.4 %collective-permute-start.6 = (f32[2,2,128,128]{3,2,1,0:T(8,128)S(1)}, f32[2,2,128,128]{3,2,1,0:T(8,128)S(1)}, u32[]{:S(2)}, u32[]{:S(2)}) collective-permute-start(f32[2,2,128,128]{3,2,1,0:T(8,128)S(1)} %get-tuple-element.29.refs_5_.refs_9_), channel_id=1, source_target_pairs={{0,8},{8,16},{16,24},{24,32},{32,40},{40,48},{48,56},{56,64},{64,7... | collective-permute-start | bytes 786440 | tf_op jit(solution)/shard_map/ppermute | solution.py:470
  20.0 3.6 %copy-start.3 = (f32[2,128,128]{2,1,0:T(8,128)S(1)}, f32[2,128,128]{2,1,0:T(8,128)}, u32[]{:S(2)}) copy-start(f32[2,128,128]{2,1,0:T(8,128)} %refs_1_.3) | copy-start | bytes 393220
  20.8 12.1 %collective-permute-start.5 = (f32[1,2,128,128]{3,2,1,0:T(8,128)S(1)}, f32[1,2,128,128]{3,2,1,0:T(8,128)S(1)}, u32[]{:S(2)}, u32[]{:S(2)}) collective-permute-start(f32[1,2,128,128]{3,2,1,0:T(8,128)S(1)} %get-tuple-element.34.refs_10_), channel_id=1, source_target_pairs={{0,8},{8,16},{16,24},{24,32},{32,40},{40,48},{48,56},{56,64},{64,7... | collective-permute-start | bytes 393224 | tf_op jit(solution)/shard_map/ppermute | solution.py:470
  22.4 13.6 %collective-permute-start.4 = (f32[1,2,128,128]{3,2,1,0:T(8,128)S(1)}, f32[1,2,128,128]{3,2,1,0:T(8,128)S(1)}, u32[]{:S(2)}, u32[]{:S(2)}) collective-permute-start(f32[1,2,128,128]{3,2,1,0:T(8,128)S(1)} %get-tuple-element.30.refs_8_.refs_11_), channel_id=1, source_target_pairs={{0,8},{8,16},{16,24},{24,32},{32,40},{40,48},{48,56},{56,64},{64,7... | collective-permute-start | bytes 393224 | tf_op jit(solution)/shard_map/ppermute | solution.py:470
  23.6 9.4 %copy-start.6 = (bf16[256,384]{1,0:T(8,128)(2,1)S(1)}, bf16[256,384]{1,0:T(8,128)(2,1)}, u32[]{:S(2)}) copy-start(bf16[256,384]{1,0:T(8,128)(2,1)} %constant.26.clone.refs_3_) | copy-start | bytes 589828
  32.9 10.1 %collective-permute-start.8 = (f32[2,2,128,128]{3,2,1,0:T(8,128)S(1)}, f32[2,2,128,128]{3,2,1,0:T(8,128)S(1)}, u32[]{:S(2)}, u32[]{:S(2)}) collective-permute-start(f32[2,2,128,128]{3,2,1,0:T(8,128)S(1)} %tick1_0.1.refs_9_.refs_12_), channel_id=1, source_target_pairs={{0,8},{8,16},{16,24},{24,32},{32,40},{40,48},{48,56},{56,64},{64,7... | collective-permute-start | bytes 786440 | tf_op jit(solution)/shard_map/ppermute | solution.py:470
  35.1 10.9 %collective-permute-start.9 = (f32[1,2,128,128]{3,2,1,0:T(8,128)S(1)}, f32[1,2,128,128]{3,2,1,0:T(8,128)S(1)}, u32[]{:S(2)}, u32[]{:S(2)}) collective-permute-start(f32[1,2,128,128]{3,2,1,0:T(8,128)S(1)} %tick1_2.1.refs_9_.refs_13_), channel_id=1, source_target_pairs={{0,8},{8,16},{16,24},{24,32},{32,40},{40,48},{48,56},{56,64},{64,7... | collective-permute-start | bytes 393224 | tf_op jit(solution)/shard_map/ppermute | solution.py:470
  38.1 10.0 %collective-permute-start.7 = (f32[1,2,128,128]{3,2,1,0:T(8,128)S(1)}, f32[1,2,128,128]{3,2,1,0:T(8,128)S(1)}, u32[]{:S(2)}, u32[]{:S(2)}) collective-permute-start(f32[1,2,128,128]{3,2,1,0:T(8,128)S(1)} %tick1_3.1.refs_8_.refs_14_), channel_id=1, source_target_pairs={{0,8},{8,16},{16,24},{24,32},{32,40},{40,48},{48,56},{56,64},{64,7... | collective-permute-start | bytes 393224 | tf_op jit(solution)/shard_map/ppermute | solution.py:470

commit v9 on v7

--- a/solution.py
+++ b/solution.py
@@ -11,7 +11,7 @@
 from jax.sharding import PartitionSpec as P
 
 TICKS = 3
-GROUPS = [[0, 1], [2], [3]]
+GROUPS = [[0], [1, 2], [3]]
 
 fresnel = 0.1
 VMEM_LIMIT = 24 * 1024 * 1024

time: 49.7 us -> 52.7 us (1.060); the launches traced: 49.4 us -> 51.8 us
  waiting for transfers between devices: 11 us -> 14.8 us
  starting transfers between devices: 10.8 us -> 9.29 us
    ppermute x6, waiting for transfers between devices: 9.66 us -> 13.5 us  [shards(): arrived = [lax.ppermute(left, 'depth', onward) for left in done]]
    ppermute x6, starting transfers between devices: 6.76 us -> 5.28 us  [shards(): arrived = [lax.ppermute(left, 'depth', onward) for left in done]]
  transfers between devices with their start and end apart: 10 -> 10, of which waited for: 4 -> 5; matrix products, arithmetic and copies ran while one was open for 1% -> 1% of each run, Pallas kernels for 44% -> 43%
where the time goes in v9:
time: 52.7 us; the launch traced here: 51.8 us
  Pallas kernels  26.7 us (51%)
  waiting for transfers between devices  14.8 us (28%)
  starting transfers between devices  9.29 us (18%)
  local copies, waits for them, and re-layouts  0.54 us (1%)
    pallas_call x13, Pallas kernels, call(): pl.pallas_call(kernel, grid=grid, in_specs=specs, out_specs=out_specs, ou...  23.1 us
    ppermute x6, waiting for transfers between devices, shards(): arrived = [lax.ppermute(left, 'depth', onward) for left in done]  13.5 us
    ppermute x6, starting transfers between devices, shards(): arrived = [lax.ppermute(left, 'depth', onward) for left in done]  5.28 us
    ppermute x4, starting transfers between devices, shards(): rims = [lax.ppermute(first, 'tile', back) for first in firsts]  4.01 us
    pallas_call x2, Pallas kernels, edge_rows(): pl.pallas_call(functools.partial(edge_kernel, layers[0]), out_shape=[shap...  2.75 us
    ppermute x4, waiting for transfers between devices, shards(): rims = [lax.ppermute(first, 'tile', back) for first in firsts]  1.32 us
  transfers between devices with their start and end apart: 10, of which 5 were waited for; matrix products, arithmetic and copies ran while one was open for 1% of the time, Pallas kernels for 43%

profile of v9, /device:TPU:96, one launch (start us, length us, event | category | flops | bytes accessed | tf_op | source)
XLA Modules:
  0.0 51.8 jit_solution(14670349397920547202)
XLA Ops:
  0.0 1.2 %edge0.1.refs_4_ = f32[1,2,2,128,128]{4,3,2,1,0:T(8,128)S(1)} custom-call(f32[4,256,256]{2,1,0:T(8,128)} %phase_ref.5, f32[4,256,256]{2,1,0:T(8,128)} %absorb_ref.5), custom_call_target="tpu_custom_call" | custom-call | flops 1310720 | bytes 524288 | tf_op jit(solution)/shard_map/edge0/pallas_call | solution.py:107
  1.2 0.0 copy-start.8
  1.2 0.0 copy-start.7
  1.2 0.0 copy-start
  1.2 0.0 copy-start.1
  1.2 2.5 %collective-permute-start = (f32[1,2,2,128,128]{4,3,2,1,0:T(8,128)S(1)}, f32[1,2,2,128,128]{4,3,2,1,0:T(8,128)}, u32[]{:S(2)}, u32[]{:S(2)}) collective-permute-start(f32[1,2,2,128,128]{4,3,2,1,0:T(8,128)S(1)} %edge0.1.refs_4_), channel_id=1, source_target_pairs={{0,7},{1,0},{2,1},{3,2},{4,3},{5,4},{6,5},{7,6},{8,15},{9,8},{10,9... | collective-permute-start | bytes 786440 | tf_op jit(solution)/shard_map/ppermute | solution.py:437
  3.7 1.6 %edge1.1 = (f32[1,2,2,128,128]{4,3,2,1,0:T(8,128)S(1)}, f32[1,2,2,128,128]{4,3,2,1,0:T(8,128)S(1)}, f32[1,2,2,128,128]{4,3,2,1,0:T(8,128)S(1)}) custom-call(f32[4,256,256]{2,1,0:T(8,128)} %phase_ref.5, f32[4,256,256]{2,1,0:T(8,128)} %absorb_ref.5), custom_call_target="tpu_custom_call" | custom-call | flops 3932160 | bytes 1572864 | tf_op jit(solution)/shard_map/edge1/pallas_call | solution.py:107
  5.3 0.7 %collective-permute-start.1 = (f32[1,2,2,128,128]{4,3,2,1,0:T(8,128)S(1)}, f32[1,2,2,128,128]{4,3,2,1,0:T(8,128)}, u32[]{:S(2)}, u32[]{:S(2)}) collective-permute-start(f32[1,2,2,128,128]{4,3,2,1,0:T(8,128)S(1)} %get-tuple-element.21.refs_4_), channel_id=1, source_target_pairs={{0,7},{1,0},{2,1},{3,2},{4,3},{5,4},{6,5},{7,6},{8,15},{9,8},{10,9... | collective-permute-start | bytes 786440 | tf_op jit(solution)/shard_map/ppermute | solution.py:437
  6.0 0.3 collective-permute-start.2
  6.3 0.6 %collective-permute-start.3 = (f32[1,2,2,128,128]{4,3,2,1,0:T(8,128)S(1)}, f32[1,2,2,128,128]{4,3,2,1,0:T(8,128)S(1)}, u32[]{:S(2)}, u32[]{:S(2)}) collective-permute-start(f32[1,2,2,128,128]{4,3,2,1,0:T(8,128)S(1)} %get-tuple-element.25.refs_4_), channel_id=1, source_target_pairs={{0,7},{1,0},{2,1},{3,2},{4,3},{5,4},{6,5},{7,6},{8,15},{9,8},{10,9... | collective-permute-start | bytes 786440 | tf_op jit(solution)/shard_map/ppermute | solution.py:437
  6.8 0.0 copy-done.8
  6.8 0.0 copy-done.7
  6.8 0.1 dynamic-slice_add_fusion
  6.9 0.1 copy.11
  7.0 0.1 broadcast_in_dim.10
  7.1 0.0 copy-done
  7.1 0.0 copy-done.1
  7.1 0.0 copy-start.2
  7.1 0.0 copy-start.4
  7.1 0.0 copy-start.5
  7.1 0.8 %rest.1.refs_5_ = f32[4,2,2,128,128]{4,3,2,1,0:T(8,128)S(1)} custom-call(f32[4,256,256]{2,1,0:T(8,128)S(1)} %copy-done, f32[4,256,256]{2,1,0:T(8,128)S(1)} %copy-done.1), custom_call_target="tpu_custom_call" | custom-call | flops 5242880 | bytes 2097152 | tf_op jit(solution)/shard_map/rest/pallas_call | solution.py:129
  8.0 0.0 collective-permute-done.refs_6_
  8.0 0.1 broadcast_in_dim.11.refs_0_
  8.1 0.1 copy-done.2
  8.2 0.1 copy-done.4
  8.2 0.1 copy-done.5
  8.3 2.2 %enter0.1 = (f32[4,2,128,128]{3,2,1,0:T(8,128)S(1)}, f32[2,2,384,128]{3,2,1,0:T(8,128)S(1)}) custom-call(s32[24,128]{1,0:T(8,128)S(1)} %broadcast_in_dim.11.refs_0_, f32[4,2,128,128]{3,2,1,0:T(8,128)S(1)} %bitcast.7, bf16[2,256,256]{2,1,0:T(8,128)(2,1)S(1)} %copy-done.4, bf16[512,256]{1,0:T(8,128)(2,1)S(1)} %copy-done.5, ...), custom_call_target="tpu_custom_call" | custom-call | flops 3221225472 | bytes 786432 | tf_op jit(solution)/shard_map/enter0/pallas_call | solution.py:328
  10.5 0.0 collective-permute-done.1.refs_6_
  10.5 2.1 %enter1.1 = (f32[4,2,128,128]{3,2,1,0:T(8,128)S(1)}, f32[2,2,384,128]{3,2,1,0:T(8,128)S(1)}) custom-call(s32[24,128]{1,0:T(8,128)S(1)} %broadcast_in_dim.11.refs_0_, f32[4,2,128,128]{3,2,1,0:T(8,128)S(1)} %get-tuple-element.20.refs_1_, bf16[2,256,256]{2,1,0:T(8,128)(2,1)S(1)} %copy-done.4, bf16[512,256]{1,0:T(8,128)(2,1)S(1)} %copy-done.5, ...), custom_call_target="tpu_custom_call" | custom-call | flops 3221225472 | bytes 786432 | tf_op jit(solution)/shard_map/enter1/pallas_call | solution.py:328
  12.6 0.6 %collective-permute-done.2.refs_6_ = f32[1,2,2,128,128]{4,3,2,1,0:T(8,128)} collective-permute-done((f32[1,2,2,128,128]{4,3,2,1,0:T(8,128)S(1)}, f32[1,2,2,128,128]{4,3,2,1,0:T(8,128)}, u32[]{:S(2)}, u32[]{:S(2)}) %collective-permute-start.2) | collective-permute-done | bytes 262176 | tf_op jit(solution)/shard_map/ppermute | solution.py:437
  13.2 0.0 copy-start.6
  13.2 2.1 %enter2.1 = (f32[4,2,128,128]{3,2,1,0:T(8,128)S(1)}, f32[2,2,384,128]{3,2,1,0:T(8,128)S(1)}) custom-call(s32[24,128]{1,0:T(8,128)S(1)} %broadcast_in_dim.11.refs_0_, f32[4,2,128,128]{3,2,1,0:T(8,128)S(1)} %get-tuple-element.22.refs_1_, bf16[2,256,256]{2,1,0:T(8,128)(2,1)S(1)} %copy-done.4, bf16[512,256]{1,0:T(8,128)(2,1)S(1)} %copy-done.5, ...), custom_call_target="tpu_custom_call" | custom-call | flops 3221225472 | bytes 786432 | tf_op jit(solution)/shard_map/enter2/pallas_call | solution.py:328
  15.3 0.7 %collective-permute-done.3.refs_6_ = f32[1,2,2,128,128]{4,3,2,1,0:T(8,128)S(1)} collective-permute-done((f32[1,2,2,128,128]{4,3,2,1,0:T(8,128)S(1)}, f32[1,2,2,128,128]{4,3,2,1,0:T(8,128)S(1)}, u32[]{:S(2)}, u32[]{:S(2)}) %collective-permute-start.3) | collective-permute-done | bytes 262176 | tf_op jit(solution)/shard_map/ppermute | solution.py:437
  16.0 0.0 copy-done.6
  16.0 0.6 %leave0.1 = (f32[1,2,128,128]{3,2,1,0:T(8,128)S(1)}, f32[2,2,384,128]{3,2,1,0:T(8,128)S(1)}) custom-call(s32[24,128]{1,0:T(8,128)S(1)} %broadcast_in_dim.11.refs_0_, f32[4,2,128,128]{3,2,1,0:T(8,128)S(1)} %get-tuple-element.24.refs_1_, bf16[2,256,256]{2,1,0:T(8,128)(2,1)S(1)} %copy-done.4, bf16[256,384]{1,0:T(8,128)(2,1)S(1)} %copy-done.6, ...), custom_call_target="tpu_custom_call" | custom-call | flops 805306368 | bytes 786432 | tf_op jit(solution)/shard_map/leave0/pallas_call | solution.py:328
  16.6 1.6 %collective-permute-start.6 = (f32[1,2,128,128]{3,2,1,0:T(8,128)S(1)}, f32[1,2,128,128]{3,2,1,0:T(8,128)S(1)}, u32[]{:S(2)}, u32[]{:S(2)}) collective-permute-start(f32[1,2,128,128]{3,2,1,0:T(8,128)S(1)} %get-tuple-element.27.refs_5_.refs_9_), channel_id=1, source_target_pairs={{0,8},{8,16},{16,24},{24,32},{32,40},{40,48},{48,56},{56,64},{64,7... | collective-permute-start | bytes 393224 | tf_op jit(solution)/shard_map/ppermute | solution.py:471
  18.2 0.0 copy-start.3
  18.2 1.1 %leave1.1 = (f32[2,2,128,128]{3,2,1,0:T(8,128)S(1)}, f32[1,2,128,128]{3,2,1,0:T(8,128)S(1)}) custom-call(s32[24,128]{1,0:T(8,128)S(1)} %broadcast_in_dim.11.refs_0_, f32[4,2,128,128]{3,2,1,0:T(8,128)S(1)} %get-tuple-element.24.refs_1_, bf16[2,256,256]{2,1,0:T(8,128)(2,1)S(1)} %copy-done.4, bf16[512,256]{1,0:T(8,128)(2,1)S(1)} %copy-done.5, ...), custom_call_target="tpu_custom_call" | custom-call | flops 2415919104 | bytes 786432 | tf_op jit(solution)/shard_map/leave1/pallas_call | solution.py:328
  19.3 1.6 %collective-permute-start.4 = (f32[1,2,128,128]{3,2,1,0:T(8,128)S(1)}, f32[1,2,128,128]{3,2,1,0:T(8,128)S(1)}, u32[]{:S(2)}, u32[]{:S(2)}) collective-permute-start(f32[1,2,128,128]{3,2,1,0:T(8,128)S(1)} %get-tuple-element.28.refs_8_.refs_11_), channel_id=1, source_target_pairs={{0,8},{8,16},{16,24},{24,32},{32,40},{40,48},{48,56},{56,64},{64,7... | collective-permute-start | bytes 393224 | tf_op jit(solution)/shard_map/ppermute | solution.py:471
  20.8 1.2 %collective-permute-start.5 = (f32[2,2,128,128]{3,2,1,0:T(8,128)S(1)}, f32[2,2,128,128]{3,2,1,0:T(8,128)S(1)}, u32[]{:S(2)}, u32[]{:S(2)}) collective-permute-start(f32[2,2,128,128]{3,2,1,0:T(8,128)S(1)} %get-tuple-element.32.refs_10_), channel_id=1, source_target_pairs={{0,8},{8,16},{16,24},{24,32},{32,40},{40,48},{48,56},{56,64},{64,7... | collective-permute-start | bytes 786440 | tf_op jit(solution)/shard_map/ppermute | solution.py:471
  22.0 0.0 copy-done.3
  22.0 2.4 %collective-permute-done.6.refs_1_ = f32[1,2,128,128]{3,2,1,0:T(8,128)S(1)} collective-permute-done((f32[1,2,128,128]{3,2,1,0:T(8,128)S(1)}, f32[1,2,128,128]{3,2,1,0:T(8,128)S(1)}, u32[]{:S(2)}, u32[]{:S(2)}) %collective-permute-start.6) | collective-permute-done | bytes 131104 | tf_op jit(solution)/shard_map/ppermute | solution.py:471
  24.4 2.1 %tick1_0.1.refs_9_.refs_12_ = f32[1,2,128,128]{3,2,1,0:T(8,128)S(1)} custom-call(s32[24,128]{1,0:T(8,128)S(1)} %broadcast_in_dim.11.refs_0_, f32[1,2,128,128]{3,2,1,0:T(8,128)S(1)} %collective-permute-done.6.refs_1_, bf16[2,256,256]{2,1,0:T(8,128)(2,1)S(1)} %copy-done.4, bf16[256,384]{1,0:T(8,128)(2,1)S(1)} %copy-done.6, ...), custom_call_target="tpu_custom_call" | custom-call | flops 3221225472 | bytes 3145728 | tf_op jit(solution)/shard_map/tick1_0/pallas_call | solution.py:328
  26.5 0.1 collective-permute-start.8
  26.6 6.9 %collective-permute-done.5.refs_1_ = f32[2,2,128,128]{3,2,1,0:T(8,128)S(1)} collective-permute-done((f32[2,2,128,128]{3,2,1,0:T(8,128)S(1)}, f32[2,2,128,128]{3,2,1,0:T(8,128)S(1)}, u32[]{:S(2)}, u32[]{:S(2)}) %collective-permute-start.5) | collective-permute-done | bytes 262176 | tf_op jit(solution)/shard_map/ppermute | solution.py:471
  33.5 3.0 %tick1_1.1.refs_9_.refs_13_ = f32[2,2,128,128]{3,2,1,0:T(8,128)S(1)} custom-call(s32[24,128]{1,0:T(8,128)S(1)} %broadcast_in_dim.11.refs_0_, f32[2,2,128,128]{3,2,1,0:T(8,128)S(1)} %collective-permute-done.5.refs_1_, bf16[2,256,256]{2,1,0:T(8,128)(2,1)S(1)} %copy-done.4, bf16[512,256]{1,0:T(8,128)(2,1)S(1)} %copy-done.5, ...), custom_call_target="tpu_custom_call" | custom-call | flops 6442450944 | bytes 3145728 | tf_op jit(solution)/shard_map/tick1_1/pallas_call | solution.py:328
  36.5 0.1 collective-permute-start.9
  36.5 0.0 collective-permute-done.4.refs_1_
  36.5 2.1 %tick1_3.1.refs_8_.refs_14_ = f32[1,2,128,128]{3,2,1,0:T(8,128)S(1)} custom-call(s32[24,128]{1,0:T(8,128)S(1)} %broadcast_in_dim.11.refs_0_, f32[1,2,128,128]{3,2,1,0:T(8,128)S(1)} %collective-permute-done.4.refs_1_, bf16[2,256,256]{2,1,0:T(8,128)(2,1)S(1)} %copy-done.4, bf16[256,384]{1,0:T(8,128)(2,1)S(1)} %copy-done.6, ...), custom_call_target="tpu_custom_call" | custom-call | flops 3221225472 | bytes 3145728 | tf_op jit(solution)/shard_map/tick1_3/pallas_call | solution.py:328
  38.7 0.8 %collective-permute-start.7 = (f32[1,2,128,128]{3,2,1,0:T(8,128)S(1)}, f32[1,2,128,128]{3,2,1,0:T(8,128)S(1)}, u32[]{:S(2)}, u32[]{:S(2)}) collective-permute-start(f32[1,2,128,128]{3,2,1,0:T(8,128)S(1)} %tick1_3.1.refs_8_.refs_14_), channel_id=1, source_target_pairs={{0,8},{8,16},{16,24},{24,32},{32,40},{40,48},{48,56},{56,64},{64,7... | collective-permute-start | bytes 393224 | tf_op jit(solution)/shard_map/ppermute | solution.py:471
  39.5 0.0 collective-permute-done.8.refs_1_
  39.5 2.2 %tick2_0.1 = (f32[1,2,128,128]{3,2,1,0:T(8,128)S(1)}, f32[3,4,2,128,128]{4,3,2,1,0:T(8,128)}) custom-call(s32[24,128]{1,0:T(8,128)S(1)} %broadcast_in_dim.11.refs_0_, f32[1,2,128,128]{3,2,1,0:T(8,128)S(1)} %collective-permute-done.8.refs_1_, bf16[2,256,256]{2,1,0:T(8,128)(2,1)S(1)} %copy-done.4, bf16[256,384]{1,0:T(8,128)(2,1)S(1)} %copy-done.6, ...), custom_call_target="tpu_custom_call" | custom-call | flops 3221225472 | bytes 3145728 | tf_op jit(solution)/shard_map/tick2_0/pallas_call | solution.py:328
  41.7 4.2 %collective-permute-done.9.refs_1_ = f32[2,2,128,128]{3,2,1,0:T(8,128)S(1)} collective-permute-done((f32[2,2,128,128]{3,2,1,0:T(8,128)S(1)}, f32[2,2,128,128]{3,2,1,0:T(8,128)S(1)}, u32[]{:S(2)}, u32[]{:S(2)}) %collective-permute-start.9) | collective-permute-done | bytes 262176 | tf_op jit(solution)/shard_map/ppermute | solution.py:471
  45.8 3.0 %tick2_1.1.refs_10_.refs_12_ = f32[2,2,128,128]{3,2,1,0:T(8,128)S(1)} custom-call(s32[24,128]{1,0:T(8,128)S(1)} %broadcast_in_dim.11.refs_0_, f32[2,2,128,128]{3,2,1,0:T(8,128)S(1)} %collective-permute-done.9.refs_1_, bf16[2,256,256]{2,1,0:T(8,128)(2,1)S(1)} %copy-done.4, bf16[512,256]{1,0:T(8,128)(2,1)S(1)} %copy-done.5, ...), custom_call_target="tpu_custom_call" | custom-call | flops 6442450944 | bytes 3145728 | tf_op jit(solution)/shard_map/tick2_1/pallas_call | solution.py:328
  48.8 0.0 collective-permute-done.7.refs_1_
  48.8 2.8 %tick2_3.1 = f32[3,4,2,128,128]{4,3,2,1,0:T(8,128)} custom-call(s32[24,128]{1,0:T(8,128)S(1)} %broadcast_in_dim.11.refs_0_, f32[1,2,128,128]{3,2,1,0:T(8,128)S(1)} %collective-permute-done.7.refs_1_, bf16[2,256,256]{2,1,0:T(8,128)(2,1)S(1)} %copy-done.4, bf16[256,384]{1,0:T(8,128)(2,1)S(1)} %copy-done.6, ...), custom_call_target="tpu_custom_call", output_to_operand_aliasing={{}: (11, {})} | custom-call | flops 3221225472 | bytes 3145728 | tf_op jit(solution)/shard_map/tick2_3/pallas_call | solution.py:328
  (3 shorter events, 0.0 us)
Async XLA Ops:
  1.2 5.7 %copy-start.8 = (s32[18,4]{0,1:T(4,128)S(1)}, s32[18,4]{0,1:T(4,128)}, u32[]{:S(2)}) copy-start(s32[18,4]{0,1:T(4,128)} %param.13) | copy-start | bytes 868
  1.2 5.7 %copy-start.7 = (s32[18,4]{0,1:T(4,128)S(1)}, s32[18,4]{0,1:T(4,128)}, u32[]{:S(2)}) copy-start(s32[18,4]{0,1:T(4,128)} %param.14) | copy-start | bytes 868
  1.2 5.9 %copy-start = (f32[4,256,256]{2,1,0:T(8,128)S(1)}, f32[4,256,256]{2,1,0:T(8,128)}, u32[]{:S(2)}) copy-start(f32[4,256,256]{2,1,0:T(8,128)} %phase_ref.5) | copy-start | bytes 3145732
  1.2 5.9 %copy-start.1 = (f32[4,256,256]{2,1,0:T(8,128)S(1)}, f32[4,256,256]{2,1,0:T(8,128)}, u32[]{:S(2)}) copy-start(f32[4,256,256]{2,1,0:T(8,128)} %absorb_ref.5) | copy-start | bytes 3145732
  1.2 6.8 %collective-permute-start = (f32[1,2,2,128,128]{4,3,2,1,0:T(8,128)S(1)}, f32[1,2,2,128,128]{4,3,2,1,0:T(8,128)}, u32[]{:S(2)}, u32[]{:S(2)}) collective-permute-start(f32[1,2,2,128,128]{4,3,2,1,0:T(8,128)S(1)} %edge0.1.refs_4_), channel_id=1, source_target_pairs={{0,7},{1,0},{2,1},{3,2},{4,3},{5,4},{6,5},{7,6},{8,15},{9,8},{10,9... | collective-permute-start | bytes 786440 | tf_op jit(solution)/shard_map/ppermute | solution.py:437
  5.3 5.2 %collective-permute-start.1 = (f32[1,2,2,128,128]{4,3,2,1,0:T(8,128)S(1)}, f32[1,2,2,128,128]{4,3,2,1,0:T(8,128)}, u32[]{:S(2)}, u32[]{:S(2)}) collective-permute-start(f32[1,2,2,128,128]{4,3,2,1,0:T(8,128)S(1)} %get-tuple-element.21.refs_4_), channel_id=1, source_target_pairs={{0,7},{1,0},{2,1},{3,2},{4,3},{5,4},{6,5},{7,6},{8,15},{9,8},{10,9... | collective-permute-start | bytes 786440 | tf_op jit(solution)/shard_map/ppermute | solution.py:437
  6.0 7.2 %collective-permute-start.2 = (f32[1,2,2,128,128]{4,3,2,1,0:T(8,128)S(1)}, f32[1,2,2,128,128]{4,3,2,1,0:T(8,128)}, u32[]{:S(2)}, u32[]{:S(2)}) collective-permute-start(f32[1,2,2,128,128]{4,3,2,1,0:T(8,128)S(1)} %get-tuple-element.23.refs_4_), channel_id=1, source_target_pairs={{0,7},{1,0},{2,1},{3,2},{4,3},{5,4},{6,5},{7,6},{8,15},{9,8},{10,9... | collective-permute-start | bytes 786440 | tf_op jit(solution)/shard_map/ppermute | solution.py:437
  6.3 9.7 %collective-permute-start.3 = (f32[1,2,2,128,128]{4,3,2,1,0:T(8,128)S(1)}, f32[1,2,2,128,128]{4,3,2,1,0:T(8,128)S(1)}, u32[]{:S(2)}, u32[]{:S(2)}) collective-permute-start(f32[1,2,2,128,128]{4,3,2,1,0:T(8,128)S(1)} %get-tuple-element.25.refs_4_), channel_id=1, source_target_pairs={{0,7},{1,0},{2,1},{3,2},{4,3},{5,4},{6,5},{7,6},{8,15},{9,8},{10,9... | collective-permute-start | bytes 786440 | tf_op jit(solution)/shard_map/ppermute | solution.py:437
  7.1 1.0 %copy-start.2 = (f32[1,4,2,128,128]{4,3,2,1,0:T(8,128)S(1)}, f32[1,4,2,128,128]{4,3,2,1,0:T(8,128)}, u32[]{:S(2)}) copy-start(f32[1,4,2,128,128]{4,3,2,1,0:T(8,128)} %param.12) | copy-start | bytes 1572868
  7.1 1.1 %copy-start.4 = (bf16[2,256,256]{2,1,0:T(8,128)(2,1)S(1)}, bf16[2,256,256]{2,1,0:T(8,128)(2,1)}, u32[]{:S(2)}) copy-start(bf16[2,256,256]{2,1,0:T(8,128)(2,1)} %constant.24.clone.refs_2_) | copy-start | bytes 786436
  7.1 1.2 %copy-start.5 = (bf16[512,256]{1,0:T(8,128)(2,1)S(1)}, bf16[512,256]{1,0:T(8,128)(2,1)}, u32[]{:S(2)}) copy-start(bf16[512,256]{1,0:T(8,128)(2,1)} %constant.25.clone.refs_3_) | copy-start | bytes 786436
  13.2 2.8 %copy-start.6 = (bf16[256,384]{1,0:T(8,128)(2,1)S(1)}, bf16[256,384]{1,0:T(8,128)(2,1)}, u32[]{:S(2)}) copy-start(bf16[256,384]{1,0:T(8,128)(2,1)} %constant.26.clone.refs_3_) | copy-start | bytes 589828
  16.6 7.8 %collective-permute-start.6 = (f32[1,2,128,128]{3,2,1,0:T(8,128)S(1)}, f32[1,2,128,128]{3,2,1,0:T(8,128)S(1)}, u32[]{:S(2)}, u32[]{:S(2)}) collective-permute-start(f32[1,2,128,128]{3,2,1,0:T(8,128)S(1)} %get-tuple-element.27.refs_5_.refs_9_), channel_id=1, source_target_pairs={{0,8},{8,16},{16,24},{24,32},{32,40},{40,48},{48,56},{56,64},{64,7... | collective-permute-start | bytes 393224 | tf_op jit(solution)/shard_map/ppermute | solution.py:471
  18.2 3.8 %copy-start.3 = (f32[2,128,128]{2,1,0:T(8,128)S(1)}, f32[2,128,128]{2,1,0:T(8,128)}, u32[]{:S(2)}) copy-start(f32[2,128,128]{2,1,0:T(8,128)} %refs_1_.3) | copy-start | bytes 393220
  19.3 17.3 %collective-permute-start.4 = (f32[1,2,128,128]{3,2,1,0:T(8,128)S(1)}, f32[1,2,128,128]{3,2,1,0:T(8,128)S(1)}, u32[]{:S(2)}, u32[]{:S(2)}) collective-permute-start(f32[1,2,128,128]{3,2,1,0:T(8,128)S(1)} %get-tuple-element.28.refs_8_.refs_11_), channel_id=1, source_target_pairs={{0,8},{8,16},{16,24},{24,32},{32,40},{40,48},{48,56},{56,64},{64,7... | collective-permute-start | bytes 393224 | tf_op jit(solution)/shard_map/ppermute | solution.py:471
  20.8 12.7 %collective-permute-start.5 = (f32[2,2,128,128]{3,2,1,0:T(8,128)S(1)}, f32[2,2,128,128]{3,2,1,0:T(8,128)S(1)}, u32[]{:S(2)}, u32[]{:S(2)}) collective-permute-start(f32[2,2,128,128]{3,2,1,0:T(8,128)S(1)} %get-tuple-element.32.refs_10_), channel_id=1, source_target_pairs={{0,8},{8,16},{16,24},{24,32},{32,40},{40,48},{48,56},{56,64},{64,7... | collective-permute-start | bytes 786440 | tf_op jit(solution)/shard_map/ppermute | solution.py:471
  26.5 12.9 %collective-permute-start.8 = (f32[1,2,128,128]{3,2,1,0:T(8,128)S(1)}, f32[1,2,128,128]{3,2,1,0:T(8,128)S(1)}, u32[]{:S(2)}, u32[]{:S(2)}) collective-permute-start(f32[1,2,128,128]{3,2,1,0:T(8,128)S(1)} %tick1_0.1.refs_9_.refs_12_), channel_id=1, source_target_pairs={{0,8},{8,16},{16,24},{24,32},{32,40},{40,48},{48,56},{56,64},{64,7... | collective-permute-start | bytes 393224 | tf_op jit(solution)/shard_map/ppermute | solution.py:471
  36.5 9.4 %collective-permute-start.9 = (f32[2,2,128,128]{3,2,1,0:T(8,128)S(1)}, f32[2,2,128,128]{3,2,1,0:T(8,128)S(1)}, u32[]{:S(2)}, u32[]{:S(2)}) collective-permute-start(f32[2,2,128,128]{3,2,1,0:T(8,128)S(1)} %tick1_1.1.refs_9_.refs_13_), channel_id=1, source_target_pairs={{0,8},{8,16},{16,24},{24,32},{32,40},{40,48},{48,56},{56,64},{64,7... | collective-permute-start | bytes 786440 | tf_op jit(solution)/shard_map/ppermute | solution.py:471
  38.7 10.2 %collective-permute-start.7 = (f32[1,2,128,128]{3,2,1,0:T(8,128)S(1)}, f32[1,2,128,128]{3,2,1,0:T(8,128)S(1)}, u32[]{:S(2)}, u32[]{:S(2)}) collective-permute-start(f32[1,2,128,128]{3,2,1,0:T(8,128)S(1)} %tick1_3.1.refs_8_.refs_14_), channel_id=1, source_target_pairs={{0,8},{8,16},{16,24},{24,32},{32,40},{40,48},{48,56},{56,64},{64,7... | collective-permute-start | bytes 393224 | tf_op jit(solution)/shard_map/ppermute | solution.py:471
